TPU v7x, 32 devices: a whole 2x2x4 slice. The times are simulated.
32 devices in a mesh: groups: 1, patch: 32 (over z, y, x, core), level: 1.
Axes of the slice: x: 2, y: 2, z: 4, core: 2. Of those that a mesh axis runs over, the one named last changes fastest.
Arguments:
- layer_input: bfloat16 [1, 4096, 1536], P('groups', 'patch', 'level'), may hold values from -24 to 24, as said below
- cotangent: bfloat16 [1, 4096, 1536], P('groups', 'patch', 'level'), may hold values from -6 to 6
- neighbours: int32 [4096, 6], P('patch'), may hold values from 0 to 192, as said below
- boundary: int32 [32, 64], P('patch'), may hold values from 0 to 127, as said below
- gauge_index: int32 [4096, 6], P('patch'), may hold values from 0 to 1023
- gauge_angles: float32 [1024], replicated, may hold values from -3.140625 to 3.140625
- norm_gain: float32 [1536], replicated, may hold values from 0.5 to 1.5
- up_weight: bfloat16 [1536, 2048], P('patch', 'level'), may hold values from -0.15625 to 0.15625
- down_weight: bfloat16 [1536, 2048], P('patch', 'level'), may hold values from -0.125 to 0.125
- self_real: bfloat16 [32, 32], replicated, may hold values from -0.75 to 0.75
- self_imag: bfloat16 [32, 32], replicated, may hold values from -0.75 to 0.75
- near_real: bfloat16 [32, 32], replicated, may hold values from -1.5 to 1.5
- near_imag: bfloat16 [32, 32], replicated, may hold values from -1.5 to 1.5
Outputs:
- layer_grad: bfloat16 [1, 4096, 1536], P('groups', 'patch', 'level')
Inputs may be any that keep to these rules, and one draw needn't show every extreme that they name: `layer_input`: the layer input is a real field; rows and features carry differing scales. `neighbours`: entry i of a column's row refers to its patch's extended rows: i < 128 is the patch's own column i, then 32 boundary columns of the previous patch in the cycle, then 32 of the next one; 192 appears only in the last entry and marks an absent neighbour. `boundary`: row p holds 64 distinct local columns of patch p: the first 32 are seen by patch p - 1, the rest by patch p + 1 (patches form a cycle).
All inputs are finite; a program needn't handle non-finite values.
Results may differ from a plain program's by a relative error of at most 0.014.
Values may be sent and summed in bfloat16 or wider, within the bound.
No kernel may reach another device: no remote copies, remote signals or barrier semaphores. Data moves between devices by JAX's collectives and lax.ppermute only.
A program may use at most 64 MiB of HBM per device.

v0:
```python
import jax
import jax.numpy as jnp
from jax import lax
from jax.experimental import pallas as pl
from jax.experimental.pallas import tpu as pltpu
from jax.sharding import PartitionSpec as P


CH = 64


def padded(shard, sides, width):
    for axis, dim in sides:
        devices, length = (lax.axis_size(axis), shard.shape[dim])
        up = [(i, (i + 1) % devices) for i in range(devices)]
        down = [(j, i) for i, j in up]
        last = lax.slice_in_dim(shard, length - width, length, axis=dim)
        leading = lax.slice_in_dim(shard, 0, width, axis=dim)
        before = lax.ppermute(last, axis, up)
        after = lax.ppermute(leading, axis, down)
        shard = jnp.concatenate([before, shard, after], axis=dim)
    return shard


def real_form(real_part, imag_part):
    upper = jnp.concatenate([real_part, imag_part], axis=1)
    lower = jnp.concatenate([-imag_part, real_part], axis=1)
    return jnp.concatenate([upper, lower], axis=0)


def rotate_quarter(values, channels):
    shape = values.shape
    split = values.reshape(shape[:-1] + (shape[-1] // channels, 2, channels // 2))
    turned = jnp.stack([-split[..., 1, :], split[..., 0, :]], axis=-2)
    return turned.reshape(shape)


def per_level(values, form, channels):
    shape = values.shape
    split = values.reshape(shape[:-1] + (shape[-1] // channels, channels))
    result = jnp.einsum("bclw,wv->bclv", split, form, preferred_element_type=jnp.float32)
    return result.reshape(shape)


def mlp_back(columns_in, grads, norm_gain, up_mat, down_mat):
    values = columns_in.astype(jnp.float32)
    root_scale = lax.rsqrt(jnp.mean(values * values, axis=-1, keepdims=True) + 1e-05)
    normed = (values * root_scale * norm_gain).astype(jnp.bfloat16)
    pre_act = jnp.einsum("brw,wh->brh", normed, up_mat, preferred_element_type=jnp.float32)
    back_hidden = jnp.einsum("brw,wh->brh", grads, down_mat, preferred_element_type=jnp.float32)
    sigmoid_pre = jax.nn.sigmoid(pre_act)
    grad_pre = (back_hidden * sigmoid_pre * (1.0 + pre_act * (1.0 - sigmoid_pre))).astype(
        jnp.bfloat16
    )
    grad_normed = jnp.einsum("brh,wh->brw", grad_pre, up_mat, preferred_element_type=jnp.float32)
    mixed_mean = jnp.mean(norm_gain * grad_normed * values, axis=-1, keepdims=True)
    return (
        root_scale * norm_gain * grad_normed
        - values * root_scale * root_scale * root_scale * mixed_mean
    )


def general(
    layer_input,
    cotangent,
    neighbours,
    boundary,
    gauge_index,
    gauge_angles,
    norm_gain,
    up_weight,
    down_weight,
    self_real,
    self_imag,
    near_real,
    near_imag,
):
    samples, columns, width = layer_input.shape
    border = boundary.shape[1] // 2
    low_rows = boundary[0, :border]
    high_rows = boundary[0, border:]
    sent = jnp.stack([layer_input[:, low_rows], layer_input[:, high_rows]])
    cycle = padded(sent, (("patch", 0),), 1)
    extended = jnp.concatenate(
        [layer_input, cycle[0], cycle[3], jnp.zeros((samples, 1, width), jnp.bfloat16)], axis=1
    )
    sentinel = columns + 2 * border
    present = (neighbours < sentinel).astype(jnp.float32)
    edge_weight = present / jnp.sum(present, axis=1, keepdims=True)
    phase = gauge_angles[gauge_index]
    cosine = jnp.cos(phase)
    sine = jnp.sin(phase)
    near_form = real_form(near_real, near_imag)
    self_form = real_form(self_real, self_imag)
    gathered = jnp.zeros((samples, columns, width), jnp.float32)
    for entry in range(6):
        near = extended[:, neighbours[:, entry]].astype(jnp.float32)
        turned = rotate_quarter(near, CH)
        gathered = (
            gathered
            + (
                cosine[None, :, entry : entry + 1] * near
                + sine[None, :, entry : entry + 1] * turned
            )
            * edge_weight[None, :, entry : entry + 1]
        )
    gathered = gathered.astype(jnp.bfloat16)
    convolved = per_level(gathered, near_form, CH) + per_level(layer_input, self_form, CH)
    conv_out = (layer_input.astype(jnp.float32) + convolved).astype(jnp.bfloat16)
    conv_out = lax.optimization_barrier(conv_out)
    up_part, down_part = (
        lax.all_gather(up_weight, "patch", axis=0, tiled=True),
        lax.all_gather(down_weight, "patch", axis=0, tiled=True),
    )
    up_whole, down_whole = (
        lax.all_gather(up_part, "level", axis=1, tiled=True),
        lax.all_gather(down_part, "level", axis=1, tiled=True),
    )
    half_cols, half_grads = (
        lax.all_to_all(conv_out, "level", split_axis=1, concat_axis=2, tiled=True),
        lax.all_to_all(cotangent, "level", split_axis=1, concat_axis=2, tiled=True),
    )
    terms = mlp_back(half_cols, half_grads, norm_gain, up_whole, down_whole)
    column_grad = (half_grads.astype(jnp.float32) + terms).astype(jnp.bfloat16)
    grad_conv = lax.all_to_all(column_grad, "level", split_axis=2, concat_axis=1, tiled=True)
    grad_conv = lax.optimization_barrier(grad_conv)
    pulled = per_level(grad_conv, near_form.T, CH)
    own_back = per_level(grad_conv, self_form.T, CH)
    pulled_turn = rotate_quarter(pulled, CH)
    spread = jnp.zeros((samples, sentinel + 1, width), jnp.float32)
    for entry in range(6):
        edges = (
            cosine[None, :, entry : entry + 1] * pulled
            - sine[None, :, entry : entry + 1] * pulled_turn
        ) * edge_weight[None, :, entry : entry + 1]
        spread = spread.at[:, neighbours[:, entry]].add(edges)
    back_sent = jnp.stack(
        [spread[:, columns : columns + border], spread[:, columns + border : sentinel]]
    )
    back_cycle = padded(back_sent.astype(jnp.bfloat16), (("patch", 0),), 1).astype(back_sent.dtype)
    local_terms = (
        spread[:, :columns].at[:, low_rows].add(back_cycle[0]).at[:, high_rows].add(back_cycle[3])
    )
    return (grad_conv.astype(jnp.float32) + own_back + local_terms).astype(jnp.bfloat16)


BLOCK = 256
TEAM = 4


def iota(shape, dim):
    return lax.broadcasted_iota(jnp.int32, shape, dim)


def mm(a, b, dims=((1,), (0,))):
    return lax.dot_general(a, b, (dims, ((), ())), preferred_element_type=jnp.float32)


def turn(values):
    width = values.shape[1]
    half = CH // 2
    later = pltpu.roll(values, width - half, 1)
    earlier = pltpu.roll(values, half, 1)
    return jnp.where(iota(values.shape, 1) % CH < half, -later, earlier)


def call(body, outs, args, scratch=(), raw=()):
    vmem = pl.BlockSpec(memory_space=pltpu.VMEM)
    args = [
        value if i in raw else pltpu.with_memory_space_constraint(value, pltpu.VMEM)
        for i, value in enumerate(args)
    ]
    specs = [pl.BlockSpec(memory_space=pl.ANY) if i in raw else vmem for i in range(len(args))]
    return pl.pallas_call(
        body,
        out_shape=outs,
        in_specs=specs,
        out_specs=jax.tree.map(lambda _: vmem, outs),
        scratch_shapes=scratch,
        compiler_params=pltpu.CompilerParams(vmem_limit_bytes=24 << 20),
    )(*args)


def struct(shape, dtype=jnp.bfloat16):
    return pltpu.VMEM(shape, dtype)


def picked(bound_ref, columns):
    count = bound_ref.shape[1]
    return (iota((columns, count), 0) == bound_ref[...]).astype(jnp.bfloat16)


def weights_body(up_ref, down_ref, *refs):
    *parts, sem = refs
    mine = lax.axis_index("patch") % TEAM
    span = parts[0].shape[2]
    copies = []
    for k in range(TEAM):
        at = pl.multiple_of((mine ^ k) * span, 128)
        for which, ref in enumerate((up_ref, down_ref)):
            copies.append(
                pltpu.make_async_copy(
                    ref.at[:, pl.ds(at, span)], parts[k].at[which], sem.at[2 * k + which]
                )
            )
            copies[-1].start()
    for one in copies:
        one.wait()


def border_body(x_ref, bound_ref, low_ref, high_ref):
    border = low_ref.shape[0]
    rows = mm(picked(bound_ref, x_ref.shape[0]), x_ref[...], ((0,), (0,))).astype(jnp.bfloat16)
    low_ref[...] = rows[:border]
    high_ref[...] = rows[border:]


def spread_form(real_ref, imag_ref):
    half = real_ref.shape[0]
    tall = (iota((BLOCK, half), 0) % half == iota((BLOCK, half), 1)).astype(jnp.bfloat16)

    def tiled(ref):
        rows = mm(tall, ref[...]).astype(jnp.bfloat16)
        return mm(rows, tall, ((1,), (1,)))

    real, imag = tiled(real_ref), tiled(imag_ref)
    row, col = iota((BLOCK, BLOCK), 0), iota((BLOCK, BLOCK), 1)
    row_real = row % CH < half
    col_real = col % CH < half
    form = jnp.where(row_real == col_real, real, jnp.where(row_real, imag, -imag))
    return jnp.where(row // CH == col // CH, form, 0.0).astype(jnp.bfloat16)


def prep_body(sentinel, near_ref, index_ref, angle_ref, nr, ni, sr, si, mix_ref, form_ref):
    entries, columns = near_ref.shape
    table = angle_ref[...]
    index = index_ref[...]
    phases = []
    for k in range(entries):
        spot = jnp.broadcast_to(index[k : k + 1], (table.shape[0], columns))
        found = jnp.take_along_axis(table, spot % 128, axis=1)
        hit = iota(found.shape, 0) == spot // 128
        phases.append(jnp.sum(jnp.where(hit, found, 0.0), axis=0, keepdims=True))
    phase = jnp.concatenate(phases, axis=0)
    near = near_ref[...]
    present = (near < sentinel).astype(jnp.float32)
    weight = present / jnp.sum(present, axis=0, keepdims=True)
    cosine, sine = jnp.cos(phase) * weight, jnp.sin(phase) * weight
    height = mix_ref.shape[1]
    place = iota((height, columns), 0)
    mix_cos = jnp.zeros((height, columns), jnp.float32)
    mix_sin = jnp.zeros((height, columns), jnp.float32)
    for k in range(entries):
        hit = near[k : k + 1] == place
        mix_cos = mix_cos + jnp.where(hit, cosine[k : k + 1], 0.0)
        mix_sin = mix_sin + jnp.where(hit, sine[k : k + 1], 0.0)
    mix_ref[0] = mix_cos.astype(jnp.bfloat16)
    mix_ref[1] = mix_sin.astype(jnp.bfloat16)
    form_ref[0] = spread_form(nr, ni)
    form_ref[1] = spread_form(sr, si)


def conv_body(x_ref, before_ref, after_ref, mix_ref, form_ref, gain_ref, conv_ref, norm_ref, ext):
    columns, width = x_ref.shape
    border = before_ref.shape[0]
    ext[:columns] = x_ref[...]
    ext[columns : columns + border] = before_ref[...]
    ext[columns + border : columns + 2 * border] = after_ref[...]
    rest = ext.shape[0] - columns - 2 * border
    if rest:
        ext[columns + 2 * border :] = jnp.zeros((rest, width), jnp.bfloat16)
    source = ext[...]
    over = ((0,), (0,))
    gathered = mm(mix_ref[0], source, over) + turn(mm(mix_ref[1], source, over))
    gathered = gathered.astype(jnp.bfloat16)
    square = jnp.zeros((columns, BLOCK), jnp.float32)
    for b in range(width // BLOCK):
        at = slice(b * BLOCK, (b + 1) * BLOCK)
        x = x_ref[:, at]
        out = x.astype(jnp.float32) + (mm(gathered[:, at], form_ref[0]) + mm(x, form_ref[1]))
        out = out.astype(jnp.bfloat16)
        conv_ref[:, at] = out
        out = out.astype(jnp.float32)
        square = square + out * out
    scale = lax.rsqrt(jnp.sum(square, axis=1, keepdims=True) / width + 1e-05)
    norm_ref[...] = (conv_ref[...].astype(jnp.float32) * scale * gain_ref[...]).astype(jnp.bfloat16)


def ring_place(group, groups):
    return jnp.where(group % 2 == 0, group // 2, groups - 1 - group // 2)


def ring_group(place, groups):
    return jnp.where(place < groups // 2, 2 * place, 2 * (groups - 1 - place) + 1)


def column_body(steps, groups, *refs):
    norms, grads, chunks = refs[:TEAM], refs[TEAM : 2 * TEAM], refs[2 * TEAM : 2 * TEAM + len(steps)]
    mine_ref, cross_ref, send_ref, xs, gs, ups, downs = refs[2 * TEAM + len(steps) :]
    columns = norms[0].shape[0]
    me = lax.axis_index("patch")
    group, member = me // TEAM, me % TEAM
    place = ring_place(group, groups)
    for k in range(TEAM):
        xs[k * columns : (k + 1) * columns] = norms[k][...]
        gs[k * columns : (k + 1) * columns] = grads[k][...]
    for (shift, first), ref in zip(steps, chunks):
        rows = ref.shape[1] // 2
        owner = ring_group((place + shift + groups) % groups, groups)
        for half in range(2):
            at = pl.multiple_of((owner * TEAM + (member ^ (first + half))) * rows, 16)
            span = slice(half * rows, (half + 1) * rows)
            ups[pl.ds(at, rows)] = ref[0, span]
            downs[pl.ds(at, rows)] = ref[1, span]
    pre_act = mm(xs[...], ups[...])
    back = mm(gs[...], downs[...])
    gate = jax.nn.sigmoid(pre_act)
    grad_pre = (back * gate * (1.0 + pre_act * (1.0 - gate))).astype(jnp.bfloat16)
    up = ups[...]
    for k, (ref, slot) in enumerate(((mine_ref, None), (send_ref, 0), (cross_ref, None), (send_ref, 1))):
        rows = mm(grad_pre[k * columns : (k + 1) * columns], up, ((1,), (1,)))
        if slot is None:
            ref[...] = rows
        else:
            ref[slot] = rows.astype(jnp.bfloat16)


def shifted_back(mix, form, grads):
    spread = mm(mix[0], grads) - turn(mm(mix[1], grads))
    spread = spread.astype(jnp.bfloat16)
    width = grads.shape[1]
    return [
        mm(spread[:, b * BLOCK : (b + 1) * BLOCK], form, ((1,), (1,)))
        for b in range(width // BLOCK)
    ]


def join_body(cross_ref, part_ref, out_ref):
    out_ref[...] = (cross_ref[...] + part_ref[1].astype(jnp.float32)).astype(jnp.bfloat16)


def grad_body(mine_ref, part_ref, cross_ref, conv_ref, cot_ref, gain_ref, mix_ref, form_ref, grad_ref, prev_ref, next_ref):
    columns, width = conv_ref.shape
    border = prev_ref.shape[0]
    grad_normed = mine_ref[...] + part_ref[0].astype(jnp.float32) + cross_ref[...].astype(jnp.float32)
    values = conv_ref[...].astype(jnp.float32)
    scaled = gain_ref[...] * grad_normed
    scale = lax.rsqrt(jnp.sum(values * values, axis=1, keepdims=True) / width + 1e-05)
    mixed = jnp.sum(scaled * values, axis=1, keepdims=True) / width
    grads = cot_ref[...].astype(jnp.float32) + (
        scale * scaled - values * (scale * scale * scale * mixed)
    )
    grads = grads.astype(jnp.bfloat16)
    grad_ref[...] = grads
    outer = [mix_ref[i, columns:] for i in range(2)]
    for b, rows in enumerate(shifted_back(outer, form_ref[0], grads)):
        at = slice(b * BLOCK, (b + 1) * BLOCK)
        rows = rows.astype(jnp.bfloat16)
        prev_ref[:, at] = rows[:border]
        next_ref[:, at] = rows[border : 2 * border]


def own_body(grad_ref, mix_ref, form_ref, local_ref):
    columns, _ = grad_ref.shape
    grads = grad_ref[...]
    inner = [mix_ref[i, :columns] for i in range(2)]
    for b, rows in enumerate(shifted_back(inner, form_ref[0], grads)):
        at = slice(b * BLOCK, (b + 1) * BLOCK)
        own = grads[:, at]
        local_ref[:, at] = own.astype(jnp.float32) + (mm(own, form_ref[1], ((1,), (1,))) + rows)


def last_body(local_ref, low_ref, high_ref, bound_ref, out_ref):
    border = low_ref.shape[0]
    chosen = picked(bound_ref, local_ref.shape[0]).astype(jnp.float32)
    low = chosen[:, :border].astype(jnp.bfloat16)
    high = chosen[:, border:].astype(jnp.bfloat16)
    out_ref[...] = (local_ref[...] + mm(low, low_ref[...]) + mm(high, high_ref[...])).astype(jnp.bfloat16)


def per_device(
    layer_input,
    cotangent,
    neighbours,
    boundary,
    gauge_index,
    gauge_angles,
    norm_gain,
    up_weight,
    down_weight,
    self_real,
    self_imag,
    near_real,
    near_imag,
):
    samples, columns, width = layer_input.shape
    devices = lax.axis_size("patch")
    rows, hidden = up_weight.shape
    border = boundary.shape[1] // 2
    span = hidden // TEAM
    fits = (
        lax.axis_size("level") == 1
        and samples == 1
        and devices % (2 * TEAM) == 0
        and width % BLOCK == 0
        and hidden % (TEAM * 128) == 0
        and rows % 16 == 0
        and border % 16 == 0
        and 2 * border <= columns
        and width * span <= 1 << 20
        and gauge_angles.shape[0] % 128 == 0
        and columns == 128
    )
    if not fits:
        return general(
            layer_input,
            cotangent,
            neighbours,
            boundary,
            gauge_index,
            gauge_angles,
            norm_gain,
            up_weight,
            down_weight,
            self_real,
            self_imag,
            near_real,
            near_imag,
        )
    groups = devices // TEAM
    sentinel = columns + 2 * border
    extent = -(-sentinel // 128) * 128
    x = layer_input[0]
    cot = cotangent[0]
    angles = gauge_angles.reshape(-1, 128)
    gain = norm_gain.reshape(1, -1)

    def permute(value, pairs):
        return lax.ppermute(value, "patch", pairs)

    def swap(value, bits):
        return permute(value, [(i, i ^ bits) for i in range(devices)])

    def step(value, shift):
        return permute(value, [(i, (i + shift) % devices) for i in range(devices)])

    order = list(range(0, groups, 2)) + list(range(groups - 1, 0, -2))

    def around(value, shift):
        pairs = [
            (order[k] * TEAM + j, order[(k + shift) % groups] * TEAM + j)
            for k in range(groups)
            for j in range(TEAM)
        ]
        return permute(value, pairs)

    parts = call(
        weights_body,
        [struct((2, rows, span))] * TEAM,
        [up_weight, down_weight],
        [pltpu.SemaphoreType.DMA((2 * TEAM,))],
        (0, 1),
    )
    near_part = swap(parts[1], 1)
    far_parts = [swap(parts[2], 2), swap(parts[3], 3)]
    first = jnp.concatenate([parts[0], near_part], axis=1)
    second = jnp.concatenate(far_parts, axis=1)
    steps, chunks = [(0, 0), (0, 2)], [first, second]
    forth = [first, second]
    back = [first, second]
    half = groups // 2
    for s in range(1, half + 1):
        for which in range(2):
            if s < half or which == 0:
                forth[which] = around(forth[which], 1)
                steps.append((-s, 2 * which))
                chunks.append(forth[which])
            if s < half or which == 1:
                back[which] = around(back[which], -1)
                steps.append((s, 2 * which))
                chunks.append(back[which])

    low, high = call(border_body, [struct((border, width))] * 2, [x, boundary])
    before = step(high, 1)
    after = step(low, -1)
    cot_near = swap(cot, 1)
    cot_far = swap(cot, 2)
    cot_cross = swap(cot_far, 1)

    mix, form = call(
        lambda *refs: prep_body(sentinel, *refs),
        [struct((2, extent, columns)), struct((2, BLOCK, BLOCK))],
        [neighbours.T, gauge_index.T, angles, near_real, near_imag, self_real, self_imag],
    )
    conv, norm = call(
        conv_body,
        [struct((columns, width))] * 2,
        [x, before, after, mix, form, gain],
        [pltpu.VMEM((extent, width), jnp.bfloat16)],
    )
    norm_near = swap(norm, 1)
    norm_far = swap(norm, 2)
    norm_cross = swap(norm_far, 1)

    wide = struct((columns, width), jnp.float32)
    mine, cross, send = call(
        lambda *refs: column_body(steps, groups, *refs),
        [wide, wide, struct((2, columns, width))],
        [norm, norm_near, norm_far, norm_cross, cot, cot_near, cot_far, cot_cross, *chunks],
        [
            pltpu.VMEM((TEAM * columns, width), jnp.bfloat16),
            pltpu.VMEM((TEAM * columns, width), jnp.bfloat16),
            pltpu.VMEM((width, span), jnp.bfloat16),
            pltpu.VMEM((width, span), jnp.bfloat16),
        ],
    )
    received = swap(send, 1)
    crossing = call(join_body, struct((columns, width)), [cross, received])
    crossed = swap(crossing, 2)
    grads, to_prev, to_next = call(
        grad_body,
        [struct((columns, width)), struct((border, width)), struct((border, width))],
        [mine, received, crossed, conv, cot, gain, mix, form],
    )
    from_prev = step(to_next, 1)
    from_next = step(to_prev, -1)
    local = call(own_body, wide, [grads, mix, form])
    out = pl.pallas_call(
        last_body, out_shape=jax.ShapeDtypeStruct((columns, width), jnp.bfloat16)
    )(*(pltpu.with_memory_space_constraint(v, pltpu.VMEM) for v in (local, from_prev, from_next, boundary)))
    return out[None]


def solution(mesh):
    in_specs = (
        P("groups", "patch", "level"),
        P("groups", "patch", "level"),
        P("patch", None),
        P("patch", None),
        P("patch", None),
        P(),
        P(),
        P("patch", "level"),
        P("patch", "level"),
        P(),
        P(),
        P(),
        P(),
    )
    out_specs = P("groups", "patch", "level")

    return jax.shard_map(
        per_device, mesh=mesh, in_specs=in_specs, out_specs=out_specs, check_vma=False
    )
```

profile of v0, /device:TPU:0, one launch (start us, length us, event | category | flops | bytes accessed | tf_op | source)
XLA Modules:
  0.0 90.7 jit_solution(7881878000128984911)
XLA Ops:
  0.0 1.0 %copy-done.2 = bf16[48,2048]{1,0:T(8,128)(2,1)S(1)} copy-done((bf16[48,2048]{1,0:T(8,128)(2,1)S(1)}, bf16[48,2048]{1,0:T(8,128)(2,1)}, u32[]{:S(2)}) %copy-start.2) | copy-done | bytes 196632
  2.1 3.0 %collective-permute-start.9 = (bf16[2,48,512]{2,1,0:T(8,128)(2,1)S(1)}, bf16[2,48,512]{2,1,0:T(8,128)(2,1)S(1)}, u32[]{:S(2)}, u32[]{:S(2)}) collective-permute-start(bf16[2,48,512]{2,1,0:T(8,128)(2,1)S(1)} %get-tuple-element.28), channel_id=1, source_target_pairs={{0,2},{1,3},{2,0},{3,1},{4,6},{5,7},{6,4},{7,5},{8,10},{9,11},{10,... | collective-permute-start | bytes 294920 | tf_op jit(solution)/shard_map/ppermute | solution.py:439
  6.1 1.5 %collective-permute-start.8 = (bf16[2,48,512]{2,1,0:T(8,128)(2,1)S(1)}, bf16[2,48,512]{2,1,0:T(8,128)(2,1)S(1)}, u32[]{:S(2)}, u32[]{:S(2)}) collective-permute-start(bf16[2,48,512]{2,1,0:T(8,128)(2,1)S(1)} %get-tuple-element.27), channel_id=1, source_target_pairs={{0,1},{1,0},{2,3},{3,2},{4,5},{5,4},{6,7},{7,6},{8,9},{9,8},{10,11... | collective-permute-start | bytes 294920 | tf_op jit(solution)/shard_map/ppermute | solution.py:439
  8.8 10.7 %collective-permute-done.10 = bf16[2,48,512]{2,1,0:T(8,128)(2,1)S(1)} collective-permute-done((bf16[2,48,512]{2,1,0:T(8,128)(2,1)S(1)}, bf16[2,48,512]{2,1,0:T(8,128)(2,1)S(1)}, u32[]{:S(2)}, u32[]{:S(2)}) %collective-permute-start.10) | collective-permute-done | bytes 98336 | tf_op jit(solution)/shard_map/ppermute | solution.py:439
  19.5 1.1 %collective-permute-start.14 = (bf16[2,96,512]{2,1,0:T(8,128)(2,1)S(1)}, bf16[2,96,512]{2,1,0:T(8,128)(2,1)S(1)}, u32[]{:S(2)}, u32[]{:S(2)}) collective-permute-start(bf16[2,96,512]{2,1,0:T(8,128)(2,1)S(1)} %constant_dynamic-update-slice_fusion.2.refs_9_), channel_id=1, source_target_pairs={{0,4},{1,5},{2,6},{3,7},{8,0},{9,1},{10,2},{11,3},{16,8},{17,9},{1... | collective-permute-start | bytes 589832 | tf_op jit(solution)/shard_map/ppermute | solution.py:439
  20.7 4.6 %collective-permute-start.1 = (bf16[32,1536]{1,0:T(8,128)(2,1)S(1)}, bf16[32,1536]{1,0:T(8,128)(2,1)S(1)}, u32[]{:S(2)}, u32[]{:S(2)}) collective-permute-start(bf16[32,1536]{1,0:T(8,128)(2,1)S(1)} %get-tuple-element.22), channel_id=1, source_target_pairs={{0,31},{1,0},{2,1},{3,2},{4,3},{5,4},{6,5},{7,6},{8,7},{9,8},{10,9... | collective-permute-start | bytes 294920 | tf_op jit(solution)/shard_map/ppermute | solution.py:439
  25.3 2.1 %collective-permute-done.1.after_ref = bf16[32,1536]{1,0:T(8,128)(2,1)S(1)} collective-permute-done((bf16[32,1536]{1,0:T(8,128)(2,1)S(1)}, bf16[32,1536]{1,0:T(8,128)(2,1)S(1)}, u32[]{:S(2)}, u32[]{:S(2)}) %collective-permute-start.1) | collective-permute-done | bytes 98336 | tf_op jit(solution)/shard_map/ppermute | solution.py:439
  27.5 2.0 %collective-permute-start.11 = (bf16[2,96,512]{2,1,0:T(8,128)(2,1)S(1)}, bf16[2,96,512]{2,1,0:T(8,128)(2,1)S(1)}, u32[]{:S(2)}, u32[]{:S(2)}) collective-permute-start(bf16[2,96,512]{2,1,0:T(8,128)(2,1)S(1)} %constant_dynamic-update-slice_fusion.refs_8_), channel_id=1, source_target_pairs={{0,8},{1,9},{2,10},{3,11},{8,16},{9,17},{10,18},{11,19},{16,24},{1... | collective-permute-start | bytes 589832 | tf_op jit(solution)/shard_map/ppermute | solution.py:439
  30.2 2.2 %collective-permute-done.13.refs_12_ = bf16[2,96,512]{2,1,0:T(8,128)(2,1)S(1)} collective-permute-done((bf16[2,96,512]{2,1,0:T(8,128)(2,1)S(1)}, bf16[2,96,512]{2,1,0:T(8,128)(2,1)S(1)}, u32[]{:S(2)}, u32[]{:S(2)}) %collective-permute-start.13) | collective-permute-done | bytes 196640 | tf_op jit(solution)/shard_map/ppermute | solution.py:439
  32.4 1.0 %shard_map.129 = (bf16[128,1536]{1,0:T(8,128)(2,1)S(1)}, bf16[128,1536]{1,0:T(8,128)(2,1)S(1)}) custom-call(bf16[128,1536]{1,0:T(8,128)(2,1)S(1)} %bitcast.7, bf16[32,1536]{1,0:T(8,128)(2,1)S(1)} %collective-permute-done.before_ref, bf16[32,1536]{1,0:T(8,128)(2,1)S(1)} %collective-permute-done.1.after_ref, ...), custom_call_target="tpu_custom_call" | custom-call | tf_op jit(solution)/shard_map/pallas_call | solution.py:174
  33.4 1.2 %collective-permute-done.12.refs_11_ = bf16[2,96,512]{2,1,0:T(8,128)(2,1)S(1)} collective-permute-done((bf16[2,96,512]{2,1,0:T(8,128)(2,1)S(1)}, bf16[2,96,512]{2,1,0:T(8,128)(2,1)S(1)}, u32[]{:S(2)}, u32[]{:S(2)}) %collective-permute-start.12) | collective-permute-done | bytes 196640 | tf_op jit(solution)/shard_map/ppermute | solution.py:439
  35.1 1.1 %collective-permute-start.17 = (bf16[2,96,512]{2,1,0:T(8,128)(2,1)S(1)}, bf16[2,96,512]{2,1,0:T(8,128)(2,1)S(1)}, u32[]{:S(2)}, u32[]{:S(2)}) collective-permute-start(bf16[2,96,512]{2,1,0:T(8,128)(2,1)S(1)} %collective-permute-done.13.refs_12_), channel_id=1, source_target_pairs={{0,8},{1,9},{2,10},{3,11},{8,16},{9,17},{10,18},{11,19},{16,24},{1... | collective-permute-start | bytes 589832 | tf_op jit(solution)/shard_map/ppermute | solution.py:439
  38.1 1.7 %collective-permute-start.15 = (bf16[2,96,512]{2,1,0:T(8,128)(2,1)S(1)}, bf16[2,96,512]{2,1,0:T(8,128)(2,1)S(1)}, u32[]{:S(2)}, u32[]{:S(2)}) collective-permute-start(bf16[2,96,512]{2,1,0:T(8,128)(2,1)S(1)} %collective-permute-done.11.refs_10_), channel_id=1, source_target_pairs={{0,8},{1,9},{2,10},{3,11},{8,16},{9,17},{10,18},{11,19},{16,24},{1... | collective-permute-start | bytes 589832 | tf_op jit(solution)/shard_map/ppermute | solution.py:439
  39.8 3.1 %collective-permute-done.17.refs_16_ = bf16[2,96,512]{2,1,0:T(8,128)(2,1)S(1)} collective-permute-done((bf16[2,96,512]{2,1,0:T(8,128)(2,1)S(1)}, bf16[2,96,512]{2,1,0:T(8,128)(2,1)S(1)}, u32[]{:S(2)}, u32[]{:S(2)}) %collective-permute-start.17) | collective-permute-done | bytes 196640 | tf_op jit(solution)/shard_map/ppermute | solution.py:439
  44.2 2.5 %collective-permute-done.15.refs_14_ = bf16[2,96,512]{2,1,0:T(8,128)(2,1)S(1)} collective-permute-done((bf16[2,96,512]{2,1,0:T(8,128)(2,1)S(1)}, bf16[2,96,512]{2,1,0:T(8,128)(2,1)S(1)}, u32[]{:S(2)}, u32[]{:S(2)}) %collective-permute-start.15) | collective-permute-done | bytes 196640 | tf_op jit(solution)/shard_map/ppermute | solution.py:439
  46.7 1.1 %collective-permute-start.21 = (bf16[2,96,512]{2,1,0:T(8,128)(2,1)S(1)}, bf16[2,96,512]{2,1,0:T(8,128)(2,1)S(1)}, u32[]{:S(2)}, u32[]{:S(2)}) collective-permute-start(bf16[2,96,512]{2,1,0:T(8,128)(2,1)S(1)} %collective-permute-done.17.refs_16_), channel_id=1, source_target_pairs={{0,8},{1,9},{2,10},{3,11},{8,16},{9,17},{10,18},{11,19},{16,24},{1... | collective-permute-start | bytes 589832 | tf_op jit(solution)/shard_map/ppermute | solution.py:439
  47.8 1.1 %collective-permute-start.19 = (bf16[2,96,512]{2,1,0:T(8,128)(2,1)S(1)}, bf16[2,96,512]{2,1,0:T(8,128)(2,1)S(1)}, u32[]{:S(2)}, u32[]{:S(2)}) collective-permute-start(bf16[2,96,512]{2,1,0:T(8,128)(2,1)S(1)} %collective-permute-done.15.refs_14_), channel_id=1, source_target_pairs={{0,8},{1,9},{2,10},{3,11},{8,16},{9,17},{10,18},{11,19},{16,24},{1... | collective-permute-start | bytes 589832 | tf_op jit(solution)/shard_map/ppermute | solution.py:439
  48.8 1.4 %collective-permute-done.22.refs_21_ = bf16[2,96,512]{2,1,0:T(8,128)(2,1)S(1)} collective-permute-done((bf16[2,96,512]{2,1,0:T(8,128)(2,1)S(1)}, bf16[2,96,512]{2,1,0:T(8,128)(2,1)S(1)}, u32[]{:S(2)}, u32[]{:S(2)}) %collective-permute-start.22) | collective-permute-done | bytes 196640 | tf_op jit(solution)/shard_map/ppermute | solution.py:439
  50.5 3.9 %collective-permute-done.21.refs_20_ = bf16[2,96,512]{2,1,0:T(8,128)(2,1)S(1)} collective-permute-done((bf16[2,96,512]{2,1,0:T(8,128)(2,1)S(1)}, bf16[2,96,512]{2,1,0:T(8,128)(2,1)S(1)}, u32[]{:S(2)}, u32[]{:S(2)}) %collective-permute-start.21) | collective-permute-done | bytes 196640 | tf_op jit(solution)/shard_map/ppermute | solution.py:439
  54.5 2.8 %collective-permute-done.19.refs_18_ = bf16[2,96,512]{2,1,0:T(8,128)(2,1)S(1)} collective-permute-done((bf16[2,96,512]{2,1,0:T(8,128)(2,1)S(1)}, bf16[2,96,512]{2,1,0:T(8,128)(2,1)S(1)}, u32[]{:S(2)}, u32[]{:S(2)}) %collective-permute-start.19) | collective-permute-done | bytes 196640 | tf_op jit(solution)/shard_map/ppermute | solution.py:439
  57.3 1.1 %collective-permute-start.23 = (bf16[2,96,512]{2,1,0:T(8,128)(2,1)S(1)}, bf16[2,96,512]{2,1,0:T(8,128)(2,1)S(1)}, u32[]{:S(2)}, u32[]{:S(2)}) collective-permute-start(bf16[2,96,512]{2,1,0:T(8,128)(2,1)S(1)} %collective-permute-done.19.refs_18_), channel_id=1, source_target_pairs={{0,8},{1,9},{2,10},{3,11},{8,16},{9,17},{10,18},{11,19},{16,24},{1... | collective-permute-start | bytes 589832 | tf_op jit(solution)/shard_map/ppermute | solution.py:439
  58.4 2.1 %collective-permute-done.24.refs_23_ = bf16[2,96,512]{2,1,0:T(8,128)(2,1)S(1)} collective-permute-done((bf16[2,96,512]{2,1,0:T(8,128)(2,1)S(1)}, bf16[2,96,512]{2,1,0:T(8,128)(2,1)S(1)}, u32[]{:S(2)}, u32[]{:S(2)}) %collective-permute-start.24) | collective-permute-done | bytes 196640 | tf_op jit(solution)/shard_map/ppermute | solution.py:439
  60.5 2.5 %collective-permute-done.23.refs_22_ = bf16[2,96,512]{2,1,0:T(8,128)(2,1)S(1)} collective-permute-done((bf16[2,96,512]{2,1,0:T(8,128)(2,1)S(1)}, bf16[2,96,512]{2,1,0:T(8,128)(2,1)S(1)}, u32[]{:S(2)}, u32[]{:S(2)}) %collective-permute-start.23) | collective-permute-done | bytes 196640 | tf_op jit(solution)/shard_map/ppermute | solution.py:439
  63.0 4.0 %shard_map.131 = (f32[128,1536]{1,0:T(8,128)S(1)}, f32[128,1536]{1,0:T(8,128)S(1)}, bf16[2,128,1536]{2,1,0:T(8,128)(2,1)S(1)}) custom-call(bf16[128,1536]{1,0:T(8,128)(2,1)S(1)} %get-tuple-element.25.refs_0_, bf16[128,1536]{1,0:T(8,128)(2,1)S(1)} %collective-permute-done.2.refs_1_, bf16[128,1536]{1,0:T(8,128)(2,1)S(1)} %collective-permute-done.3.refs_2_, ...), custom_call_target="tpu_custom_call" | custom-call | tf_op jit(solution)/shard_map/pallas_call | solution.py:174
  67.1 2.3 %collective-permute-done.25.part_ref = bf16[2,128,1536]{2,1,0:T(8,128)(2,1)S(1)} collective-permute-done((bf16[2,128,1536]{2,1,0:T(8,128)(2,1)S(1)}, bf16[2,128,1536]{2,1,0:T(8,128)(2,1)S(1)}, u32[]{:S(2)}, u32[]{:S(2)}) %collective-permute-start.25) | collective-permute-done | bytes 786464 | tf_op jit(solution)/shard_map/ppermute | solution.py:439
  69.5 1.5 %collective-permute-start.26 = (bf16[128,1536]{1,0:T(8,128)(2,1)S(1)}, bf16[128,1536]{1,0:T(8,128)(2,1)S(1)}, u32[]{:S(2)}, u32[]{:S(2)}) collective-permute-start(bf16[128,1536]{1,0:T(8,128)(2,1)S(1)} %shard_map.132), channel_id=1, source_target_pairs={{0,2},{1,3},{2,0},{3,1},{4,6},{5,7},{6,4},{7,5},{8,10},{9,11},{10,... | collective-permute-start | bytes 1179656 | tf_op jit(solution)/shard_map/ppermute | solution.py:439
  71.0 9.7 %collective-permute-done.26.cross_ref = bf16[128,1536]{1,0:T(8,128)(2,1)S(1)} collective-permute-done((bf16[128,1536]{1,0:T(8,128)(2,1)S(1)}, bf16[128,1536]{1,0:T(8,128)(2,1)S(1)}, u32[]{:S(2)}, u32[]{:S(2)}) %collective-permute-start.26) | collective-permute-done | bytes 393248 | tf_op jit(solution)/shard_map/ppermute | solution.py:439
  80.7 1.2 %shard_map.133 = (bf16[128,1536]{1,0:T(8,128)(2,1)S(1)}, bf16[32,1536]{1,0:T(8,128)(2,1)S(1)}, bf16[32,1536]{1,0:T(8,128)(2,1)S(1)}) custom-call(f32[128,1536]{1,0:T(8,128)S(1)} %get-tuple-element.30.mine_ref, bf16[2,128,1536]{2,1,0:T(8,128)(2,1)S(1)} %collective-permute-done.25.part_ref, bf16[128,1536]{1,0:T(8,128)(2,1)S(1)} %collective-permute-done.26.cross_ref, ...), custom_call_target="tpu_custom_call" | custom-call | tf_op jit(solution)/shard_map/pallas_call | solution.py:174
  82.0 5.3 %collective-permute-start.28 = (bf16[32,1536]{1,0:T(8,128)(2,1)S(1)}, bf16[32,1536]{1,0:T(8,128)(2,1)S(1)}, u32[]{:S(2)}, u32[]{:S(2)}) collective-permute-start(bf16[32,1536]{1,0:T(8,128)(2,1)S(1)} %get-tuple-element.36), channel_id=1, source_target_pairs={{0,31},{1,0},{2,1},{3,2},{4,3},{5,4},{6,5},{7,6},{8,7},{9,8},{10,9... | collective-permute-start | bytes 294920 | tf_op jit(solution)/shard_map/ppermute | solution.py:439
  87.3 1.1 %shard_map.134.local_ref = f32[128,1536]{1,0:T(8,128)S(1)} custom-call(bf16[128,1536]{1,0:T(8,128)(2,1)S(1)} %get-tuple-element.34.grad_ref, bf16[2,256,128]{2,1,0:T(8,128)(2,1)S(1)} %get-tuple-element.23.mix_ref, bf16[2,256,256]{2,1,0:T(8,128)(2,1)S(1)} %get-tuple-element.24.form_ref), custom_call_target="tpu_custom_call" | custom-call | tf_op jit(solution)/shard_map/pallas_call | solution.py:174
  88.4 1.2 %collective-permute-done.27.low_ref = bf16[32,1536]{1,0:T(8,128)(2,1)S(1)} collective-permute-done((bf16[32,1536]{1,0:T(8,128)(2,1)S(1)}, bf16[32,1536]{1,0:T(8,128)(2,1)S(1)}, u32[]{:S(2)}, u32[]{:S(2)}) %collective-permute-start.27) | collective-permute-done | bytes 98336 | tf_op jit(solution)/shard_map/ppermute | solution.py:439
  89.6 1.1 %shard_map.135 = bf16[128,1536]{1,0:T(8,128)(2,1)} custom-call(f32[128,1536]{1,0:T(8,128)S(1)} %shard_map.134.local_ref, bf16[32,1536]{1,0:T(8,128)(2,1)S(1)} %collective-permute-done.27.low_ref, bf16[32,1536]{1,0:T(8,128)(2,1)S(1)} %collective-permute-done.28.high_ref, s32[1,64]{1,0:T(1,128)S(1)} %copy-done.11), custom_call_target="tpu_custom_call" | custom-call | tf_op jit(solution)/shard_map/pallas_call | solution.py:528
  (66 shorter events, 8.3 us)
Async XLA Ops:
  0.0 5.2 %copy-start = (bf16[1,128,1536]{2,1,0:T(8,128)(2,1)S(1)}, bf16[1,128,1536]{2,1,0:T(8,128)(2,1)}, u32[]{:S(2)}) copy-start(bf16[1,128,1536]{2,1,0:T(8,128)(2,1)} %param.13) | copy-start | bytes 1179652
  2.1 6.3 %collective-permute-start.9 = (bf16[2,48,512]{2,1,0:T(8,128)(2,1)S(1)}, bf16[2,48,512]{2,1,0:T(8,128)(2,1)S(1)}, u32[]{:S(2)}, u32[]{:S(2)}) collective-permute-start(bf16[2,48,512]{2,1,0:T(8,128)(2,1)S(1)} %get-tuple-element.28), channel_id=1, source_target_pairs={{0,2},{1,3},{2,0},{3,1},{4,6},{5,7},{6,4},{7,5},{8,10},{9,11},{10,... | collective-permute-start | bytes 294920 | tf_op jit(solution)/shard_map/ppermute | solution.py:439
  5.1 30.0 %collective-permute-start.6 = (bf16[128,1536]{1,0:T(8,128)(2,1)}, bf16[128,1536]{1,0:T(8,128)(2,1)S(1)}, u32[]{:S(2)}, u32[]{:S(2)}) collective-permute-start(bf16[128,1536]{1,0:T(8,128)(2,1)} %bitcast.8), channel_id=1, source_target_pairs={{0,2},{1,3},{2,0},{3,1},{4,6},{5,7},{6,4},{7,5},{8,10},{9,11},{10,... | collective-permute-start | bytes 1179656 | tf_op jit(solution)/shard_map/ppermute | solution.py:439
  5.2 31.0 %collective-permute-start.5 = (bf16[128,1536]{1,0:T(8,128)(2,1)}, bf16[128,1536]{1,0:T(8,128)(2,1)S(1)}, u32[]{:S(2)}, u32[]{:S(2)}) collective-permute-start(bf16[128,1536]{1,0:T(8,128)(2,1)} %bitcast.9), channel_id=1, source_target_pairs={{0,1},{1,0},{2,3},{3,2},{4,5},{5,4},{6,7},{7,6},{8,9},{9,8},{10,11... | collective-permute-start | bytes 1179656 | tf_op jit(solution)/shard_map/ppermute | solution.py:439
  6.0 14.6 %collective-permute-start = (bf16[32,1536]{1,0:T(8,128)(2,1)S(1)}, bf16[32,1536]{1,0:T(8,128)(2,1)S(1)}, u32[]{:S(2)}, u32[]{:S(2)}) collective-permute-start(bf16[32,1536]{1,0:T(8,128)(2,1)S(1)} %get-tuple-element.21), channel_id=1, source_target_pairs={{0,1},{1,2},{2,3},{3,4},{4,5},{5,6},{6,7},{7,8},{8,9},{9,10},{10,1... | collective-permute-start | bytes 294920 | tf_op jit(solution)/shard_map/ppermute | solution.py:439
  6.1 19.2 %collective-permute-start.8 = (bf16[2,48,512]{2,1,0:T(8,128)(2,1)S(1)}, bf16[2,48,512]{2,1,0:T(8,128)(2,1)S(1)}, u32[]{:S(2)}, u32[]{:S(2)}) collective-permute-start(bf16[2,48,512]{2,1,0:T(8,128)(2,1)S(1)} %get-tuple-element.27), channel_id=1, source_target_pairs={{0,1},{1,0},{2,3},{3,2},{4,5},{5,4},{6,7},{7,6},{8,9},{9,8},{10,11... | collective-permute-start | bytes 294920 | tf_op jit(solution)/shard_map/ppermute | solution.py:439
  8.3 11.2 %collective-permute-start.10 = (bf16[2,48,512]{2,1,0:T(8,128)(2,1)S(1)}, bf16[2,48,512]{2,1,0:T(8,128)(2,1)S(1)}, u32[]{:S(2)}, u32[]{:S(2)}) collective-permute-start(bf16[2,48,512]{2,1,0:T(8,128)(2,1)S(1)} %get-tuple-element.29), channel_id=1, source_target_pairs={{0,3},{1,2},{2,1},{3,0},{4,7},{5,6},{6,5},{7,4},{8,11},{9,10},{10,... | collective-permute-start | bytes 294920 | tf_op jit(solution)/shard_map/ppermute | solution.py:439
  19.5 8.0 %collective-permute-start.14 = (bf16[2,96,512]{2,1,0:T(8,128)(2,1)S(1)}, bf16[2,96,512]{2,1,0:T(8,128)(2,1)S(1)}, u32[]{:S(2)}, u32[]{:S(2)}) collective-permute-start(bf16[2,96,512]{2,1,0:T(8,128)(2,1)S(1)} %constant_dynamic-update-slice_fusion.2.refs_9_), channel_id=1, source_target_pairs={{0,4},{1,5},{2,6},{3,7},{8,0},{9,1},{10,2},{11,3},{16,8},{17,9},{1... | collective-permute-start | bytes 589832 | tf_op jit(solution)/shard_map/ppermute | solution.py:439
  20.7 8.8 %copy-start.12 = (f32[1536]{0:T(1024)S(1)}, f32[1536]{0:T(1024)}, u32[]{:S(2)}) copy-start(f32[1536]{0:T(1024)} %param.19) | copy-start | bytes 18436
  20.7 6.8 %collective-permute-start.1 = (bf16[32,1536]{1,0:T(8,128)(2,1)S(1)}, bf16[32,1536]{1,0:T(8,128)(2,1)S(1)}, u32[]{:S(2)}, u32[]{:S(2)}) collective-permute-start(bf16[32,1536]{1,0:T(8,128)(2,1)S(1)} %get-tuple-element.22), channel_id=1, source_target_pairs={{0,31},{1,0},{2,1},{3,2},{4,3},{5,4},{6,5},{7,6},{8,7},{9,8},{10,9... | collective-permute-start | bytes 294920 | tf_op jit(solution)/shard_map/ppermute | solution.py:439
  25.2 7.2 %collective-permute-start.13 = (bf16[2,96,512]{2,1,0:T(8,128)(2,1)S(1)}, bf16[2,96,512]{2,1,0:T(8,128)(2,1)S(1)}, u32[]{:S(2)}, u32[]{:S(2)}) collective-permute-start(bf16[2,96,512]{2,1,0:T(8,128)(2,1)S(1)} %constant_dynamic-update-slice_fusion.2.refs_9_), channel_id=1, source_target_pairs={{0,8},{1,9},{2,10},{3,11},{8,16},{9,17},{10,18},{11,19},{16,24},{1... | collective-permute-start | bytes 589832 | tf_op jit(solution)/shard_map/ppermute | solution.py:439
  27.5 7.2 %collective-permute-start.12 = (bf16[2,96,512]{2,1,0:T(8,128)(2,1)S(1)}, bf16[2,96,512]{2,1,0:T(8,128)(2,1)S(1)}, u32[]{:S(2)}, u32[]{:S(2)}) collective-permute-start(bf16[2,96,512]{2,1,0:T(8,128)(2,1)S(1)} %constant_dynamic-update-slice_fusion.refs_8_), channel_id=1, source_target_pairs={{0,4},{1,5},{2,6},{3,7},{8,0},{9,1},{10,2},{11,3},{16,8},{17,9},{1... | collective-permute-start | bytes 589832 | tf_op jit(solution)/shard_map/ppermute | solution.py:439
  27.5 7.7 %collective-permute-start.11 = (bf16[2,96,512]{2,1,0:T(8,128)(2,1)S(1)}, bf16[2,96,512]{2,1,0:T(8,128)(2,1)S(1)}, u32[]{:S(2)}, u32[]{:S(2)}) collective-permute-start(bf16[2,96,512]{2,1,0:T(8,128)(2,1)S(1)} %constant_dynamic-update-slice_fusion.refs_8_), channel_id=1, source_target_pairs={{0,8},{1,9},{2,10},{3,11},{8,16},{9,17},{10,18},{11,19},{16,24},{1... | collective-permute-start | bytes 589832 | tf_op jit(solution)/shard_map/ppermute | solution.py:439
  32.4 5.7 %collective-permute-start.18 = (bf16[2,96,512]{2,1,0:T(8,128)(2,1)S(1)}, bf16[2,96,512]{2,1,0:T(8,128)(2,1)S(1)}, u32[]{:S(2)}, u32[]{:S(2)}) collective-permute-start(bf16[2,96,512]{2,1,0:T(8,128)(2,1)S(1)} %collective-permute-done.14.refs_13_), channel_id=1, source_target_pairs={{0,4},{1,5},{2,6},{3,7},{8,0},{9,1},{10,2},{11,3},{16,8},{17,9},{1... | collective-permute-start | bytes 589832 | tf_op jit(solution)/shard_map/ppermute | solution.py:439
  32.4 30.6 %copy-start.1 = (bf16[1,128,1536]{2,1,0:T(8,128)(2,1)S(1)}, bf16[1,128,1536]{2,1,0:T(8,128)(2,1)}, u32[]{:S(2)}) copy-start(bf16[1,128,1536]{2,1,0:T(8,128)(2,1)} %param.14) | copy-start | bytes 1179652
  34.6 13.1 %collective-permute-start.3 = (bf16[128,1536]{1,0:T(8,128)(2,1)S(1)}, bf16[128,1536]{1,0:T(8,128)(2,1)S(1)}, u32[]{:S(2)}, u32[]{:S(2)}) collective-permute-start(bf16[128,1536]{1,0:T(8,128)(2,1)S(1)} %get-tuple-element.25.refs_0_), channel_id=1, source_target_pairs={{0,2},{1,3},{2,0},{3,1},{4,6},{5,7},{6,4},{7,5},{8,10},{9,11},{10,... | collective-permute-start | bytes 1179656 | tf_op jit(solution)/shard_map/ppermute | solution.py:439
  35.1 13.7 %collective-permute-start.2 = (bf16[128,1536]{1,0:T(8,128)(2,1)S(1)}, bf16[128,1536]{1,0:T(8,128)(2,1)S(1)}, u32[]{:S(2)}, u32[]{:S(2)}) collective-permute-start(bf16[128,1536]{1,0:T(8,128)(2,1)S(1)} %get-tuple-element.25.refs_0_), channel_id=1, source_target_pairs={{0,1},{1,0},{2,3},{3,2},{4,5},{5,4},{6,7},{7,6},{8,9},{9,8},{10,11... | collective-permute-start | bytes 1179656 | tf_op jit(solution)/shard_map/ppermute | solution.py:439
  35.1 7.8 %collective-permute-start.17 = (bf16[2,96,512]{2,1,0:T(8,128)(2,1)S(1)}, bf16[2,96,512]{2,1,0:T(8,128)(2,1)S(1)}, u32[]{:S(2)}, u32[]{:S(2)}) collective-permute-start(bf16[2,96,512]{2,1,0:T(8,128)(2,1)S(1)} %collective-permute-done.13.refs_12_), channel_id=1, source_target_pairs={{0,8},{1,9},{2,10},{3,11},{8,16},{9,17},{10,18},{11,19},{16,24},{1... | collective-permute-start | bytes 589832 | tf_op jit(solution)/shard_map/ppermute | solution.py:439
  36.2 7.0 %collective-permute-start.16 = (bf16[2,96,512]{2,1,0:T(8,128)(2,1)S(1)}, bf16[2,96,512]{2,1,0:T(8,128)(2,1)S(1)}, u32[]{:S(2)}, u32[]{:S(2)}) collective-permute-start(bf16[2,96,512]{2,1,0:T(8,128)(2,1)S(1)} %collective-permute-done.12.refs_11_), channel_id=1, source_target_pairs={{0,4},{1,5},{2,6},{3,7},{8,0},{9,1},{10,2},{11,3},{16,8},{17,9},{1... | collective-permute-start | bytes 589832 | tf_op jit(solution)/shard_map/ppermute | solution.py:439
  38.1 8.6 %collective-permute-start.15 = (bf16[2,96,512]{2,1,0:T(8,128)(2,1)S(1)}, bf16[2,96,512]{2,1,0:T(8,128)(2,1)S(1)}, u32[]{:S(2)}, u32[]{:S(2)}) collective-permute-start(bf16[2,96,512]{2,1,0:T(8,128)(2,1)S(1)} %collective-permute-done.11.refs_10_), channel_id=1, source_target_pairs={{0,8},{1,9},{2,10},{3,11},{8,16},{9,17},{10,18},{11,19},{16,24},{1... | collective-permute-start | bytes 589832 | tf_op jit(solution)/shard_map/ppermute | solution.py:439
  42.9 15.5 %collective-permute-start.7 = (bf16[128,1536]{1,0:T(8,128)(2,1)S(1)}, bf16[128,1536]{1,0:T(8,128)(2,1)S(1)}, u32[]{:S(2)}, u32[]{:S(2)}) collective-permute-start(bf16[128,1536]{1,0:T(8,128)(2,1)S(1)} %collective-permute-done.6.refs_6_), channel_id=1, source_target_pairs={{0,1},{1,0},{2,3},{3,2},{4,5},{5,4},{6,7},{7,6},{8,9},{9,8},{10,11... | collective-permute-start | bytes 1179656 | tf_op jit(solution)/shard_map/ppermute | solution.py:439
  43.3 7.0 %collective-permute-start.22 = (bf16[2,96,512]{2,1,0:T(8,128)(2,1)S(1)}, bf16[2,96,512]{2,1,0:T(8,128)(2,1)S(1)}, u32[]{:S(2)}, u32[]{:S(2)}) collective-permute-start(bf16[2,96,512]{2,1,0:T(8,128)(2,1)S(1)} %collective-permute-done.18.refs_17_), channel_id=1, source_target_pairs={{0,4},{1,5},{2,6},{3,7},{8,0},{9,1},{10,2},{11,3},{16,8},{17,9},{1... | collective-permute-start | bytes 589832 | tf_op jit(solution)/shard_map/ppermute | solution.py:439
  46.7 7.8 %collective-permute-start.21 = (bf16[2,96,512]{2,1,0:T(8,128)(2,1)S(1)}, bf16[2,96,512]{2,1,0:T(8,128)(2,1)S(1)}, u32[]{:S(2)}, u32[]{:S(2)}) collective-permute-start(bf16[2,96,512]{2,1,0:T(8,128)(2,1)S(1)} %collective-permute-done.17.refs_16_), channel_id=1, source_target_pairs={{0,8},{1,9},{2,10},{3,11},{8,16},{9,17},{10,18},{11,19},{16,24},{1... | collective-permute-start | bytes 589832 | tf_op jit(solution)/shard_map/ppermute | solution.py:439
  47.8 9.6 %collective-permute-start.19 = (bf16[2,96,512]{2,1,0:T(8,128)(2,1)S(1)}, bf16[2,96,512]{2,1,0:T(8,128)(2,1)S(1)}, u32[]{:S(2)}, u32[]{:S(2)}) collective-permute-start(bf16[2,96,512]{2,1,0:T(8,128)(2,1)S(1)} %collective-permute-done.15.refs_14_), channel_id=1, source_target_pairs={{0,8},{1,9},{2,10},{3,11},{8,16},{9,17},{10,18},{11,19},{16,24},{1... | collective-permute-start | bytes 589832 | tf_op jit(solution)/shard_map/ppermute | solution.py:439
  48.8 14.2 %collective-permute-start.4 = (bf16[128,1536]{1,0:T(8,128)(2,1)S(1)}, bf16[128,1536]{1,0:T(8,128)(2,1)S(1)}, u32[]{:S(2)}, u32[]{:S(2)}) collective-permute-start(bf16[128,1536]{1,0:T(8,128)(2,1)S(1)} %collective-permute-done.3.refs_2_), channel_id=1, source_target_pairs={{0,1},{1,0},{2,3},{3,2},{4,5},{5,4},{6,7},{7,6},{8,9},{9,8},{10,11... | collective-permute-start | bytes 1179656 | tf_op jit(solution)/shard_map/ppermute | solution.py:439
  50.2 8.2 %collective-permute-start.20 = (bf16[2,96,512]{2,1,0:T(8,128)(2,1)S(1)}, bf16[2,96,512]{2,1,0:T(8,128)(2,1)S(1)}, u32[]{:S(2)}, u32[]{:S(2)}) collective-permute-start(bf16[2,96,512]{2,1,0:T(8,128)(2,1)S(1)} %collective-permute-done.16.refs_15_), channel_id=1, source_target_pairs={{0,4},{1,5},{2,6},{3,7},{8,0},{9,1},{10,2},{11,3},{16,8},{17,9},{1... | collective-permute-start | bytes 589832 | tf_op jit(solution)/shard_map/ppermute | solution.py:439
  54.4 6.1 %collective-permute-start.24 = (bf16[2,96,512]{2,1,0:T(8,128)(2,1)S(1)}, bf16[2,96,512]{2,1,0:T(8,128)(2,1)S(1)}, u32[]{:S(2)}, u32[]{:S(2)}) collective-permute-start(bf16[2,96,512]{2,1,0:T(8,128)(2,1)S(1)} %collective-permute-done.22.refs_21_), channel_id=1, source_target_pairs={{0,4},{1,5},{2,6},{3,7},{8,0},{9,1},{10,2},{11,3},{16,8},{17,9},{1... | collective-permute-start | bytes 589832 | tf_op jit(solution)/shard_map/ppermute | solution.py:439
  57.3 5.7 %collective-permute-start.23 = (bf16[2,96,512]{2,1,0:T(8,128)(2,1)S(1)}, bf16[2,96,512]{2,1,0:T(8,128)(2,1)S(1)}, u32[]{:S(2)}, u32[]{:S(2)}) collective-permute-start(bf16[2,96,512]{2,1,0:T(8,128)(2,1)S(1)} %collective-permute-done.19.refs_18_), channel_id=1, source_target_pairs={{0,8},{1,9},{2,10},{3,11},{8,16},{9,17},{10,18},{11,19},{16,24},{1... | collective-permute-start | bytes 589832 | tf_op jit(solution)/shard_map/ppermute | solution.py:439
  67.0 2.4 %collective-permute-start.25 = (bf16[2,128,1536]{2,1,0:T(8,128)(2,1)S(1)}, bf16[2,128,1536]{2,1,0:T(8,128)(2,1)S(1)}, u32[]{:S(2)}, u32[]{:S(2)}) collective-permute-start(bf16[2,128,1536]{2,1,0:T(8,128)(2,1)S(1)} %get-tuple-element.31), channel_id=1, source_target_pairs={{0,1},{1,0},{2,3},{3,2},{4,5},{5,4},{6,7},{7,6},{8,9},{9,8},{10,11... | collective-permute-start | bytes 2359304 | tf_op jit(solution)/shard_map/ppermute | solution.py:439
  69.5 11.2 %collective-permute-start.26 = (bf16[128,1536]{1,0:T(8,128)(2,1)S(1)}, bf16[128,1536]{1,0:T(8,128)(2,1)S(1)}, u32[]{:S(2)}, u32[]{:S(2)}) collective-permute-start(bf16[128,1536]{1,0:T(8,128)(2,1)S(1)} %shard_map.132), channel_id=1, source_target_pairs={{0,2},{1,3},{2,0},{3,1},{4,6},{5,7},{6,4},{7,5},{8,10},{9,11},{10,... | collective-permute-start | bytes 1179656 | tf_op jit(solution)/shard_map/ppermute | solution.py:439
  81.9 7.7 %collective-permute-start.27 = (bf16[32,1536]{1,0:T(8,128)(2,1)S(1)}, bf16[32,1536]{1,0:T(8,128)(2,1)S(1)}, u32[]{:S(2)}, u32[]{:S(2)}) collective-permute-start(bf16[32,1536]{1,0:T(8,128)(2,1)S(1)} %get-tuple-element.35), channel_id=1, source_target_pairs={{0,1},{1,2},{2,3},{3,4},{4,5},{5,6},{6,7},{7,8},{8,9},{9,10},{10,1... | collective-permute-start | bytes 294920 | tf_op jit(solution)/shard_map/ppermute | solution.py:439
  82.0 7.6 %collective-permute-start.28 = (bf16[32,1536]{1,0:T(8,128)(2,1)S(1)}, bf16[32,1536]{1,0:T(8,128)(2,1)S(1)}, u32[]{:S(2)}, u32[]{:S(2)}) collective-permute-start(bf16[32,1536]{1,0:T(8,128)(2,1)S(1)} %get-tuple-element.36), channel_id=1, source_target_pairs={{0,31},{1,0},{2,1},{3,2},{4,3},{5,4},{6,5},{7,6},{8,7},{9,8},{10,9... | collective-permute-start | bytes 294920 | tf_op jit(solution)/shard_map/ppermute | solution.py:439
  (10 other events, 32.3 us)
where the time goes:
time: 90.9 us; the launch traced here: 90.7 us
  waiting for transfers between devices  50.2 us (55%)
  starting transfers between devices  28.2 us (31%)
  Pallas kernels  9.52 us (10%)
  local copies, waits for them, and re-layouts  2.56 us (3%)
    ppermute x29, waiting for transfers between devices, permute(): return lax.ppermute(value, 'patch', pairs)  50.2 us
    ppermute x29, starting transfers between devices, permute(): return lax.ppermute(value, 'patch', pairs)  28.2 us
    pallas_call x8, Pallas kernels, call(): pl.pallas_call(body, out_shape=outs, in_specs=specs, out_specs=jax.tree.m...  8.43 us
    unnamed x28, local copies, waits for them, and re-layouts  2.53 us
  transfers between devices with their start and end apart: 29, of which 18 were waited for; matrix products, arithmetic and copies ran while one was open for 0% of the time, Pallas kernels for 3%

commit v1 on v0

--- a/solution.py
+++ b/solution.py
@@ -164,10 +164,10 @@
     return jnp.where(iota(values.shape, 1) % CH < half, -later, earlier)
 
 
-def call(body, outs, args, scratch=(), raw=()):
+def call(body, outs, args, scratch=(), raw=(), aliases=()):
     vmem = pl.BlockSpec(memory_space=pltpu.VMEM)
     args = [
-        value if i in raw else pltpu.with_memory_space_constraint(value, pltpu.VMEM)
+        pltpu.with_memory_space_constraint(value, pltpu.HBM if i in raw else pltpu.VMEM)
         for i, value in enumerate(args)
     ]
     specs = [pl.BlockSpec(memory_space=pl.ANY) if i in raw else vmem for i in range(len(args))]
@@ -177,6 +177,7 @@
         in_specs=specs,
         out_specs=jax.tree.map(lambda _: vmem, outs),
         scratch_shapes=scratch,
+        input_output_aliases=dict(aliases),
         compiler_params=pltpu.CompilerParams(vmem_limit_bytes=24 << 20),
     )(*args)
 
@@ -190,29 +191,35 @@
     return (iota((columns, count), 0) == bound_ref[...]).astype(jnp.bfloat16)
 
 
-def weights_body(up_ref, down_ref, *refs):
-    *parts, sem = refs
+def load_body(count, *refs):
+    up_ref, down_ref, *sources = refs[: 2 + count]
+    parts = refs[2 + count : 2 + count + TEAM]
+    *targets, sem = refs[2 + count + TEAM :]
     mine = lax.axis_index("patch") % TEAM
     span = parts[0].shape[2]
-    copies = []
+    pairs = []
     for k in range(TEAM):
         at = pl.multiple_of((mine ^ k) * span, 128)
         for which, ref in enumerate((up_ref, down_ref)):
-            copies.append(
-                pltpu.make_async_copy(
-                    ref.at[:, pl.ds(at, span)], parts[k].at[which], sem.at[2 * k + which]
-                )
-            )
-            copies[-1].start()
+            pairs.append((ref.at[:, pl.ds(at, span)], parts[k].at[which]))
+    pairs += zip(sources, targets)
+    copies = [pltpu.make_async_copy(src, dst, sem.at[i]) for i, (src, dst) in enumerate(pairs)]
+    for one in copies:
+        one.start()
     for one in copies:
         one.wait()
 
 
-def border_body(x_ref, bound_ref, low_ref, high_ref):
-    border = low_ref.shape[0]
+def is_even():
+    return lax.axis_index("patch") % 2 == 0
+
+
+def border_body(x_ref, bound_ref, inner_ref, outer_ref):
+    border = inner_ref.shape[0]
     rows = mm(picked(bound_ref, x_ref.shape[0]), x_ref[...], ((0,), (0,))).astype(jnp.bfloat16)
-    low_ref[...] = rows[:border]
-    high_ref[...] = rows[border:]
+    low, high = rows[:border], rows[border:]
+    inner_ref[...] = jnp.where(is_even(), high, low)
+    outer_ref[...] = jnp.where(is_even(), low, high)
 
 
 def spread_form(real_ref, imag_ref):
@@ -231,7 +238,7 @@
     return jnp.where(row // CH == col // CH, form, 0.0).astype(jnp.bfloat16)
 
 
-def prep_body(sentinel, near_ref, index_ref, angle_ref, nr, ni, sr, si, mix_ref, form_ref):
+def prep_body(sentinel, near_ref, index_ref, angle_ref, nr, ni, sr, si, gains, mix_ref, form_ref, gain_ref):
     entries, columns = near_ref.shape
     table = angle_ref[...]
     index = index_ref[...]
@@ -256,16 +263,18 @@
         mix_sin = mix_sin + jnp.where(hit, sine[k : k + 1], 0.0)
     mix_ref[0] = mix_cos.astype(jnp.bfloat16)
     mix_ref[1] = mix_sin.astype(jnp.bfloat16)
+    gain_ref[...] = jnp.concatenate([gains[r : r + 1] for r in range(gains.shape[0])], axis=1)
     form_ref[0] = spread_form(nr, ni)
     form_ref[1] = spread_form(sr, si)
 
 
-def conv_body(x_ref, before_ref, after_ref, mix_ref, form_ref, gain_ref, conv_ref, norm_ref, ext):
+def conv_body(x_ref, inner_ref, outer_ref, mix_ref, form_ref, gain_ref, conv_ref, norm_ref, ext):
     columns, width = x_ref.shape
-    border = before_ref.shape[0]
+    border = inner_ref.shape[0]
+    odd = lax.axis_index("patch") % 2
     ext[:columns] = x_ref[...]
-    ext[columns : columns + border] = before_ref[...]
-    ext[columns + border : columns + 2 * border] = after_ref[...]
+    ext[pl.ds(pl.multiple_of(columns + border * (1 - odd), 16), border)] = inner_ref[...]
+    ext[pl.ds(pl.multiple_of(columns + border * odd, 16), border)] = outer_ref[...]
     rest = ext.shape[0] - columns - 2 * border
     if rest:
         ext[columns + 2 * border :] = jnp.zeros((rest, width), jnp.bfloat16)
@@ -294,35 +303,74 @@
     return jnp.where(place < groups // 2, 2 * place, 2 * (groups - 1 - place) + 1)
 
 
-def column_body(steps, groups, *refs):
+STACK = (1, 3, 0, 2)
+
+
+def early_body(steps, groups, *refs):
     norms, grads, chunks = refs[:TEAM], refs[TEAM : 2 * TEAM], refs[2 * TEAM : 2 * TEAM + len(steps)]
-    mine_ref, cross_ref, send_ref, xs, gs, ups, downs = refs[2 * TEAM + len(steps) :]
+    ups, pre_ref, back_ref, x_last, g_last, xs, gs, downs = refs[2 * TEAM + len(steps) :]
     columns = norms[0].shape[0]
+    span = ups.shape[1]
     me = lax.axis_index("patch")
     group, member = me // TEAM, me % TEAM
     place = ring_place(group, groups)
-    for k in range(TEAM):
-        xs[k * columns : (k + 1) * columns] = norms[k][...]
-        gs[k * columns : (k + 1) * columns] = grads[k][...]
+    for k, m in enumerate(STACK):
+        xs[k * columns : (k + 1) * columns] = norms[m][...]
+        gs[k * columns : (k + 1) * columns] = grads[m][...]
     for (shift, first), ref in zip(steps, chunks):
         rows = ref.shape[1] // 2
         owner = ring_group((place + shift + groups) % groups, groups)
         for half in range(2):
             at = pl.multiple_of((owner * TEAM + (member ^ (first + half))) * rows, 16)
-            span = slice(half * rows, (half + 1) * rows)
-            ups[pl.ds(at, rows)] = ref[0, span]
-            downs[pl.ds(at, rows)] = ref[1, span]
-    pre_act = mm(xs[...], ups[...])
-    back = mm(gs[...], downs[...])
+            part = slice(half * rows, (half + 1) * rows)
+            ups[pl.ds(at, rows)] = ref[0, part]
+            downs[pl.ds(at, rows)] = ref[1, part]
+    owner = ring_group((place + groups // 2) % groups, groups)
+    tall = TEAM * rows
+    blank = jnp.zeros((tall, span), jnp.bfloat16)
+    at = pl.multiple_of(owner * tall, 16)
+    ups[pl.ds(at, tall)] = blank
+    downs[pl.ds(at, tall)] = blank
+    for g in range(groups):
+
+        @pl.when(owner == g)
+        def _():
+            x_last[...] = xs[:, g * tall : (g + 1) * tall]
+            g_last[...] = gs[:, g * tall : (g + 1) * tall]
+
+    pre_ref[...] = mm(xs[...], ups[...])
+    back_ref[...] = mm(gs[...], downs[...])
+
+
+def send_body(groups, ups_in, pre_ref, back_ref, x_last, g_last, first_ref, second_ref, ups, gate_ref, send_ref, up, down):
+    me = lax.axis_index("patch")
+    group, member = me // TEAM, me % TEAM
+    owner = ring_group((ring_place(group, groups) + groups // 2) % groups, groups)
+    rows = first_ref.shape[1] // 2
+    for k, ref in ((0, first_ref), (2, second_ref)):
+        for half in range(2):
+            at = pl.multiple_of((member ^ (k + half)) * rows, 16)
+            part = slice(half * rows, (half + 1) * rows)
+            up[pl.ds(at, rows)] = ref[0, part]
+            down[pl.ds(at, rows)] = ref[1, part]
+    tall = up.shape[0]
+    ups[pl.ds(pl.multiple_of(owner * tall, 16), tall)] = up[...]
+    pre_act = pre_ref[...] + mm(x_last[...], up[...])
+    back = back_ref[...] + mm(g_last[...], down[...])
     gate = jax.nn.sigmoid(pre_act)
     grad_pre = (back * gate * (1.0 + pre_act * (1.0 - gate))).astype(jnp.bfloat16)
-    up = ups[...]
-    for k, (ref, slot) in enumerate(((mine_ref, None), (send_ref, 0), (cross_ref, None), (send_ref, 1))):
-        rows = mm(grad_pre[k * columns : (k + 1) * columns], up, ((1,), (1,)))
-        if slot is None:
-            ref[...] = rows
-        else:
-            ref[slot] = rows.astype(jnp.bfloat16)
+    gate_ref[...] = grad_pre
+    columns = send_ref.shape[1]
+    rows = mm(grad_pre[: 2 * columns], ups[...], ((1,), (1,))).astype(jnp.bfloat16)
+    send_ref[0] = rows[:columns]
+    send_ref[1] = rows[columns:]
+
+
+def keep_body(gate_ref, ups, mine_ref, cross_ref):
+    columns = mine_ref.shape[0]
+    rows = mm(gate_ref[2 * columns :], ups[...], ((1,), (1,)))
+    mine_ref[...] = rows[:columns]
+    cross_ref[...] = rows[columns:]
 
 
 def shifted_back(mix, form, grads):
@@ -339,9 +387,10 @@
     out_ref[...] = (cross_ref[...] + part_ref[1].astype(jnp.float32)).astype(jnp.bfloat16)
 
 
-def grad_body(mine_ref, part_ref, cross_ref, conv_ref, cot_ref, gain_ref, mix_ref, form_ref, grad_ref, prev_ref, next_ref):
+def grad_body(mine_ref, part_ref, cross_ref, conv_ref, cot_ref, gain_ref, mix_ref, form_ref, grad_ref, inner_ref, outer_ref):
     columns, width = conv_ref.shape
-    border = prev_ref.shape[0]
+    border = inner_ref.shape[0]
+    even = is_even()
     grad_normed = mine_ref[...] + part_ref[0].astype(jnp.float32) + cross_ref[...].astype(jnp.float32)
     values = conv_ref[...].astype(jnp.float32)
     scaled = gain_ref[...] * grad_normed
@@ -356,8 +405,9 @@
     for b, rows in enumerate(shifted_back(outer, form_ref[0], grads)):
         at = slice(b * BLOCK, (b + 1) * BLOCK)
         rows = rows.astype(jnp.bfloat16)
-        prev_ref[:, at] = rows[:border]
-        next_ref[:, at] = rows[border : 2 * border]
+        prev, later = rows[:border], rows[border : 2 * border]
+        inner_ref[:, at] = jnp.where(even, later, prev)
+        outer_ref[:, at] = jnp.where(even, prev, later)
 
 
 def own_body(grad_ref, mix_ref, form_ref, local_ref):
@@ -370,12 +420,14 @@
         local_ref[:, at] = own.astype(jnp.float32) + (mm(own, form_ref[1], ((1,), (1,))) + rows)
 
 
-def last_body(local_ref, low_ref, high_ref, bound_ref, out_ref):
-    border = low_ref.shape[0]
+def last_body(local_ref, inner_ref, outer_ref, bound_ref, out_ref):
+    border = inner_ref.shape[0]
     chosen = picked(bound_ref, local_ref.shape[0]).astype(jnp.float32)
-    low = chosen[:, :border].astype(jnp.bfloat16)
-    high = chosen[:, border:].astype(jnp.bfloat16)
-    out_ref[...] = (local_ref[...] + mm(low, low_ref[...]) + mm(high, high_ref[...])).astype(jnp.bfloat16)
+    low, high = chosen[:, :border], chosen[:, border:]
+    inner = jnp.where(is_even(), high, low).astype(jnp.bfloat16)
+    outer = jnp.where(is_even(), low, high).astype(jnp.bfloat16)
+    total = local_ref[...] + mm(inner, inner_ref[...]) + mm(outer, outer_ref[...])
+    out_ref[...] = total.astype(jnp.bfloat16)
 
 
 def per_device(
@@ -432,8 +484,6 @@
     extent = -(-sentinel // 128) * 128
     x = layer_input[0]
     cot = cotangent[0]
-    angles = gauge_angles.reshape(-1, 128)
-    gain = norm_gain.reshape(1, -1)
 
     def permute(value, pairs):
         return lax.ppermute(value, "patch", pairs)
@@ -441,8 +491,8 @@
     def swap(value, bits):
         return permute(value, [(i, i ^ bits) for i in range(devices)])
 
-    def step(value, shift):
-        return permute(value, [(i, (i + shift) % devices) for i in range(devices)])
+    def outer(value):
+        return permute(value, [(i, (i - 1 + 2 * (i % 2)) % devices) for i in range(devices)])
 
     order = list(range(0, groups, 2)) + list(range(groups - 1, 0, -2))
 
@@ -454,13 +504,27 @@
         ]
         return permute(value, pairs)
 
-    parts = call(
-        weights_body,
-        [struct((2, rows, span))] * TEAM,
-        [up_weight, down_weight],
-        [pltpu.SemaphoreType.DMA((2 * TEAM,))],
-        (0, 1),
-    )
+    held = [
+        x,
+        cot,
+        boundary,
+        neighbours.T,
+        gauge_index.T,
+        gauge_angles.reshape(-1, 128),
+        near_real,
+        near_imag,
+        self_real,
+        self_imag,
+        norm_gain.reshape(-1, 128),
+    ]
+    loaded = call(
+        lambda *refs: load_body(len(held), *refs),
+        [struct((2, rows, span))] * TEAM + [struct(value.shape, value.dtype) for value in held],
+        [up_weight, down_weight, *held],
+        [pltpu.SemaphoreType.DMA((2 * TEAM + len(held),))],
+        range(2 + len(held)),
+    )
+    parts, (x, cot, boundary, *tables) = loaded[:TEAM], loaded[TEAM:]
     near_part = swap(parts[1], 1)
     far_parts = [swap(parts[2], 2), swap(parts[3], 3)]
     first = jnp.concatenate([parts[0], near_part], axis=1)
@@ -480,22 +544,26 @@
                 steps.append((s, 2 * which))
                 chunks.append(back[which])
 
-    low, high = call(border_body, [struct((border, width))] * 2, [x, boundary])
-    before = step(high, 1)
-    after = step(low, -1)
+    inner_rows, outer_rows = call(border_body, [struct((border, width))] * 2, [x, boundary])
+    inner_rows = swap(inner_rows, 1)
+    outer_rows = outer(outer_rows)
     cot_near = swap(cot, 1)
     cot_far = swap(cot, 2)
     cot_cross = swap(cot_far, 1)
 
-    mix, form = call(
+    mix, form, gain = call(
         lambda *refs: prep_body(sentinel, *refs),
-        [struct((2, extent, columns)), struct((2, BLOCK, BLOCK))],
-        [neighbours.T, gauge_index.T, angles, near_real, near_imag, self_real, self_imag],
+        [
+            struct((2, extent, columns)),
+            struct((2, BLOCK, BLOCK)),
+            struct((1, width), jnp.float32),
+        ],
+        tables,
     )
     conv, norm = call(
         conv_body,
         [struct((columns, width))] * 2,
-        [x, before, after, mix, form, gain],
+        [x, inner_rows, outer_rows, mix, form, gain],
         [pltpu.VMEM((extent, width), jnp.bfloat16)],
     )
     norm_near = swap(norm, 1)
@@ -503,31 +571,43 @@
     norm_cross = swap(norm_far, 1)
 
     wide = struct((columns, width), jnp.float32)
-    mine, cross, send = call(
-        lambda *refs: column_body(steps, groups, *refs),
-        [wide, wide, struct((2, columns, width))],
-        [norm, norm_near, norm_far, norm_cross, cot, cot_near, cot_far, cot_cross, *chunks],
+    team = TEAM * columns
+    late = len(steps) - 2
+    ups, pre, back_sum, x_last, g_last = call(
+        lambda *refs: early_body(steps[:late], groups, *refs),
+        [struct((width, span))]
+        + [struct((team, span), jnp.float32)] * 2
+        + [struct((team, TEAM * rows))] * 2,
+        [norm, norm_near, norm_far, norm_cross, cot, cot_near, cot_far, cot_cross, *chunks[:late]],
         [
-            pltpu.VMEM((TEAM * columns, width), jnp.bfloat16),
-            pltpu.VMEM((TEAM * columns, width), jnp.bfloat16),
-            pltpu.VMEM((width, span), jnp.bfloat16),
+            pltpu.VMEM((team, width), jnp.bfloat16),
+            pltpu.VMEM((team, width), jnp.bfloat16),
             pltpu.VMEM((width, span), jnp.bfloat16),
         ],
     )
+    ups, gate, send = call(
+        lambda *refs: send_body(groups, *refs),
+        [struct((width, span)), struct((team, span)), struct((2, columns, width))],
+        [ups, pre, back_sum, x_last, g_last, *chunks[late:]],
+        [pltpu.VMEM((TEAM * rows, span), jnp.bfloat16)] * 2,
+        (),
+        ((0, 0),),
+    )
+    mine, cross = call(keep_body, [wide, wide], [gate, ups])
     received = swap(send, 1)
     crossing = call(join_body, struct((columns, width)), [cross, received])
     crossed = swap(crossing, 2)
-    grads, to_prev, to_next = call(
+    grads, inner_back, outer_back = call(
         grad_body,
         [struct((columns, width)), struct((border, width)), struct((border, width))],
         [mine, received, crossed, conv, cot, gain, mix, form],
     )
-    from_prev = step(to_next, 1)
-    from_next = step(to_prev, -1)
+    inner_back = swap(inner_back, 1)
+    outer_back = outer(outer_back)
     local = call(own_body, wide, [grads, mix, form])
     out = pl.pallas_call(
         last_body, out_shape=jax.ShapeDtypeStruct((columns, width), jnp.bfloat16)
-    )(*(pltpu.with_memory_space_constraint(v, pltpu.VMEM) for v in (local, from_prev, from_next, boundary)))
+    )(*(pltpu.with_memory_space_constraint(v, pltpu.VMEM) for v in (local, inner_back, outer_back, boundary)))
     return out[None]
 
 

time: 90.9 us -> 84.6 us (0.931)
  waiting for transfers between devices: 50.2 us -> 44.8 us
  local copies, waits for them, and re-layouts: 2.56 us -> 0.03 us
  Pallas kernels: 9.52 us -> 11.1 us
    ppermute x29, waiting for transfers between devices: 50.2 us -> 44.8 us  [permute(): return lax.ppermute(value, 'patch', pairs)]
    unnamed x28 -> x2, local copies, waits for them, and re-layouts: 2.53 us -> 0.01 us
    pallas_call x8 -> x10, Pallas kernels: 8.43 us -> 9.89 us  [call(): pl.pallas_call(body, out_shape=outs, in_specs=specs, out_specs=jax.tree.m...]
  transfers between devices with their start and end apart: 29 -> 29, of which waited for: 18 -> 15; matrix products, arithmetic and copies ran while one was open for 0% -> 0% of each run, Pallas kernels for 3% -> 7%
where the time goes in v1:
time: 84.6 us; the launch traced here: 84.5 us
  waiting for transfers between devices  44.8 us (53%)
  starting transfers between devices  28.4 us (34%)
  Pallas kernels  11.1 us (13%)
    ppermute x29, waiting for transfers between devices, permute(): return lax.ppermute(value, 'patch', pairs)  44.8 us
    ppermute x29, starting transfers between devices, permute(): return lax.ppermute(value, 'patch', pairs)  28.4 us
    pallas_call x10, Pallas kernels, call(): pl.pallas_call(body, out_shape=outs, in_specs=specs, out_specs=jax.tree.m...  9.89 us
  transfers between devices with their start and end apart: 29, of which 15 were waited for; matrix products, arithmetic and copies ran while one was open for 0% of the time, Pallas kernels for 7%

profile of v1, /device:TPU:0, one launch (start us, length us, event | category | flops | bytes accessed | tf_op | source)
XLA Modules:
  0.0 84.5 jit_solution(4313351002459753428)
XLA Ops:
  0.0 1.5 %shard_map.127 = (bf16[2,48,512]{2,1,0:T(8,128)(2,1)S(1)}, bf16[2,48,512]{2,1,0:T(8,128)(2,1)S(1)}, bf16[2,48,512]{2,1,0:T(8,128)(2,1)S(1)}, bf16[2,48,512]{2,1,...) custom-call(bf16[48,2048]{1,0:T(8,128)(2,1)} %refs_0_.1, ...), custom_call_target="tpu_custom_call" | custom-call | tf_op jit(solution)/shard_map/pallas_call | solution.py:174
  1.5 3.0 %collective-permute-start.9 = (bf16[2,48,512]{2,1,0:T(8,128)(2,1)S(1)}, bf16[2,48,512]{2,1,0:T(8,128)(2,1)S(1)}, u32[]{:S(2)}, u32[]{:S(2)}) collective-permute-start(bf16[2,48,512]{2,1,0:T(8,128)(2,1)S(1)} %get-tuple-element.59), channel_id=1, source_target_pairs={{0,2},{1,3},{2,0},{3,1},{4,6},{5,7},{6,4},{7,5},{8,10},{9,11},{10,... | collective-permute-start | bytes 294920 | tf_op jit(solution)/shard_map/ppermute | solution.py:489
  4.9 4.6 %collective-permute-start.1 = (bf16[32,1536]{1,0:T(8,128)(2,1)S(1)}, bf16[32,1536]{1,0:T(8,128)(2,1)S(1)}, u32[]{:S(2)}, u32[]{:S(2)}) collective-permute-start(bf16[32,1536]{1,0:T(8,128)(2,1)S(1)} %get-tuple-element.43), channel_id=1, source_target_pairs={{0,31},{1,2},{2,1},{3,4},{4,3},{5,6},{6,5},{7,8},{8,7},{9,10},{10,... | collective-permute-start | bytes 294920 | tf_op jit(solution)/shard_map/ppermute | solution.py:489
  10.2 2.2 %collective-permute-start.6 = (bf16[128,1536]{1,0:T(8,128)(2,1)S(1)}, bf16[128,1536]{1,0:T(8,128)(2,1)S(1)}, u32[]{:S(2)}, u32[]{:S(2)}) collective-permute-start(bf16[128,1536]{1,0:T(8,128)(2,1)S(1)} %get-tuple-element.56.refs_4_.cot_ref), channel_id=1, source_target_pairs={{0,2},{1,3},{2,0},{3,1},{4,6},{5,7},{6,4},{7,5},{8,10},{9,11},{10,... | collective-permute-start | bytes 1179656 | tf_op jit(solution)/shard_map/ppermute | solution.py:489
  12.4 1.1 %collective-permute-done.10 = bf16[2,48,512]{2,1,0:T(8,128)(2,1)S(1)} collective-permute-done((bf16[2,48,512]{2,1,0:T(8,128)(2,1)S(1)}, bf16[2,48,512]{2,1,0:T(8,128)(2,1)S(1)}, u32[]{:S(2)}, u32[]{:S(2)}) %collective-permute-start.10) | collective-permute-done | bytes 98336 | tf_op jit(solution)/shard_map/ppermute | solution.py:489
  13.7 2.1 %collective-permute-start.11 = (bf16[2,96,512]{2,1,0:T(8,128)(2,1)S(1)}, bf16[2,96,512]{2,1,0:T(8,128)(2,1)S(1)}, u32[]{:S(2)}, u32[]{:S(2)}) collective-permute-start(bf16[2,96,512]{2,1,0:T(8,128)(2,1)S(1)} %constant_dynamic-update-slice_fusion.refs_8_), channel_id=1, source_target_pairs={{0,8},{1,9},{2,10},{3,11},{8,16},{9,17},{10,18},{11,19},{16,24},{1... | collective-permute-start | bytes 589832 | tf_op jit(solution)/shard_map/ppermute | solution.py:489
  15.7 1.1 %collective-permute-start.13 = (bf16[2,96,512]{2,1,0:T(8,128)(2,1)S(1)}, bf16[2,96,512]{2,1,0:T(8,128)(2,1)S(1)}, u32[]{:S(2)}, u32[]{:S(2)}) collective-permute-start(bf16[2,96,512]{2,1,0:T(8,128)(2,1)S(1)} %constant_dynamic-update-slice_fusion.2.refs_9_), channel_id=1, source_target_pairs={{0,8},{1,9},{2,10},{3,11},{8,16},{9,17},{10,18},{11,19},{16,24},{1... | collective-permute-start | bytes 589832 | tf_op jit(solution)/shard_map/ppermute | solution.py:489
  16.9 1.0 %shard_map.130 = (bf16[128,1536]{1,0:T(8,128)(2,1)S(1)}, bf16[128,1536]{1,0:T(8,128)(2,1)S(1)}) custom-call(bf16[128,1536]{1,0:T(8,128)(2,1)S(1)} %get-tuple-element.40.x_ref, bf16[32,1536]{1,0:T(8,128)(2,1)S(1)} %collective-permute-done.inner_ref, bf16[32,1536]{1,0:T(8,128)(2,1)S(1)} %collective-permute-done.1.outer_ref, ...), custom_call_target="tpu_custom_call" | custom-call | tf_op jit(solution)/shard_map/pallas_call | solution.py:174
  17.8 1.4 %collective-permute-done.14.refs_13_ = bf16[2,96,512]{2,1,0:T(8,128)(2,1)S(1)} collective-permute-done((bf16[2,96,512]{2,1,0:T(8,128)(2,1)S(1)}, bf16[2,96,512]{2,1,0:T(8,128)(2,1)S(1)}, u32[]{:S(2)}, u32[]{:S(2)}) %collective-permute-start.14) | collective-permute-done | bytes 196640 | tf_op jit(solution)/shard_map/ppermute | solution.py:489
  19.8 1.7 %collective-permute-done.11.refs_10_ = bf16[2,96,512]{2,1,0:T(8,128)(2,1)S(1)} collective-permute-done((bf16[2,96,512]{2,1,0:T(8,128)(2,1)S(1)}, bf16[2,96,512]{2,1,0:T(8,128)(2,1)S(1)}, u32[]{:S(2)}, u32[]{:S(2)}) %collective-permute-start.11) | collective-permute-done | bytes 196640 | tf_op jit(solution)/shard_map/ppermute | solution.py:489
  21.6 4.1 %collective-permute-done.13.refs_12_ = bf16[2,96,512]{2,1,0:T(8,128)(2,1)S(1)} collective-permute-done((bf16[2,96,512]{2,1,0:T(8,128)(2,1)S(1)}, bf16[2,96,512]{2,1,0:T(8,128)(2,1)S(1)}, u32[]{:S(2)}, u32[]{:S(2)}) %collective-permute-start.13) | collective-permute-done | bytes 196640 | tf_op jit(solution)/shard_map/ppermute | solution.py:489
  25.7 1.6 %collective-permute-start.12 = (bf16[2,96,512]{2,1,0:T(8,128)(2,1)S(1)}, bf16[2,96,512]{2,1,0:T(8,128)(2,1)S(1)}, u32[]{:S(2)}, u32[]{:S(2)}) collective-permute-start(bf16[2,96,512]{2,1,0:T(8,128)(2,1)S(1)} %constant_dynamic-update-slice_fusion.refs_8_), channel_id=1, source_target_pairs={{0,4},{1,5},{2,6},{3,7},{8,0},{9,1},{10,2},{11,3},{16,8},{17,9},{1... | collective-permute-start | bytes 589832 | tf_op jit(solution)/shard_map/ppermute | solution.py:489
  27.2 5.3 %collective-permute-done.12.refs_11_ = bf16[2,96,512]{2,1,0:T(8,128)(2,1)S(1)} collective-permute-done((bf16[2,96,512]{2,1,0:T(8,128)(2,1)S(1)}, bf16[2,96,512]{2,1,0:T(8,128)(2,1)S(1)}, u32[]{:S(2)}, u32[]{:S(2)}) %collective-permute-start.12) | collective-permute-done | bytes 196640 | tf_op jit(solution)/shard_map/ppermute | solution.py:489
  32.6 1.6 %collective-permute-start.18 = (bf16[2,96,512]{2,1,0:T(8,128)(2,1)S(1)}, bf16[2,96,512]{2,1,0:T(8,128)(2,1)S(1)}, u32[]{:S(2)}, u32[]{:S(2)}) collective-permute-start(bf16[2,96,512]{2,1,0:T(8,128)(2,1)S(1)} %collective-permute-done.14.refs_13_), channel_id=1, source_target_pairs={{0,4},{1,5},{2,6},{3,7},{8,0},{9,1},{10,2},{11,3},{16,8},{17,9},{1... | collective-permute-start | bytes 589832 | tf_op jit(solution)/shard_map/ppermute | solution.py:489
  34.7 2.0 %collective-permute-start.16 = (bf16[2,96,512]{2,1,0:T(8,128)(2,1)S(1)}, bf16[2,96,512]{2,1,0:T(8,128)(2,1)S(1)}, u32[]{:S(2)}, u32[]{:S(2)}) collective-permute-start(bf16[2,96,512]{2,1,0:T(8,128)(2,1)S(1)} %collective-permute-done.12.refs_11_), channel_id=1, source_target_pairs={{0,4},{1,5},{2,6},{3,7},{8,0},{9,1},{10,2},{11,3},{16,8},{17,9},{1... | collective-permute-start | bytes 589832 | tf_op jit(solution)/shard_map/ppermute | solution.py:489
  36.7 3.7 %collective-permute-done.18.refs_17_ = bf16[2,96,512]{2,1,0:T(8,128)(2,1)S(1)} collective-permute-done((bf16[2,96,512]{2,1,0:T(8,128)(2,1)S(1)}, bf16[2,96,512]{2,1,0:T(8,128)(2,1)S(1)}, u32[]{:S(2)}, u32[]{:S(2)}) %collective-permute-start.18) | collective-permute-done | bytes 196640 | tf_op jit(solution)/shard_map/ppermute | solution.py:489
  40.4 1.6 %collective-permute-start.22 = (bf16[2,96,512]{2,1,0:T(8,128)(2,1)S(1)}, bf16[2,96,512]{2,1,0:T(8,128)(2,1)S(1)}, u32[]{:S(2)}, u32[]{:S(2)}) collective-permute-start(bf16[2,96,512]{2,1,0:T(8,128)(2,1)S(1)} %collective-permute-done.18.refs_17_), channel_id=1, source_target_pairs={{0,4},{1,5},{2,6},{3,7},{8,0},{9,1},{10,2},{11,3},{16,8},{17,9},{1... | collective-permute-start | bytes 589832 | tf_op jit(solution)/shard_map/ppermute | solution.py:489
  42.0 2.2 %collective-permute-done.17.refs_16_ = bf16[2,96,512]{2,1,0:T(8,128)(2,1)S(1)} collective-permute-done((bf16[2,96,512]{2,1,0:T(8,128)(2,1)S(1)}, bf16[2,96,512]{2,1,0:T(8,128)(2,1)S(1)}, u32[]{:S(2)}, u32[]{:S(2)}) %collective-permute-start.17) | collective-permute-done | bytes 196640 | tf_op jit(solution)/shard_map/ppermute | solution.py:489
  44.9 2.2 %collective-permute-done.22.refs_21_ = bf16[2,96,512]{2,1,0:T(8,128)(2,1)S(1)} collective-permute-done((bf16[2,96,512]{2,1,0:T(8,128)(2,1)S(1)}, bf16[2,96,512]{2,1,0:T(8,128)(2,1)S(1)}, u32[]{:S(2)}, u32[]{:S(2)}) %collective-permute-start.22) | collective-permute-done | bytes 196640 | tf_op jit(solution)/shard_map/ppermute | solution.py:489
  47.0 1.6 %collective-permute-start.20 = (bf16[2,96,512]{2,1,0:T(8,128)(2,1)S(1)}, bf16[2,96,512]{2,1,0:T(8,128)(2,1)S(1)}, u32[]{:S(2)}, u32[]{:S(2)}) collective-permute-start(bf16[2,96,512]{2,1,0:T(8,128)(2,1)S(1)} %collective-permute-done.16.refs_15_), channel_id=1, source_target_pairs={{0,4},{1,5},{2,6},{3,7},{8,0},{9,1},{10,2},{11,3},{16,8},{17,9},{1... | collective-permute-start | bytes 589832 | tf_op jit(solution)/shard_map/ppermute | solution.py:489
  48.7 2.7 %collective-permute-done.19.refs_18_ = bf16[2,96,512]{2,1,0:T(8,128)(2,1)S(1)} collective-permute-done((bf16[2,96,512]{2,1,0:T(8,128)(2,1)S(1)}, bf16[2,96,512]{2,1,0:T(8,128)(2,1)S(1)}, u32[]{:S(2)}, u32[]{:S(2)}) %collective-permute-start.19) | collective-permute-done | bytes 196640 | tf_op jit(solution)/shard_map/ppermute | solution.py:489
  51.4 2.3 %collective-permute-start.24 = (bf16[2,96,512]{2,1,0:T(8,128)(2,1)S(1)}, bf16[2,96,512]{2,1,0:T(8,128)(2,1)S(1)}, u32[]{:S(2)}, u32[]{:S(2)}) collective-permute-start(bf16[2,96,512]{2,1,0:T(8,128)(2,1)S(1)} %collective-permute-done.22.refs_21_), channel_id=1, source_target_pairs={{0,4},{1,5},{2,6},{3,7},{8,0},{9,1},{10,2},{11,3},{16,8},{17,9},{1... | collective-permute-start | bytes 589832 | tf_op jit(solution)/shard_map/ppermute | solution.py:489
  54.3 2.5 %shard_map.131 = (bf16[1536,512]{1,0:T(8,128)(2,1)S(1)}, f32[512,512]{1,0:T(8,128)S(1)}, f32[512,512]{1,0:T(8,128)S(1)}, bf16[512,192]{1,0:T(8,128)(2,1)S(1)}, bf16[512,192]{1,0:T(8,128)(2,1)S(1)}) custom-call(bf16[128,1536]{1,0:T(8,128)(2,1)S(1)} %get-tuple-element.55.refs_0_, bf16[128,1536]{1,0:T(8,128)(2,1)S(1)} %collective-permute-done.2.refs_1_, ...), custom_call_target="tpu_custom_call" | custom-call | tf_op jit(solution)/shard_map/pallas_call | solution.py:174
  57.1 2.4 %collective-permute-done.23.refs_5_ = bf16[2,96,512]{2,1,0:T(8,128)(2,1)S(1)} collective-permute-done((bf16[2,96,512]{2,1,0:T(8,128)(2,1)S(1)}, bf16[2,96,512]{2,1,0:T(8,128)(2,1)S(1)}, u32[]{:S(2)}, u32[]{:S(2)}) %collective-permute-start.23) | collective-permute-done | bytes 196640 | tf_op jit(solution)/shard_map/ppermute | solution.py:489
  59.5 1.0 %shard_map.132 = (bf16[1536,512]{1,0:T(8,128)(2,1)S(1)}, bf16[512,512]{1,0:T(8,128)(2,1)S(1)}, bf16[2,128,1536]{2,1,0:T(8,128)(2,1)S(1)}) custom-call(bf16[1536,512]{1,0:T(8,128)(2,1)S(1)} %get-tuple-element.61.refs_0_, f32[512,512]{1,0:T(8,128)S(1)} %get-tuple-element.62.refs_1_, ...), custom_call_target="tpu_custom_call", output_to_operand_aliasing={{0}: (0, {})} | custom-call | tf_op jit(solution)/shard_map/pallas_call | solution.py:174
  61.3 1.7 %collective-permute-done.25.part_ref = bf16[2,128,1536]{2,1,0:T(8,128)(2,1)S(1)} collective-permute-done((bf16[2,128,1536]{2,1,0:T(8,128)(2,1)S(1)}, bf16[2,128,1536]{2,1,0:T(8,128)(2,1)S(1)}, u32[]{:S(2)}, u32[]{:S(2)}) %collective-permute-start.25) | collective-permute-done | bytes 786464 | tf_op jit(solution)/shard_map/ppermute | solution.py:489
  63.1 11.1 %collective-permute-done.26.cross_ref = bf16[128,1536]{1,0:T(8,128)(2,1)S(1)} collective-permute-done((bf16[128,1536]{1,0:T(8,128)(2,1)S(1)}, bf16[128,1536]{1,0:T(8,128)(2,1)S(1)}, u32[]{:S(2)}, u32[]{:S(2)}) %collective-permute-start.26) | collective-permute-done | bytes 393248 | tf_op jit(solution)/shard_map/ppermute | solution.py:489
  74.2 1.2 %shard_map.135 = (bf16[128,1536]{1,0:T(8,128)(2,1)S(1)}, bf16[32,1536]{1,0:T(8,128)(2,1)S(1)}, bf16[32,1536]{1,0:T(8,128)(2,1)S(1)}) custom-call(f32[128,1536]{1,0:T(8,128)S(1)} %get-tuple-element.68.mine_ref, bf16[2,128,1536]{2,1,0:T(8,128)(2,1)S(1)} %collective-permute-done.25.part_ref, bf16[128,1536]{1,0:T(8,128)(2,1)S(1)} %collective-permute-done.26.cross_ref, ...), custom_call_target="tpu_custom_call" | custom-call | tf_op jit(solution)/shard_map/pallas_call | solution.py:174
  75.6 2.3 %collective-permute-start.28 = (bf16[32,1536]{1,0:T(8,128)(2,1)S(1)}, bf16[32,1536]{1,0:T(8,128)(2,1)S(1)}, u32[]{:S(2)}, u32[]{:S(2)}) collective-permute-start(bf16[32,1536]{1,0:T(8,128)(2,1)S(1)} %get-tuple-element.74), channel_id=1, source_target_pairs={{0,31},{1,2},{2,1},{3,4},{4,3},{5,6},{6,5},{7,8},{8,7},{9,10},{10,... | collective-permute-start | bytes 294920 | tf_op jit(solution)/shard_map/ppermute | solution.py:489
  77.9 1.1 %shard_map.136.local_ref = f32[128,1536]{1,0:T(8,128)S(1)} custom-call(bf16[128,1536]{1,0:T(8,128)(2,1)S(1)} %get-tuple-element.72.grad_ref, bf16[2,256,128]{2,1,0:T(8,128)(2,1)S(1)} %get-tuple-element.52.mix_ref, bf16[2,256,256]{2,1,0:T(8,128)(2,1)S(1)} %get-tuple-element.53.form_ref), custom_call_target="tpu_custom_call" | custom-call | tf_op jit(solution)/shard_map/pallas_call | solution.py:174
  79.0 4.3 %collective-permute-done.28.outer_ref = bf16[32,1536]{1,0:T(8,128)(2,1)S(1)} collective-permute-done((bf16[32,1536]{1,0:T(8,128)(2,1)S(1)}, bf16[32,1536]{1,0:T(8,128)(2,1)S(1)}, u32[]{:S(2)}, u32[]{:S(2)}) %collective-permute-start.28) | collective-permute-done | bytes 98336 | tf_op jit(solution)/shard_map/ppermute | solution.py:489
  83.3 1.2 %shard_map.137 = bf16[128,1536]{1,0:T(8,128)(2,1)} custom-call(f32[128,1536]{1,0:T(8,128)S(1)} %shard_map.136.local_ref, bf16[32,1536]{1,0:T(8,128)(2,1)S(1)} %collective-permute-done.27.inner_ref, bf16[32,1536]{1,0:T(8,128)(2,1)S(1)} %collective-permute-done.28.outer_ref, s32[1,64]{1,0:T(1,128)S(1)} %get-tuple-element.41.bound_ref), custom_call_target="tpu_custom_call" | custom-call | tf_op jit(solution)/shard_map/pallas_call | solution.py:608
  (41 shorter events, 4.7 us)
Async XLA Ops:
  1.5 8.7 %collective-permute-start.9 = (bf16[2,48,512]{2,1,0:T(8,128)(2,1)S(1)}, bf16[2,48,512]{2,1,0:T(8,128)(2,1)S(1)}, u32[]{:S(2)}, u32[]{:S(2)}) collective-permute-start(bf16[2,48,512]{2,1,0:T(8,128)(2,1)S(1)} %get-tuple-element.59), channel_id=1, source_target_pairs={{0,2},{1,3},{2,0},{3,1},{4,6},{5,7},{6,4},{7,5},{8,10},{9,11},{10,... | collective-permute-start | bytes 294920 | tf_op jit(solution)/shard_map/ppermute | solution.py:489
  4.8 10.9 %collective-permute-start = (bf16[32,1536]{1,0:T(8,128)(2,1)S(1)}, bf16[32,1536]{1,0:T(8,128)(2,1)S(1)}, u32[]{:S(2)}, u32[]{:S(2)}) collective-permute-start(bf16[32,1536]{1,0:T(8,128)(2,1)S(1)} %get-tuple-element.42), channel_id=1, source_target_pairs={{0,1},{1,0},{2,3},{3,2},{4,5},{5,4},{6,7},{7,6},{8,9},{9,8},{10,11... | collective-permute-start | bytes 294920 | tf_op jit(solution)/shard_map/ppermute | solution.py:489
  4.9 12.0 %collective-permute-start.1 = (bf16[32,1536]{1,0:T(8,128)(2,1)S(1)}, bf16[32,1536]{1,0:T(8,128)(2,1)S(1)}, u32[]{:S(2)}, u32[]{:S(2)}) collective-permute-start(bf16[32,1536]{1,0:T(8,128)(2,1)S(1)} %get-tuple-element.43), channel_id=1, source_target_pairs={{0,31},{1,2},{2,1},{3,4},{4,3},{5,6},{6,5},{7,8},{8,7},{9,10},{10,... | collective-permute-start | bytes 294920 | tf_op jit(solution)/shard_map/ppermute | solution.py:489
  9.5 4.0 %collective-permute-start.10 = (bf16[2,48,512]{2,1,0:T(8,128)(2,1)S(1)}, bf16[2,48,512]{2,1,0:T(8,128)(2,1)S(1)}, u32[]{:S(2)}, u32[]{:S(2)}) collective-permute-start(bf16[2,48,512]{2,1,0:T(8,128)(2,1)S(1)} %get-tuple-element.60), channel_id=1, source_target_pairs={{0,3},{1,2},{2,1},{3,0},{4,7},{5,6},{6,5},{7,4},{8,11},{9,10},{10,... | collective-permute-start | bytes 294920 | tf_op jit(solution)/shard_map/ppermute | solution.py:489
  9.5 4.1 %collective-permute-start.8 = (bf16[2,48,512]{2,1,0:T(8,128)(2,1)S(1)}, bf16[2,48,512]{2,1,0:T(8,128)(2,1)S(1)}, u32[]{:S(2)}, u32[]{:S(2)}) collective-permute-start(bf16[2,48,512]{2,1,0:T(8,128)(2,1)S(1)} %get-tuple-element.58), channel_id=1, source_target_pairs={{0,1},{1,0},{2,3},{3,2},{4,5},{5,4},{6,7},{7,6},{8,9},{9,8},{10,11... | collective-permute-start | bytes 294920 | tf_op jit(solution)/shard_map/ppermute | solution.py:489
  10.2 24.0 %collective-permute-start.6 = (bf16[128,1536]{1,0:T(8,128)(2,1)S(1)}, bf16[128,1536]{1,0:T(8,128)(2,1)S(1)}, u32[]{:S(2)}, u32[]{:S(2)}) collective-permute-start(bf16[128,1536]{1,0:T(8,128)(2,1)S(1)} %get-tuple-element.56.refs_4_.cot_ref), channel_id=1, source_target_pairs={{0,2},{1,3},{2,0},{3,1},{4,6},{5,7},{6,4},{7,5},{8,10},{9,11},{10,... | collective-permute-start | bytes 1179656 | tf_op jit(solution)/shard_map/ppermute | solution.py:489
  13.6 5.7 %collective-permute-start.14 = (bf16[2,96,512]{2,1,0:T(8,128)(2,1)S(1)}, bf16[2,96,512]{2,1,0:T(8,128)(2,1)S(1)}, u32[]{:S(2)}, u32[]{:S(2)}) collective-permute-start(bf16[2,96,512]{2,1,0:T(8,128)(2,1)S(1)} %constant_dynamic-update-slice_fusion.2.refs_9_), channel_id=1, source_target_pairs={{0,4},{1,5},{2,6},{3,7},{8,0},{9,1},{10,2},{11,3},{16,8},{17,9},{1... | collective-permute-start | bytes 589832 | tf_op jit(solution)/shard_map/ppermute | solution.py:489
  13.7 7.8 %collective-permute-start.11 = (bf16[2,96,512]{2,1,0:T(8,128)(2,1)S(1)}, bf16[2,96,512]{2,1,0:T(8,128)(2,1)S(1)}, u32[]{:S(2)}, u32[]{:S(2)}) collective-permute-start(bf16[2,96,512]{2,1,0:T(8,128)(2,1)S(1)} %constant_dynamic-update-slice_fusion.refs_8_), channel_id=1, source_target_pairs={{0,8},{1,9},{2,10},{3,11},{8,16},{9,17},{10,18},{11,19},{16,24},{1... | collective-permute-start | bytes 589832 | tf_op jit(solution)/shard_map/ppermute | solution.py:489
  15.7 10.0 %collective-permute-start.13 = (bf16[2,96,512]{2,1,0:T(8,128)(2,1)S(1)}, bf16[2,96,512]{2,1,0:T(8,128)(2,1)S(1)}, u32[]{:S(2)}, u32[]{:S(2)}) collective-permute-start(bf16[2,96,512]{2,1,0:T(8,128)(2,1)S(1)} %constant_dynamic-update-slice_fusion.2.refs_9_), channel_id=1, source_target_pairs={{0,8},{1,9},{2,10},{3,11},{8,16},{9,17},{10,18},{11,19},{16,24},{1... | collective-permute-start | bytes 589832 | tf_op jit(solution)/shard_map/ppermute | solution.py:489
  16.9 17.8 %collective-permute-start.5 = (bf16[128,1536]{1,0:T(8,128)(2,1)S(1)}, bf16[128,1536]{1,0:T(8,128)(2,1)S(1)}, u32[]{:S(2)}, u32[]{:S(2)}) collective-permute-start(bf16[128,1536]{1,0:T(8,128)(2,1)S(1)} %get-tuple-element.56.refs_4_.cot_ref), channel_id=1, source_target_pairs={{0,1},{1,0},{2,3},{3,2},{4,5},{5,4},{6,7},{7,6},{8,9},{9,8},{10,11... | collective-permute-start | bytes 1179656 | tf_op jit(solution)/shard_map/ppermute | solution.py:489
  19.3 15.4 %collective-permute-start.3 = (bf16[128,1536]{1,0:T(8,128)(2,1)S(1)}, bf16[128,1536]{1,0:T(8,128)(2,1)S(1)}, u32[]{:S(2)}, u32[]{:S(2)}) collective-permute-start(bf16[128,1536]{1,0:T(8,128)(2,1)S(1)} %get-tuple-element.55.refs_0_), channel_id=1, source_target_pairs={{0,2},{1,3},{2,0},{3,1},{4,6},{5,7},{6,4},{7,5},{8,10},{9,11},{10,... | collective-permute-start | bytes 1179656 | tf_op jit(solution)/shard_map/ppermute | solution.py:489
  21.5 15.2 %collective-permute-start.2 = (bf16[128,1536]{1,0:T(8,128)(2,1)S(1)}, bf16[128,1536]{1,0:T(8,128)(2,1)S(1)}, u32[]{:S(2)}, u32[]{:S(2)}) collective-permute-start(bf16[128,1536]{1,0:T(8,128)(2,1)S(1)} %get-tuple-element.55.refs_0_), channel_id=1, source_target_pairs={{0,1},{1,0},{2,3},{3,2},{4,5},{5,4},{6,7},{7,6},{8,9},{9,8},{10,11... | collective-permute-start | bytes 1179656 | tf_op jit(solution)/shard_map/ppermute | solution.py:489
  25.7 6.9 %collective-permute-start.12 = (bf16[2,96,512]{2,1,0:T(8,128)(2,1)S(1)}, bf16[2,96,512]{2,1,0:T(8,128)(2,1)S(1)}, u32[]{:S(2)}, u32[]{:S(2)}) collective-permute-start(bf16[2,96,512]{2,1,0:T(8,128)(2,1)S(1)} %constant_dynamic-update-slice_fusion.refs_8_), channel_id=1, source_target_pairs={{0,4},{1,5},{2,6},{3,7},{8,0},{9,1},{10,2},{11,3},{16,8},{17,9},{1... | collective-permute-start | bytes 589832 | tf_op jit(solution)/shard_map/ppermute | solution.py:489
  32.6 7.8 %collective-permute-start.18 = (bf16[2,96,512]{2,1,0:T(8,128)(2,1)S(1)}, bf16[2,96,512]{2,1,0:T(8,128)(2,1)S(1)}, u32[]{:S(2)}, u32[]{:S(2)}) collective-permute-start(bf16[2,96,512]{2,1,0:T(8,128)(2,1)S(1)} %collective-permute-done.14.refs_13_), channel_id=1, source_target_pairs={{0,4},{1,5},{2,6},{3,7},{8,0},{9,1},{10,2},{11,3},{16,8},{17,9},{1... | collective-permute-start | bytes 589832 | tf_op jit(solution)/shard_map/ppermute | solution.py:489
  34.2 7.8 %collective-permute-start.15 = (bf16[2,96,512]{2,1,0:T(8,128)(2,1)S(1)}, bf16[2,96,512]{2,1,0:T(8,128)(2,1)S(1)}, u32[]{:S(2)}, u32[]{:S(2)}) collective-permute-start(bf16[2,96,512]{2,1,0:T(8,128)(2,1)S(1)} %collective-permute-done.11.refs_10_), channel_id=1, source_target_pairs={{0,8},{1,9},{2,10},{3,11},{8,16},{9,17},{10,18},{11,19},{16,24},{1... | collective-permute-start | bytes 589832 | tf_op jit(solution)/shard_map/ppermute | solution.py:489
  34.6 9.6 %collective-permute-start.17 = (bf16[2,96,512]{2,1,0:T(8,128)(2,1)S(1)}, bf16[2,96,512]{2,1,0:T(8,128)(2,1)S(1)}, u32[]{:S(2)}, u32[]{:S(2)}) collective-permute-start(bf16[2,96,512]{2,1,0:T(8,128)(2,1)S(1)} %collective-permute-done.13.refs_12_), channel_id=1, source_target_pairs={{0,8},{1,9},{2,10},{3,11},{8,16},{9,17},{10,18},{11,19},{16,24},{1... | collective-permute-start | bytes 589832 | tf_op jit(solution)/shard_map/ppermute | solution.py:489
  34.7 9.9 %collective-permute-start.16 = (bf16[2,96,512]{2,1,0:T(8,128)(2,1)S(1)}, bf16[2,96,512]{2,1,0:T(8,128)(2,1)S(1)}, u32[]{:S(2)}, u32[]{:S(2)}) collective-permute-start(bf16[2,96,512]{2,1,0:T(8,128)(2,1)S(1)} %collective-permute-done.12.refs_11_), channel_id=1, source_target_pairs={{0,4},{1,5},{2,6},{3,7},{8,0},{9,1},{10,2},{11,3},{16,8},{17,9},{1... | collective-permute-start | bytes 589832 | tf_op jit(solution)/shard_map/ppermute | solution.py:489
  36.6 17.7 %collective-permute-start.7 = (bf16[128,1536]{1,0:T(8,128)(2,1)S(1)}, bf16[128,1536]{1,0:T(8,128)(2,1)S(1)}, u32[]{:S(2)}, u32[]{:S(2)}) collective-permute-start(bf16[128,1536]{1,0:T(8,128)(2,1)S(1)} %collective-permute-done.6.refs_6_), channel_id=1, source_target_pairs={{0,1},{1,0},{2,3},{3,2},{4,5},{5,4},{6,7},{7,6},{8,9},{9,8},{10,11... | collective-permute-start | bytes 1179656 | tf_op jit(solution)/shard_map/ppermute | solution.py:489
  40.4 6.7 %collective-permute-start.22 = (bf16[2,96,512]{2,1,0:T(8,128)(2,1)S(1)}, bf16[2,96,512]{2,1,0:T(8,128)(2,1)S(1)}, u32[]{:S(2)}, u32[]{:S(2)}) collective-permute-start(bf16[2,96,512]{2,1,0:T(8,128)(2,1)S(1)} %collective-permute-done.18.refs_17_), channel_id=1, source_target_pairs={{0,4},{1,5},{2,6},{3,7},{8,0},{9,1},{10,2},{11,3},{16,8},{17,9},{1... | collective-permute-start | bytes 589832 | tf_op jit(solution)/shard_map/ppermute | solution.py:489
  42.0 12.4 %collective-permute-start.4 = (bf16[128,1536]{1,0:T(8,128)(2,1)S(1)}, bf16[128,1536]{1,0:T(8,128)(2,1)S(1)}, u32[]{:S(2)}, u32[]{:S(2)}) collective-permute-start(bf16[128,1536]{1,0:T(8,128)(2,1)S(1)} %collective-permute-done.3.refs_2_), channel_id=1, source_target_pairs={{0,1},{1,0},{2,3},{3,2},{4,5},{5,4},{6,7},{7,6},{8,9},{9,8},{10,11... | collective-permute-start | bytes 1179656 | tf_op jit(solution)/shard_map/ppermute | solution.py:489
  44.2 7.2 %collective-permute-start.19 = (bf16[2,96,512]{2,1,0:T(8,128)(2,1)S(1)}, bf16[2,96,512]{2,1,0:T(8,128)(2,1)S(1)}, u32[]{:S(2)}, u32[]{:S(2)}) collective-permute-start(bf16[2,96,512]{2,1,0:T(8,128)(2,1)S(1)} %collective-permute-done.15.refs_14_), channel_id=1, source_target_pairs={{0,8},{1,9},{2,10},{3,11},{8,16},{9,17},{10,18},{11,19},{16,24},{1... | collective-permute-start | bytes 589832 | tf_op jit(solution)/shard_map/ppermute | solution.py:489
  44.6 9.1 %collective-permute-start.21 = (bf16[2,96,512]{2,1,0:T(8,128)(2,1)S(1)}, bf16[2,96,512]{2,1,0:T(8,128)(2,1)S(1)}, u32[]{:S(2)}, u32[]{:S(2)}) collective-permute-start(bf16[2,96,512]{2,1,0:T(8,128)(2,1)S(1)} %collective-permute-done.17.refs_16_), channel_id=1, source_target_pairs={{0,8},{1,9},{2,10},{3,11},{8,16},{9,17},{10,18},{11,19},{16,24},{1... | collective-permute-start | bytes 589832 | tf_op jit(solution)/shard_map/ppermute | solution.py:489
  47.0 7.3 %collective-permute-start.20 = (bf16[2,96,512]{2,1,0:T(8,128)(2,1)S(1)}, bf16[2,96,512]{2,1,0:T(8,128)(2,1)S(1)}, u32[]{:S(2)}, u32[]{:S(2)}) collective-permute-start(bf16[2,96,512]{2,1,0:T(8,128)(2,1)S(1)} %collective-permute-done.16.refs_15_), channel_id=1, source_target_pairs={{0,4},{1,5},{2,6},{3,7},{8,0},{9,1},{10,2},{11,3},{16,8},{17,9},{1... | collective-permute-start | bytes 589832 | tf_op jit(solution)/shard_map/ppermute | solution.py:489
  51.4 5.7 %collective-permute-start.24 = (bf16[2,96,512]{2,1,0:T(8,128)(2,1)S(1)}, bf16[2,96,512]{2,1,0:T(8,128)(2,1)S(1)}, u32[]{:S(2)}, u32[]{:S(2)}) collective-permute-start(bf16[2,96,512]{2,1,0:T(8,128)(2,1)S(1)} %collective-permute-done.22.refs_21_), channel_id=1, source_target_pairs={{0,4},{1,5},{2,6},{3,7},{8,0},{9,1},{10,2},{11,3},{16,8},{17,9},{1... | collective-permute-start | bytes 589832 | tf_op jit(solution)/shard_map/ppermute | solution.py:489
  53.7 5.8 %collective-permute-start.23 = (bf16[2,96,512]{2,1,0:T(8,128)(2,1)S(1)}, bf16[2,96,512]{2,1,0:T(8,128)(2,1)S(1)}, u32[]{:S(2)}, u32[]{:S(2)}) collective-permute-start(bf16[2,96,512]{2,1,0:T(8,128)(2,1)S(1)} %collective-permute-done.19.refs_18_), channel_id=1, source_target_pairs={{0,8},{1,9},{2,10},{3,11},{8,16},{9,17},{10,18},{11,19},{16,24},{1... | collective-permute-start | bytes 589832 | tf_op jit(solution)/shard_map/ppermute | solution.py:489
  60.6 2.4 %collective-permute-start.25 = (bf16[2,128,1536]{2,1,0:T(8,128)(2,1)S(1)}, bf16[2,128,1536]{2,1,0:T(8,128)(2,1)S(1)}, u32[]{:S(2)}, u32[]{:S(2)}) collective-permute-start(bf16[2,128,1536]{2,1,0:T(8,128)(2,1)S(1)} %get-tuple-element.69), channel_id=1, source_target_pairs={{0,1},{1,0},{2,3},{3,2},{4,5},{5,4},{6,7},{7,6},{8,9},{9,8},{10,11... | collective-permute-start | bytes 2359304 | tf_op jit(solution)/shard_map/ppermute | solution.py:489
  63.0 11.2 %collective-permute-start.26 = (bf16[128,1536]{1,0:T(8,128)(2,1)S(1)}, bf16[128,1536]{1,0:T(8,128)(2,1)S(1)}, u32[]{:S(2)}, u32[]{:S(2)}) collective-permute-start(bf16[128,1536]{1,0:T(8,128)(2,1)S(1)} %shard_map.134), channel_id=1, source_target_pairs={{0,2},{1,3},{2,0},{3,1},{4,6},{5,7},{6,4},{7,5},{8,10},{9,11},{10,... | collective-permute-start | bytes 1179656 | tf_op jit(solution)/shard_map/ppermute | solution.py:489
  75.5 3.5 %collective-permute-start.27 = (bf16[32,1536]{1,0:T(8,128)(2,1)S(1)}, bf16[32,1536]{1,0:T(8,128)(2,1)S(1)}, u32[]{:S(2)}, u32[]{:S(2)}) collective-permute-start(bf16[32,1536]{1,0:T(8,128)(2,1)S(1)} %get-tuple-element.73), channel_id=1, source_target_pairs={{0,1},{1,0},{2,3},{3,2},{4,5},{5,4},{6,7},{7,6},{8,9},{9,8},{10,11... | collective-permute-start | bytes 294920 | tf_op jit(solution)/shard_map/ppermute | solution.py:489
  75.6 7.7 %collective-permute-start.28 = (bf16[32,1536]{1,0:T(8,128)(2,1)S(1)}, bf16[32,1536]{1,0:T(8,128)(2,1)S(1)}, u32[]{:S(2)}, u32[]{:S(2)}) collective-permute-start(bf16[32,1536]{1,0:T(8,128)(2,1)S(1)} %get-tuple-element.74), channel_id=1, source_target_pairs={{0,31},{1,2},{2,1},{3,4},{4,3},{5,6},{6,5},{7,8},{8,7},{9,10},{10,... | collective-permute-start | bytes 294920 | tf_op jit(solution)/shard_map/ppermute | solution.py:489

commit v2 on v1

--- a/solution.py
+++ b/solution.py
@@ -191,10 +191,16 @@
     return (iota((columns, count), 0) == bound_ref[...]).astype(jnp.bfloat16)
 
 
-def load_body(count, *refs):
-    up_ref, down_ref, *sources = refs[: 2 + count]
-    parts = refs[2 + count : 2 + count + TEAM]
-    *targets, sem = refs[2 + count + TEAM :]
+def copy_all(pairs, sem):
+    copies = [pltpu.make_async_copy(src, dst, sem.at[i]) for i, (src, dst) in enumerate(pairs)]
+    for one in copies:
+        one.start()
+    for one in copies:
+        one.wait()
+
+
+def weights_body(up_ref, down_ref, *refs):
+    *parts, sem = refs
     mine = lax.axis_index("patch") % TEAM
     span = parts[0].shape[2]
     pairs = []
@@ -202,12 +208,11 @@
         at = pl.multiple_of((mine ^ k) * span, 128)
         for which, ref in enumerate((up_ref, down_ref)):
             pairs.append((ref.at[:, pl.ds(at, span)], parts[k].at[which]))
-    pairs += zip(sources, targets)
-    copies = [pltpu.make_async_copy(src, dst, sem.at[i]) for i, (src, dst) in enumerate(pairs)]
-    for one in copies:
-        one.start()
-    for one in copies:
-        one.wait()
+    copy_all(pairs, sem)
+
+
+def load_body(count, *refs):
+    copy_all(list(zip(refs[:count], refs[count : 2 * count])), refs[-1])
 
 
 def is_even():
@@ -268,7 +273,12 @@
     form_ref[1] = spread_form(sr, si)
 
 
-def conv_body(x_ref, inner_ref, outer_ref, mix_ref, form_ref, gain_ref, conv_ref, norm_ref, ext):
+def border_mix(mix_ref, columns, border, which):
+    at = pl.multiple_of(columns + border * which, 16)
+    return [mix_ref[i, pl.ds(at, border)] for i in range(2)]
+
+
+def conv_body(x_ref, inner_ref, outer_ref, mix_ref, form_ref, gain_ref, conv_ref, norm_ref, edge_ref, ext):
     columns, width = x_ref.shape
     border = inner_ref.shape[0]
     odd = lax.axis_index("patch") % 2
@@ -293,6 +303,9 @@
         square = square + out * out
     scale = lax.rsqrt(jnp.sum(square, axis=1, keepdims=True) / width + 1e-05)
     norm_ref[...] = (conv_ref[...].astype(jnp.float32) * scale * gain_ref[...]).astype(jnp.bfloat16)
+    across = jnp.broadcast_to(scale, (columns, columns)).T[:1]
+    for i, rows in enumerate(border_mix(mix_ref, columns, border, odd)):
+        edge_ref[i] = (rows.astype(jnp.float32) * across).astype(jnp.bfloat16)
 
 
 def ring_place(group, groups):
@@ -306,16 +319,32 @@
 STACK = (1, 3, 0, 2)
 
 
+def far_owner(groups):
+    place = ring_place(lax.axis_index("patch") // TEAM, groups)
+    return ring_group((place + groups // 2) % groups, groups)
+
+
+def take_columns(owner, groups, pairs):
+    for g in range(groups):
+
+        @pl.when(owner == g)
+        def _():
+            for source, target in pairs:
+                tall = target.shape[1]
+                target[...] = source[:, g * tall : (g + 1) * tall]
+
+
 def early_body(steps, groups, *refs):
-    norms, grads, chunks = refs[:TEAM], refs[TEAM : 2 * TEAM], refs[2 * TEAM : 2 * TEAM + len(steps)]
-    ups, pre_ref, back_ref, x_last, g_last, xs, gs, downs = refs[2 * TEAM + len(steps) :]
+    norms, grads, chunks = refs[:2], refs[2 : 2 + TEAM], refs[2 + TEAM : 2 + TEAM + len(steps)]
+    ups, pre_ref, back_ref, x_last, g_last, xs, gs, downs = refs[2 + TEAM + len(steps) :]
     columns = norms[0].shape[0]
     span = ups.shape[1]
     me = lax.axis_index("patch")
     group, member = me // TEAM, me % TEAM
     place = ring_place(group, groups)
+    for k in range(2):
+        xs[k * columns : (k + 1) * columns] = norms[k][...]
     for k, m in enumerate(STACK):
-        xs[k * columns : (k + 1) * columns] = norms[m][...]
         gs[k * columns : (k + 1) * columns] = grads[m][...]
     for (shift, first), ref in zip(steps, chunks):
         rows = ref.shape[1] // 2
@@ -325,42 +354,47 @@
             part = slice(half * rows, (half + 1) * rows)
             ups[pl.ds(at, rows)] = ref[0, part]
             downs[pl.ds(at, rows)] = ref[1, part]
-    owner = ring_group((place + groups // 2) % groups, groups)
+    owner = far_owner(groups)
     tall = TEAM * rows
     blank = jnp.zeros((tall, span), jnp.bfloat16)
     at = pl.multiple_of(owner * tall, 16)
     ups[pl.ds(at, tall)] = blank
     downs[pl.ds(at, tall)] = blank
-    for g in range(groups):
-
-        @pl.when(owner == g)
-        def _():
-            x_last[...] = xs[:, g * tall : (g + 1) * tall]
-            g_last[...] = gs[:, g * tall : (g + 1) * tall]
-
+    take_columns(owner, groups, ((xs, x_last), (gs, g_last)))
     pre_ref[...] = mm(xs[...], ups[...])
     back_ref[...] = mm(gs[...], downs[...])
 
 
-def send_body(groups, ups_in, pre_ref, back_ref, x_last, g_last, first_ref, second_ref, ups, gate_ref, send_ref, up, down):
-    me = lax.axis_index("patch")
-    group, member = me // TEAM, me % TEAM
-    owner = ring_group((ring_place(group, groups) + groups // 2) % groups, groups)
-    rows = first_ref.shape[1] // 2
-    for k, ref in ((0, first_ref), (2, second_ref)):
+def rest_body(groups, cross_ref, far_ref, ups, pre_ref, x_last, xs):
+    columns = cross_ref.shape[0]
+    xs[:columns] = cross_ref[...]
+    xs[columns:] = far_ref[...]
+    take_columns(far_owner(groups), groups, ((xs, x_last),))
+    pre_ref[...] = mm(xs[...], ups[...])
+
+
+def send_body(groups, ups_in, pre_a, pre_b, back_ref, xa_last, xb_last, g_last, *refs):
+    parts, (ups, gate_ref, send_ref, up, down) = refs[:4], refs[4:]
+    member = lax.axis_index("patch") % TEAM
+    rows = parts[0].shape[1] // 2
+    for k in range(2):
         for half in range(2):
-            at = pl.multiple_of((member ^ (k + half)) * rows, 16)
+            at = pl.multiple_of((member ^ (2 * k + half)) * rows, 16)
             part = slice(half * rows, (half + 1) * rows)
-            up[pl.ds(at, rows)] = ref[0, part]
-            down[pl.ds(at, rows)] = ref[1, part]
+            up[pl.ds(at, rows)] = parts[2 * k][0, part]
+            down[pl.ds(at, rows)] = parts[2 * k + 1][0, part]
     tall = up.shape[0]
-    ups[pl.ds(pl.multiple_of(owner * tall, 16), tall)] = up[...]
-    pre_act = pre_ref[...] + mm(x_last[...], up[...])
+    ups[pl.ds(pl.multiple_of(far_owner(groups) * tall, 16), tall)] = up[...]
+    columns = send_ref.shape[1]
+    first = pre_a[...] + mm(xa_last[...], up[...])
+    second = pre_b[...] + mm(xb_last[...], up[...])
+    pre_act = jnp.concatenate(
+        [first[:columns], second[:columns], first[columns:], second[columns:]], axis=0
+    )
     back = back_ref[...] + mm(g_last[...], down[...])
     gate = jax.nn.sigmoid(pre_act)
     grad_pre = (back * gate * (1.0 + pre_act * (1.0 - gate))).astype(jnp.bfloat16)
     gate_ref[...] = grad_pre
-    columns = send_ref.shape[1]
     rows = mm(grad_pre[: 2 * columns], ups[...], ((1,), (1,))).astype(jnp.bfloat16)
     send_ref[0] = rows[:columns]
     send_ref[1] = rows[columns:]
@@ -387,27 +421,50 @@
     out_ref[...] = (cross_ref[...] + part_ref[1].astype(jnp.float32)).astype(jnp.bfloat16)
 
 
-def grad_body(mine_ref, part_ref, cross_ref, conv_ref, cot_ref, gain_ref, mix_ref, form_ref, grad_ref, inner_ref, outer_ref):
-    columns, width = conv_ref.shape
+def column_grad(grad_normed, values, scale, gain):
+    scaled = gain * grad_normed
+    mixed = jnp.sum(scaled * values, axis=1, keepdims=True) / values.shape[1]
+    return scale * scaled - values * (scale * scale * scale * mixed)
+
+
+def scale_of(values):
+    return lax.rsqrt(jnp.sum(values * values, axis=1, keepdims=True) / values.shape[1] + 1e-05)
+
+
+def edge_body(
+    mine_ref, cross_ref, part_ref, conv_ref, cot_ref, far_ref, gain_ref, mix_ref, edge_ref, form_ref, own_ref, other_ref
+):
+    columns, _ = conv_ref.shape
+    border = own_ref.shape[0]
+    odd = lax.axis_index("patch") % 2
+    values = conv_ref[...].astype(jnp.float32)
+    share = mine_ref[...] + part_ref[0].astype(jnp.float32)
+    grads = column_grad(share, values, scale_of(values), gain_ref[...])
+    grads = (cot_ref[...].astype(jnp.float32) + grads).astype(jnp.bfloat16)
+    outer = border_mix(mix_ref, columns, border, odd)
+    scaled_values = far_ref[...].astype(jnp.float32) / gain_ref[...]
+    share = cross_ref[...] + part_ref[1].astype(jnp.float32)
+    others = column_grad(share, scaled_values, 1.0, gain_ref[...]).astype(jnp.bfloat16)
+    edge = [edge_ref[i] for i in range(2)]
+    for ref, mix, source in ((own_ref, outer, grads), (other_ref, edge, others)):
+        for b, rows in enumerate(shifted_back(mix, form_ref[0], source)):
+            ref[:, b * BLOCK : (b + 1) * BLOCK] = rows.astype(jnp.bfloat16)
+
+
+def grad_body(
+    mine_ref, part_ref, cross_ref, conv_ref, cot_ref, gain_ref, mix_ref, form_ref, grad_ref, inner_ref
+):
+    columns, _ = conv_ref.shape
     border = inner_ref.shape[0]
-    even = is_even()
+    odd = lax.axis_index("patch") % 2
     grad_normed = mine_ref[...] + part_ref[0].astype(jnp.float32) + cross_ref[...].astype(jnp.float32)
     values = conv_ref[...].astype(jnp.float32)
-    scaled = gain_ref[...] * grad_normed
-    scale = lax.rsqrt(jnp.sum(values * values, axis=1, keepdims=True) / width + 1e-05)
-    mixed = jnp.sum(scaled * values, axis=1, keepdims=True) / width
-    grads = cot_ref[...].astype(jnp.float32) + (
-        scale * scaled - values * (scale * scale * scale * mixed)
-    )
-    grads = grads.astype(jnp.bfloat16)
+    grads = column_grad(grad_normed, values, scale_of(values), gain_ref[...])
+    grads = (cot_ref[...].astype(jnp.float32) + grads).astype(jnp.bfloat16)
     grad_ref[...] = grads
-    outer = [mix_ref[i, columns:] for i in range(2)]
-    for b, rows in enumerate(shifted_back(outer, form_ref[0], grads)):
-        at = slice(b * BLOCK, (b + 1) * BLOCK)
-        rows = rows.astype(jnp.bfloat16)
-        prev, later = rows[:border], rows[border : 2 * border]
-        inner_ref[:, at] = jnp.where(even, later, prev)
-        outer_ref[:, at] = jnp.where(even, prev, later)
+    inner = border_mix(mix_ref, columns, border, 1 - odd)
+    for b, rows in enumerate(shifted_back(inner, form_ref[0], grads)):
+        inner_ref[:, b * BLOCK : (b + 1) * BLOCK] = rows.astype(jnp.bfloat16)
 
 
 def own_body(grad_ref, mix_ref, form_ref, local_ref):
@@ -420,13 +477,14 @@
         local_ref[:, at] = own.astype(jnp.float32) + (mm(own, form_ref[1], ((1,), (1,))) + rows)
 
 
-def last_body(local_ref, inner_ref, outer_ref, bound_ref, out_ref):
+def last_body(local_ref, inner_ref, outer_ref, other_ref, bound_ref, out_ref):
     border = inner_ref.shape[0]
     chosen = picked(bound_ref, local_ref.shape[0]).astype(jnp.float32)
     low, high = chosen[:, :border], chosen[:, border:]
     inner = jnp.where(is_even(), high, low).astype(jnp.bfloat16)
     outer = jnp.where(is_even(), low, high).astype(jnp.bfloat16)
-    total = local_ref[...] + mm(inner, inner_ref[...]) + mm(outer, outer_ref[...])
+    total = local_ref[...] + mm(inner, inner_ref[...])
+    total = total + (mm(outer, outer_ref[...]) + mm(outer, other_ref[...]))
     out_ref[...] = total.astype(jnp.bfloat16)
 
 
@@ -491,8 +549,9 @@
     def swap(value, bits):
         return permute(value, [(i, i ^ bits) for i in range(devices)])
 
-    def outer(value):
-        return permute(value, [(i, (i - 1 + 2 * (i % 2)) % devices) for i in range(devices)])
+    def outer(value, bits=0):
+        pairs = [(i ^ bits, (i - 1 + 2 * (i % 2)) % devices) for i in range(devices)]
+        return permute(value, pairs)
 
     order = list(range(0, groups, 2)) + list(range(groups - 1, 0, -2))
 
@@ -517,14 +576,20 @@
         self_imag,
         norm_gain.reshape(-1, 128),
     ]
-    loaded = call(
+    x, cot, boundary, *tables = call(
         lambda *refs: load_body(len(held), *refs),
-        [struct((2, rows, span))] * TEAM + [struct(value.shape, value.dtype) for value in held],
-        [up_weight, down_weight, *held],
-        [pltpu.SemaphoreType.DMA((2 * TEAM + len(held),))],
-        range(2 + len(held)),
-    )
-    parts, (x, cot, boundary, *tables) = loaded[:TEAM], loaded[TEAM:]
+        [struct(value.shape, value.dtype) for value in held],
+        held,
+        [pltpu.SemaphoreType.DMA((len(held),))],
+        range(len(held)),
+    )
+    parts = call(
+        weights_body,
+        [struct((2, rows, span))] * TEAM,
+        [up_weight, down_weight],
+        [pltpu.SemaphoreType.DMA((2 * TEAM,))],
+        (0, 1),
+    )
     near_part = swap(parts[1], 1)
     far_parts = [swap(parts[2], 2), swap(parts[3], 3)]
     first = jnp.concatenate([parts[0], near_part], axis=1)
@@ -533,16 +598,15 @@
     forth = [first, second]
     back = [first, second]
     half = groups // 2
-    for s in range(1, half + 1):
+    for s in range(1, half):
         for which in range(2):
-            if s < half or which == 0:
-                forth[which] = around(forth[which], 1)
-                steps.append((-s, 2 * which))
-                chunks.append(forth[which])
-            if s < half or which == 1:
-                back[which] = around(back[which], -1)
-                steps.append((s, 2 * which))
-                chunks.append(back[which])
+            forth[which] = around(forth[which], 1)
+            back[which] = around(back[which], -1)
+            steps += [(-s, 2 * which), (s, 2 * which)]
+            chunks += [forth[which], back[which]]
+    last_chunks = []
+    for which in range(2):
+        last_chunks += [around(forth[which][:1], 1), around(back[which][1:], -1)]
 
     inner_rows, outer_rows = call(border_body, [struct((border, width))] * 2, [x, boundary])
     inner_rows = swap(inner_rows, 1)
@@ -560,36 +624,47 @@
         ],
         tables,
     )
-    conv, norm = call(
+    conv, norm, edge = call(
         conv_body,
-        [struct((columns, width))] * 2,
+        [struct((columns, width))] * 2 + [struct((2, border, columns))],
         [x, inner_rows, outer_rows, mix, form, gain],
         [pltpu.VMEM((extent, width), jnp.bfloat16)],
     )
     norm_near = swap(norm, 1)
     norm_far = swap(norm, 2)
     norm_cross = swap(norm_far, 1)
+    edge = swap(edge, 2)
 
     wide = struct((columns, width), jnp.float32)
     team = TEAM * columns
-    late = len(steps) - 2
-    ups, pre, back_sum, x_last, g_last = call(
-        lambda *refs: early_body(steps[:late], groups, *refs),
-        [struct((width, span))]
-        + [struct((team, span), jnp.float32)] * 2
-        + [struct((team, TEAM * rows))] * 2,
-        [norm, norm_near, norm_far, norm_cross, cot, cot_near, cot_far, cot_cross, *chunks[:late]],
+    tall = TEAM * rows
+    ups, pre_a, back_sum, xa_last, g_last = call(
+        lambda *refs: early_body(steps, groups, *refs),
         [
-            pltpu.VMEM((team, width), jnp.bfloat16),
+            struct((width, span)),
+            struct((team // 2, span), jnp.float32),
+            struct((team, span), jnp.float32),
+            struct((team // 2, tall)),
+            struct((team, tall)),
+        ],
+        [norm_near, norm, cot, cot_near, cot_far, cot_cross, *chunks],
+        [
+            pltpu.VMEM((team // 2, width), jnp.bfloat16),
             pltpu.VMEM((team, width), jnp.bfloat16),
             pltpu.VMEM((width, span), jnp.bfloat16),
         ],
     )
+    pre_b, xb_last = call(
+        lambda *refs: rest_body(groups, *refs),
+        [struct((team // 2, span), jnp.float32), struct((team // 2, tall))],
+        [norm_cross, norm_far, ups],
+        [pltpu.VMEM((team // 2, width), jnp.bfloat16)],
+    )
     ups, gate, send = call(
         lambda *refs: send_body(groups, *refs),
         [struct((width, span)), struct((team, span)), struct((2, columns, width))],
-        [ups, pre, back_sum, x_last, g_last, *chunks[late:]],
-        [pltpu.VMEM((TEAM * rows, span), jnp.bfloat16)] * 2,
+        [ups, pre_a, pre_b, back_sum, xa_last, xb_last, g_last, *last_chunks],
+        [pltpu.VMEM((tall, span), jnp.bfloat16)] * 2,
         (),
         ((0, 0),),
     )
@@ -597,17 +672,23 @@
     received = swap(send, 1)
     crossing = call(join_body, struct((columns, width)), [cross, received])
     crossed = swap(crossing, 2)
-    grads, inner_back, outer_back = call(
+    own_rows, other_rows = call(
+        edge_body,
+        [struct((border, width))] * 2,
+        [mine, cross, received, conv, cot, norm_far, gain, mix, edge, form],
+    )
+    own_rows = outer(own_rows)
+    other_rows = outer(other_rows, 2)
+    grads, inner_back = call(
         grad_body,
-        [struct((columns, width)), struct((border, width)), struct((border, width))],
+        [struct((columns, width)), struct((border, width))],
         [mine, received, crossed, conv, cot, gain, mix, form],
     )
     inner_back = swap(inner_back, 1)
-    outer_back = outer(outer_back)
     local = call(own_body, wide, [grads, mix, form])
     out = pl.pallas_call(
         last_body, out_shape=jax.ShapeDtypeStruct((columns, width), jnp.bfloat16)
-    )(*(pltpu.with_memory_space_constraint(v, pltpu.VMEM) for v in (local, inner_back, outer_back, boundary)))
+    )(*(pltpu.with_memory_space_constraint(v, pltpu.VMEM) for v in (local, inner_back, own_rows, other_rows, boundary)))
     return out[None]
 
 

time: 84.6 us -> 90.6 us (1.071)
  starting transfers between devices: 28.4 us -> 37.7 us
  waiting for transfers between devices: 44.8 us -> 39.1 us
  Pallas kernels: 11.1 us -> 13.4 us
    ppermute x29 -> x33, starting transfers between devices: 28.4 us -> 37.7 us  [permute(): return lax.ppermute(value, 'patch', pairs)]
    ppermute x29 -> x33, waiting for transfers between devices: 44.8 us -> 39.1 us  [permute(): return lax.ppermute(value, 'patch', pairs)]
    pallas_call x10 -> x13, Pallas kernels: 9.89 us -> 12 us  [call(): pl.pallas_call(body, out_shape=outs, in_specs=specs, out_specs=jax.tree.m...]
  transfers between devices with their start and end apart: 29 -> 33, of which waited for: 15 -> 17; matrix products, arithmetic and copies ran while one was open for 0% -> 0% of each run, Pallas kernels for 7% -> 11%
where the time goes in v2:
time: 90.6 us; the launch traced here: 90.4 us
  waiting for transfers between devices  39.1 us (43%)
  starting transfers between devices  37.7 us (42%)
  Pallas kernels  13.4 us (15%)
    ppermute x33, waiting for transfers between devices, permute(): return lax.ppermute(value, 'patch', pairs)  39.1 us
    ppermute x33, starting transfers between devices, permute(): return lax.ppermute(value, 'patch', pairs)  37.7 us
    pallas_call x13, Pallas kernels, call(): pl.pallas_call(body, out_shape=outs, in_specs=specs, out_specs=jax.tree.m...  12 us
  transfers between devices with their start and end apart: 33, of which 17 were waited for; matrix products, arithmetic and copies ran while one was open for 0% of the time, Pallas kernels for 11%

profile of v2, /device:TPU:0, one launch (start us, length us, event | category | flops | bytes accessed | tf_op | source)
XLA Modules:
  0.0 90.4 jit_solution(2311179667022728859)
XLA Ops:
  0.0 1.2 %shard_map.127 = (bf16[128,1536]{1,0:T(8,128)(2,1)S(1)}, bf16[128,1536]{1,0:T(8,128)(2,1)S(1)}, s32[1,64]{1,0:T(1,128)S(1)}, s32[6,128]{1,0:T(8,128)S(1)}, s32[6...) custom-call(bf16[128,1536]{1,0:T(8,128)(2,1)} %bitcast.7, ...), custom_call_target="tpu_custom_call" | custom-call | tf_op jit(solution)/shard_map/pallas_call | solution.py:174
  2.0 6.6 %collective-permute-start.1 = (bf16[32,1536]{1,0:T(8,128)(2,1)S(1)}, bf16[32,1536]{1,0:T(8,128)(2,1)S(1)}, u32[]{:S(2)}, u32[]{:S(2)}) collective-permute-start(bf16[32,1536]{1,0:T(8,128)(2,1)S(1)} %get-tuple-element.47), channel_id=1, source_target_pairs={{0,31},{1,2},{2,1},{3,4},{4,3},{5,6},{6,5},{7,8},{8,7},{9,10},{10,... | collective-permute-start | bytes 294920 | tf_op jit(solution)/shard_map/ppermute | solution.py:547
  9.7 2.1 %collective-permute-start.7 = (bf16[2,48,512]{2,1,0:T(8,128)(2,1)S(1)}, bf16[2,48,512]{2,1,0:T(8,128)(2,1)S(1)}, u32[]{:S(2)}, u32[]{:S(2)}) collective-permute-start(bf16[2,48,512]{2,1,0:T(8,128)(2,1)S(1)} %get-tuple-element.63), channel_id=1, source_target_pairs={{0,2},{1,3},{2,0},{3,1},{4,6},{5,7},{6,4},{7,5},{8,10},{9,11},{10,... | collective-permute-start | bytes 294920 | tf_op jit(solution)/shard_map/ppermute | solution.py:547
  11.8 8.1 %collective-permute-done.7 = bf16[2,48,512]{2,1,0:T(8,128)(2,1)S(1)} collective-permute-done((bf16[2,48,512]{2,1,0:T(8,128)(2,1)S(1)}, bf16[2,48,512]{2,1,0:T(8,128)(2,1)S(1)}, u32[]{:S(2)}, u32[]{:S(2)}) %collective-permute-start.7) | collective-permute-done | bytes 98336 | tf_op jit(solution)/shard_map/ppermute | solution.py:547
  20.0 2.8 %collective-permute-start.11 = (bf16[2,96,512]{2,1,0:T(8,128)(2,1)S(1)}, bf16[2,96,512]{2,1,0:T(8,128)(2,1)S(1)}, u32[]{:S(2)}, u32[]{:S(2)}) collective-permute-start(bf16[2,96,512]{2,1,0:T(8,128)(2,1)S(1)} %constant_dynamic-update-slice_fusion.2.refs_7_), channel_id=1, source_target_pairs={{0,8},{1,9},{2,10},{3,11},{8,16},{9,17},{10,18},{11,19},{16,24},{1... | collective-permute-start | bytes 589832 | tf_op jit(solution)/shard_map/ppermute | solution.py:547
  22.9 2.1 %collective-permute-start.9 = (bf16[2,96,512]{2,1,0:T(8,128)(2,1)S(1)}, bf16[2,96,512]{2,1,0:T(8,128)(2,1)S(1)}, u32[]{:S(2)}, u32[]{:S(2)}) collective-permute-start(bf16[2,96,512]{2,1,0:T(8,128)(2,1)S(1)} %constant_dynamic-update-slice_fusion.refs_6_), channel_id=1, source_target_pairs={{0,8},{1,9},{2,10},{3,11},{8,16},{9,17},{10,18},{11,19},{16,24},{1... | collective-permute-start | bytes 589832 | tf_op jit(solution)/shard_map/ppermute | solution.py:547
  26.7 1.6 %collective-permute-done.11.refs_10_ = bf16[2,96,512]{2,1,0:T(8,128)(2,1)S(1)} collective-permute-done((bf16[2,96,512]{2,1,0:T(8,128)(2,1)S(1)}, bf16[2,96,512]{2,1,0:T(8,128)(2,1)S(1)}, u32[]{:S(2)}, u32[]{:S(2)}) %collective-permute-start.11) | collective-permute-done | bytes 196640 | tf_op jit(solution)/shard_map/ppermute | solution.py:547
  29.3 1.3 %collective-permute-done.12.refs_11_ = bf16[2,96,512]{2,1,0:T(8,128)(2,1)S(1)} collective-permute-done((bf16[2,96,512]{2,1,0:T(8,128)(2,1)S(1)}, bf16[2,96,512]{2,1,0:T(8,128)(2,1)S(1)}, u32[]{:S(2)}, u32[]{:S(2)}) %collective-permute-start.12) | collective-permute-done | bytes 196640 | tf_op jit(solution)/shard_map/ppermute | solution.py:547
  30.6 1.6 %collective-permute-start.15 = (bf16[2,96,512]{2,1,0:T(8,128)(2,1)S(1)}, bf16[2,96,512]{2,1,0:T(8,128)(2,1)S(1)}, u32[]{:S(2)}, u32[]{:S(2)}) collective-permute-start(bf16[2,96,512]{2,1,0:T(8,128)(2,1)S(1)} %collective-permute-done.11.refs_10_), channel_id=1, source_target_pairs={{0,8},{1,9},{2,10},{3,11},{8,16},{9,17},{10,18},{11,19},{16,24},{1... | collective-permute-start | bytes 589832 | tf_op jit(solution)/shard_map/ppermute | solution.py:547
  32.5 2.0 %collective-permute-start.16 = (bf16[2,96,512]{2,1,0:T(8,128)(2,1)S(1)}, bf16[2,96,512]{2,1,0:T(8,128)(2,1)S(1)}, u32[]{:S(2)}, u32[]{:S(2)}) collective-permute-start(bf16[2,96,512]{2,1,0:T(8,128)(2,1)S(1)} %collective-permute-done.12.refs_11_), channel_id=1, source_target_pairs={{0,4},{1,5},{2,6},{3,7},{8,0},{9,1},{10,2},{11,3},{16,8},{17,9},{1... | collective-permute-start | bytes 589832 | tf_op jit(solution)/shard_map/ppermute | solution.py:547
  35.3 1.3 %collective-permute-start.14 = (bf16[2,96,512]{2,1,0:T(8,128)(2,1)S(1)}, bf16[2,96,512]{2,1,0:T(8,128)(2,1)S(1)}, u32[]{:S(2)}, u32[]{:S(2)}) collective-permute-start(bf16[2,96,512]{2,1,0:T(8,128)(2,1)S(1)} %collective-permute-done.10.refs_9_), channel_id=1, source_target_pairs={{0,4},{1,5},{2,6},{3,7},{8,0},{9,1},{10,2},{11,3},{16,8},{17,9},{1... | collective-permute-start | bytes 589832 | tf_op jit(solution)/shard_map/ppermute | solution.py:547
  37.1 2.5 %collective-permute-start.19 = (bf16[2,96,512]{2,1,0:T(8,128)(2,1)S(1)}, bf16[2,96,512]{2,1,0:T(8,128)(2,1)S(1)}, u32[]{:S(2)}, u32[]{:S(2)}) collective-permute-start(bf16[2,96,512]{2,1,0:T(8,128)(2,1)S(1)} %collective-permute-done.15.refs_14_), channel_id=1, source_target_pairs={{0,8},{1,9},{2,10},{3,11},{8,16},{9,17},{10,18},{11,19},{16,24},{1... | collective-permute-start | bytes 589832 | tf_op jit(solution)/shard_map/ppermute | solution.py:547
  39.5 1.0 %collective-permute-done.16.refs_15_ = bf16[2,96,512]{2,1,0:T(8,128)(2,1)S(1)} collective-permute-done((bf16[2,96,512]{2,1,0:T(8,128)(2,1)S(1)}, bf16[2,96,512]{2,1,0:T(8,128)(2,1)S(1)}, u32[]{:S(2)}, u32[]{:S(2)}) %collective-permute-start.16) | collective-permute-done | bytes 196640 | tf_op jit(solution)/shard_map/ppermute | solution.py:547
  40.6 1.7 %collective-permute-start.20 = (bf16[2,96,512]{2,1,0:T(8,128)(2,1)S(1)}, bf16[2,96,512]{2,1,0:T(8,128)(2,1)S(1)}, u32[]{:S(2)}, u32[]{:S(2)}) collective-permute-start(bf16[2,96,512]{2,1,0:T(8,128)(2,1)S(1)} %collective-permute-done.16.refs_15_), channel_id=1, source_target_pairs={{0,4},{1,5},{2,6},{3,7},{8,0},{9,1},{10,2},{11,3},{16,8},{17,9},{1... | collective-permute-start | bytes 589832 | tf_op jit(solution)/shard_map/ppermute | solution.py:547
  42.3 1.4 %collective-permute-start.17 = (bf16[2,96,512]{2,1,0:T(8,128)(2,1)S(1)}, bf16[2,96,512]{2,1,0:T(8,128)(2,1)S(1)}, u32[]{:S(2)}, u32[]{:S(2)}) collective-permute-start(bf16[2,96,512]{2,1,0:T(8,128)(2,1)S(1)} %collective-permute-done.13.refs_12_), channel_id=1, source_target_pairs={{0,8},{1,9},{2,10},{3,11},{8,16},{9,17},{10,18},{11,19},{16,24},{1... | collective-permute-start | bytes 589832 | tf_op jit(solution)/shard_map/ppermute | solution.py:547
  45.3 1.2 %collective-permute-done.19.refs_18_ = bf16[2,96,512]{2,1,0:T(8,128)(2,1)S(1)} collective-permute-done((bf16[2,96,512]{2,1,0:T(8,128)(2,1)S(1)}, bf16[2,96,512]{2,1,0:T(8,128)(2,1)S(1)}, u32[]{:S(2)}, u32[]{:S(2)}) %collective-permute-start.19) | collective-permute-done | bytes 196640 | tf_op jit(solution)/shard_map/ppermute | solution.py:547
  47.1 1.9 %collective-permute-done.17.refs_16_ = bf16[2,96,512]{2,1,0:T(8,128)(2,1)S(1)} collective-permute-done((bf16[2,96,512]{2,1,0:T(8,128)(2,1)S(1)}, bf16[2,96,512]{2,1,0:T(8,128)(2,1)S(1)}, u32[]{:S(2)}, u32[]{:S(2)}) %collective-permute-start.17) | collective-permute-done | bytes 196640 | tf_op jit(solution)/shard_map/ppermute | solution.py:547
  49.0 1.7 %collective-permute-start.18 = (bf16[2,96,512]{2,1,0:T(8,128)(2,1)S(1)}, bf16[2,96,512]{2,1,0:T(8,128)(2,1)S(1)}, u32[]{:S(2)}, u32[]{:S(2)}) collective-permute-start(bf16[2,96,512]{2,1,0:T(8,128)(2,1)S(1)} %collective-permute-done.14.refs_13_), channel_id=1, source_target_pairs={{0,4},{1,5},{2,6},{3,7},{8,0},{9,1},{10,2},{11,3},{16,8},{17,9},{1... | collective-permute-start | bytes 589832 | tf_op jit(solution)/shard_map/ppermute | solution.py:547
  50.8 3.9 %collective-permute-done.18.refs_17_ = bf16[2,96,512]{2,1,0:T(8,128)(2,1)S(1)} collective-permute-done((bf16[2,96,512]{2,1,0:T(8,128)(2,1)S(1)}, bf16[2,96,512]{2,1,0:T(8,128)(2,1)S(1)}, u32[]{:S(2)}, u32[]{:S(2)}) %collective-permute-start.18) | collective-permute-done | bytes 196640 | tf_op jit(solution)/shard_map/ppermute | solution.py:547
  54.7 1.8 %collective-permute-start.25 = (bf16[1,96,512]{2,1,0:T(8,128)(2,1)S(1)}, bf16[1,96,512]{2,1,0:T(8,128)(2,1)S(1)}, u32[]{:S(2)}, u32[]{:S(2)}) collective-permute-start(bf16[1,96,512]{2,1,0:T(8,128)(2,1)S(1)} %slice.18), channel_id=1, source_target_pairs={{0,8},{1,9},{2,10},{3,11},{8,16},{9,17},{10,18},{11,19},{16,24},{1... | collective-permute-start | bytes 294920 | tf_op jit(solution)/shard_map/ppermute | solution.py:547
  56.8 1.8 %collective-permute-start.23 = (bf16[1,96,512]{2,1,0:T(8,128)(2,1)S(1)}, bf16[1,96,512]{2,1,0:T(8,128)(2,1)S(1)}, u32[]{:S(2)}, u32[]{:S(2)}) collective-permute-start(bf16[1,96,512]{2,1,0:T(8,128)(2,1)S(1)} %slice.16), channel_id=1, source_target_pairs={{0,8},{1,9},{2,10},{3,11},{8,16},{9,17},{10,18},{11,19},{16,24},{1... | collective-permute-start | bytes 294920 | tf_op jit(solution)/shard_map/ppermute | solution.py:547
  58.8 1.9 %shard_map.132 = (bf16[1536,512]{1,0:T(8,128)(2,1)S(1)}, f32[256,512]{1,0:T(8,128)S(1)}, f32[512,512]{1,0:T(8,128)S(1)}, bf16[256,192]{1,0:T(8,128)(2,1)S(1)}, bf16[512,192]{1,0:T(8,128)(2,1)S(1)}) custom-call(bf16[128,1536]{1,0:T(8,128)(2,1)S(1)} %collective-permute-done.2.refs_0_, bf16[128,1536]{1,0:T(8,128)(2,1)S(1)} %get-tuple-element.59.refs_1_, ...), custom_call_target="tpu_custom_call" | custom-call | tf_op jit(solution)/shard_map/pallas_call | solution.py:174
  61.6 1.7 %collective-permute-done.24.refs_8_ = bf16[1,96,512]{2,1,0:T(8,128)(2,1)S(1)} collective-permute-done((bf16[1,96,512]{2,1,0:T(8,128)(2,1)S(1)}, bf16[1,96,512]{2,1,0:T(8,128)(2,1)S(1)}, u32[]{:S(2)}, u32[]{:S(2)}) %collective-permute-start.24) | collective-permute-done | bytes 98336 | tf_op jit(solution)/shard_map/ppermute | solution.py:547
  64.9 1.7 %collective-permute-done.27.part_ref = bf16[2,128,1536]{2,1,0:T(8,128)(2,1)S(1)} collective-permute-done((bf16[2,128,1536]{2,1,0:T(8,128)(2,1)S(1)}, bf16[2,128,1536]{2,1,0:T(8,128)(2,1)S(1)}, u32[]{:S(2)}, u32[]{:S(2)}) %collective-permute-start.27) | collective-permute-done | bytes 786464 | tf_op jit(solution)/shard_map/ppermute | solution.py:547
  66.7 1.1 %collective-permute-start.28 = (bf16[128,1536]{1,0:T(8,128)(2,1)S(1)}, bf16[128,1536]{1,0:T(8,128)(2,1)S(1)}, u32[]{:S(2)}, u32[]{:S(2)}) collective-permute-start(bf16[128,1536]{1,0:T(8,128)(2,1)S(1)} %shard_map.136), channel_id=1, source_target_pairs={{0,2},{1,3},{2,0},{3,1},{4,6},{5,7},{6,4},{7,5},{8,10},{9,11},{10,... | collective-permute-start | bytes 1179656 | tf_op jit(solution)/shard_map/ppermute | solution.py:547
  68.8 9.5 %collective-permute-done.30.edge_ref = bf16[2,32,128]{2,1,0:T(8,128)(2,1)S(1)} collective-permute-done((bf16[2,32,128]{2,1,0:T(8,128)(2,1)S(1)}, bf16[2,32,128]{2,1,0:T(8,128)(2,1)S(1)}, u32[]{:S(2)}, u32[]{:S(2)}) %collective-permute-start.30) | collective-permute-done | bytes 16416 | tf_op jit(solution)/shard_map/ppermute | solution.py:547
  78.3 1.5 %shard_map.139 = (bf16[32,1536]{1,0:T(8,128)(2,1)S(1)}, bf16[32,1536]{1,0:T(8,128)(2,1)S(1)}) custom-call(f32[128,1536]{1,0:T(8,128)S(1)} %get-tuple-element.74.mine_ref, f32[128,1536]{1,0:T(8,128)S(1)} %get-tuple-element.76.cross_ref, bf16[2,128,1536]{2,1,0:T(8,128)(2,1)S(1)} %collective-permute-done.27.part_ref, ...), custom_call_target="tpu_custom_call" | custom-call | tf_op jit(solution)/shard_map/pallas_call | solution.py:174
  79.7 2.6 %collective-permute-start.31 = (bf16[32,1536]{1,0:T(8,128)(2,1)S(1)}, bf16[32,1536]{1,0:T(8,128)(2,1)S(1)}, u32[]{:S(2)}, u32[]{:S(2)}) collective-permute-start(bf16[32,1536]{1,0:T(8,128)(2,1)S(1)} %get-tuple-element.81), channel_id=1, source_target_pairs={{0,31},{1,2},{2,1},{3,4},{4,3},{5,6},{6,5},{7,8},{8,7},{9,10},{10,... | collective-permute-start | bytes 294920 | tf_op jit(solution)/shard_map/ppermute | solution.py:547
  83.4 1.1 %shard_map.138.local_ref = f32[128,1536]{1,0:T(8,128)S(1)} custom-call(bf16[128,1536]{1,0:T(8,128)(2,1)S(1)} %get-tuple-element.78.grad_ref, bf16[2,256,128]{2,1,0:T(8,128)(2,1)S(1)} %get-tuple-element.56.mix_ref, bf16[2,256,256]{2,1,0:T(8,128)(2,1)S(1)} %get-tuple-element.57.form_ref), custom_call_target="tpu_custom_call" | custom-call | tf_op jit(solution)/shard_map/pallas_call | solution.py:174
  84.5 2.9 %collective-permute-done.31.outer_ref = bf16[32,1536]{1,0:T(8,128)(2,1)S(1)} collective-permute-done((bf16[32,1536]{1,0:T(8,128)(2,1)S(1)}, bf16[32,1536]{1,0:T(8,128)(2,1)S(1)}, u32[]{:S(2)}, u32[]{:S(2)}) %collective-permute-start.31) | collective-permute-done | bytes 98336 | tf_op jit(solution)/shard_map/ppermute | solution.py:547
  87.4 1.7 %collective-permute-done.32.other_ref = bf16[32,1536]{1,0:T(8,128)(2,1)S(1)} collective-permute-done((bf16[32,1536]{1,0:T(8,128)(2,1)S(1)}, bf16[32,1536]{1,0:T(8,128)(2,1)S(1)}, u32[]{:S(2)}, u32[]{:S(2)}) %collective-permute-start.32) | collective-permute-done | bytes 98336 | tf_op jit(solution)/shard_map/ppermute | solution.py:547
  89.1 1.3 %shard_map.140 = bf16[128,1536]{1,0:T(8,128)(2,1)} custom-call(f32[128,1536]{1,0:T(8,128)S(1)} %shard_map.138.local_ref, bf16[32,1536]{1,0:T(8,128)(2,1)S(1)} %collective-permute-done.29.inner_ref, bf16[32,1536]{1,0:T(8,128)(2,1)S(1)} %collective-permute-done.31.outer_ref, bf16[32,1536]{1,0:T(8,128)(2,1)S(1)} %collective-permute-done.32.other_ref, ...), custom_call_target="tpu_custom_call" | custom-call | tf_op jit(solution)/shard_map/pallas_call | solution.py:689
  (56 shorter events, 13.4 us)
Async XLA Ops:
  1.5 21.4 %collective-permute-start = (bf16[32,1536]{1,0:T(8,128)(2,1)S(1)}, bf16[32,1536]{1,0:T(8,128)(2,1)S(1)}, u32[]{:S(2)}, u32[]{:S(2)}) collective-permute-start(bf16[32,1536]{1,0:T(8,128)(2,1)S(1)} %get-tuple-element.46), channel_id=1, source_target_pairs={{0,1},{1,0},{2,3},{3,2},{4,5},{5,4},{6,7},{7,6},{8,9},{9,8},{10,11... | collective-permute-start | bytes 294920 | tf_op jit(solution)/shard_map/ppermute | solution.py:547
  2.0 23.6 %collective-permute-start.1 = (bf16[32,1536]{1,0:T(8,128)(2,1)S(1)}, bf16[32,1536]{1,0:T(8,128)(2,1)S(1)}, u32[]{:S(2)}, u32[]{:S(2)}) collective-permute-start(bf16[32,1536]{1,0:T(8,128)(2,1)S(1)} %get-tuple-element.47), channel_id=1, source_target_pairs={{0,31},{1,2},{2,1},{3,4},{4,3},{5,6},{6,5},{7,8},{8,7},{9,10},{10,... | collective-permute-start | bytes 294920 | tf_op jit(solution)/shard_map/ppermute | solution.py:547
  8.6 26.7 %collective-permute-start.4 = (bf16[128,1536]{1,0:T(8,128)(2,1)S(1)}, bf16[128,1536]{1,0:T(8,128)(2,1)S(1)}, u32[]{:S(2)}, u32[]{:S(2)}) collective-permute-start(bf16[128,1536]{1,0:T(8,128)(2,1)S(1)} %get-tuple-element.60.refs_2_.cot_ref), channel_id=1, source_target_pairs={{0,2},{1,3},{2,0},{3,1},{4,6},{5,7},{6,4},{7,5},{8,10},{9,11},{10,... | collective-permute-start | bytes 1179656 | tf_op jit(solution)/shard_map/ppermute | solution.py:547
  9.7 10.2 %collective-permute-start.7 = (bf16[2,48,512]{2,1,0:T(8,128)(2,1)S(1)}, bf16[2,48,512]{2,1,0:T(8,128)(2,1)S(1)}, u32[]{:S(2)}, u32[]{:S(2)}) collective-permute-start(bf16[2,48,512]{2,1,0:T(8,128)(2,1)S(1)} %get-tuple-element.63), channel_id=1, source_target_pairs={{0,2},{1,3},{2,0},{3,1},{4,6},{5,7},{6,4},{7,5},{8,10},{9,11},{10,... | collective-permute-start | bytes 294920 | tf_op jit(solution)/shard_map/ppermute | solution.py:547
  11.8 8.2 %collective-permute-start.8 = (bf16[2,48,512]{2,1,0:T(8,128)(2,1)S(1)}, bf16[2,48,512]{2,1,0:T(8,128)(2,1)S(1)}, u32[]{:S(2)}, u32[]{:S(2)}) collective-permute-start(bf16[2,48,512]{2,1,0:T(8,128)(2,1)S(1)} %get-tuple-element.64), channel_id=1, source_target_pairs={{0,3},{1,2},{2,1},{3,0},{4,7},{5,6},{6,5},{7,4},{8,11},{9,10},{10,... | collective-permute-start | bytes 294920 | tf_op jit(solution)/shard_map/ppermute | solution.py:547
  19.8 3.0 %collective-permute-start.6 = (bf16[2,48,512]{2,1,0:T(8,128)(2,1)S(1)}, bf16[2,48,512]{2,1,0:T(8,128)(2,1)S(1)}, u32[]{:S(2)}, u32[]{:S(2)}) collective-permute-start(bf16[2,48,512]{2,1,0:T(8,128)(2,1)S(1)} %get-tuple-element.62), channel_id=1, source_target_pairs={{0,1},{1,0},{2,3},{3,2},{4,5},{5,4},{6,7},{7,6},{8,9},{9,8},{10,11... | collective-permute-start | bytes 294920 | tf_op jit(solution)/shard_map/ppermute | solution.py:547
  20.0 8.3 %collective-permute-start.11 = (bf16[2,96,512]{2,1,0:T(8,128)(2,1)S(1)}, bf16[2,96,512]{2,1,0:T(8,128)(2,1)S(1)}, u32[]{:S(2)}, u32[]{:S(2)}) collective-permute-start(bf16[2,96,512]{2,1,0:T(8,128)(2,1)S(1)} %constant_dynamic-update-slice_fusion.2.refs_7_), channel_id=1, source_target_pairs={{0,8},{1,9},{2,10},{3,11},{8,16},{9,17},{10,18},{11,19},{16,24},{1... | collective-permute-start | bytes 589832 | tf_op jit(solution)/shard_map/ppermute | solution.py:547
  22.9 7.8 %collective-permute-start.12 = (bf16[2,96,512]{2,1,0:T(8,128)(2,1)S(1)}, bf16[2,96,512]{2,1,0:T(8,128)(2,1)S(1)}, u32[]{:S(2)}, u32[]{:S(2)}) collective-permute-start(bf16[2,96,512]{2,1,0:T(8,128)(2,1)S(1)} %constant_dynamic-update-slice_fusion.2.refs_7_), channel_id=1, source_target_pairs={{0,4},{1,5},{2,6},{3,7},{8,0},{9,1},{10,2},{11,3},{16,8},{17,9},{1... | collective-permute-start | bytes 589832 | tf_op jit(solution)/shard_map/ppermute | solution.py:547
  22.9 9.7 %collective-permute-start.9 = (bf16[2,96,512]{2,1,0:T(8,128)(2,1)S(1)}, bf16[2,96,512]{2,1,0:T(8,128)(2,1)S(1)}, u32[]{:S(2)}, u32[]{:S(2)}) collective-permute-start(bf16[2,96,512]{2,1,0:T(8,128)(2,1)S(1)} %constant_dynamic-update-slice_fusion.refs_6_), channel_id=1, source_target_pairs={{0,8},{1,9},{2,10},{3,11},{8,16},{9,17},{10,18},{11,19},{16,24},{1... | collective-permute-start | bytes 589832 | tf_op jit(solution)/shard_map/ppermute | solution.py:547
  25.6 8.9 %collective-permute-start.10 = (bf16[2,96,512]{2,1,0:T(8,128)(2,1)S(1)}, bf16[2,96,512]{2,1,0:T(8,128)(2,1)S(1)}, u32[]{:S(2)}, u32[]{:S(2)}) collective-permute-start(bf16[2,96,512]{2,1,0:T(8,128)(2,1)S(1)} %constant_dynamic-update-slice_fusion.refs_6_), channel_id=1, source_target_pairs={{0,4},{1,5},{2,6},{3,7},{8,0},{9,1},{10,2},{11,3},{16,8},{17,9},{1... | collective-permute-start | bytes 589832 | tf_op jit(solution)/shard_map/ppermute | solution.py:547
  28.3 16.5 %collective-permute-start.21 = (bf16[128,1536]{1,0:T(8,128)(2,1)S(1)}, bf16[128,1536]{1,0:T(8,128)(2,1)S(1)}, u32[]{:S(2)}, u32[]{:S(2)}) collective-permute-start(bf16[128,1536]{1,0:T(8,128)(2,1)S(1)} %get-tuple-element.59.refs_1_), channel_id=1, source_target_pairs={{0,2},{1,3},{2,0},{3,1},{4,6},{5,7},{6,4},{7,5},{8,10},{9,11},{10,... | collective-permute-start | bytes 1179656 | tf_op jit(solution)/shard_map/ppermute | solution.py:547
  30.6 6.4 %collective-permute-start.15 = (bf16[2,96,512]{2,1,0:T(8,128)(2,1)S(1)}, bf16[2,96,512]{2,1,0:T(8,128)(2,1)S(1)}, u32[]{:S(2)}, u32[]{:S(2)}) collective-permute-start(bf16[2,96,512]{2,1,0:T(8,128)(2,1)S(1)} %collective-permute-done.11.refs_10_), channel_id=1, source_target_pairs={{0,8},{1,9},{2,10},{3,11},{8,16},{9,17},{10,18},{11,19},{16,24},{1... | collective-permute-start | bytes 589832 | tf_op jit(solution)/shard_map/ppermute | solution.py:547
  32.5 8.1 %collective-permute-start.16 = (bf16[2,96,512]{2,1,0:T(8,128)(2,1)S(1)}, bf16[2,96,512]{2,1,0:T(8,128)(2,1)S(1)}, u32[]{:S(2)}, u32[]{:S(2)}) collective-permute-start(bf16[2,96,512]{2,1,0:T(8,128)(2,1)S(1)} %collective-permute-done.12.refs_11_), channel_id=1, source_target_pairs={{0,4},{1,5},{2,6},{3,7},{8,0},{9,1},{10,2},{11,3},{16,8},{17,9},{1... | collective-permute-start | bytes 589832 | tf_op jit(solution)/shard_map/ppermute | solution.py:547
  34.6 7.8 %collective-permute-start.13 = (bf16[2,96,512]{2,1,0:T(8,128)(2,1)S(1)}, bf16[2,96,512]{2,1,0:T(8,128)(2,1)S(1)}, u32[]{:S(2)}, u32[]{:S(2)}) collective-permute-start(bf16[2,96,512]{2,1,0:T(8,128)(2,1)S(1)} %collective-permute-done.9.refs_8_), channel_id=1, source_target_pairs={{0,8},{1,9},{2,10},{3,11},{8,16},{9,17},{10,18},{11,19},{16,24},{1... | collective-permute-start | bytes 589832 | tf_op jit(solution)/shard_map/ppermute | solution.py:547
  35.3 9.5 %collective-permute-start.14 = (bf16[2,96,512]{2,1,0:T(8,128)(2,1)S(1)}, bf16[2,96,512]{2,1,0:T(8,128)(2,1)S(1)}, u32[]{:S(2)}, u32[]{:S(2)}) collective-permute-start(bf16[2,96,512]{2,1,0:T(8,128)(2,1)S(1)} %collective-permute-done.10.refs_9_), channel_id=1, source_target_pairs={{0,4},{1,5},{2,6},{3,7},{8,0},{9,1},{10,2},{11,3},{16,8},{17,9},{1... | collective-permute-start | bytes 589832 | tf_op jit(solution)/shard_map/ppermute | solution.py:547
  37.1 9.5 %collective-permute-start.19 = (bf16[2,96,512]{2,1,0:T(8,128)(2,1)S(1)}, bf16[2,96,512]{2,1,0:T(8,128)(2,1)S(1)}, u32[]{:S(2)}, u32[]{:S(2)}) collective-permute-start(bf16[2,96,512]{2,1,0:T(8,128)(2,1)S(1)} %collective-permute-done.15.refs_14_), channel_id=1, source_target_pairs={{0,8},{1,9},{2,10},{3,11},{8,16},{9,17},{10,18},{11,19},{16,24},{1... | collective-permute-start | bytes 589832 | tf_op jit(solution)/shard_map/ppermute | solution.py:547
  40.6 6.5 %collective-permute-start.20 = (bf16[2,96,512]{2,1,0:T(8,128)(2,1)S(1)}, bf16[2,96,512]{2,1,0:T(8,128)(2,1)S(1)}, u32[]{:S(2)}, u32[]{:S(2)}) collective-permute-start(bf16[2,96,512]{2,1,0:T(8,128)(2,1)S(1)} %collective-permute-done.16.refs_15_), channel_id=1, source_target_pairs={{0,4},{1,5},{2,6},{3,7},{8,0},{9,1},{10,2},{11,3},{16,8},{17,9},{1... | collective-permute-start | bytes 589832 | tf_op jit(solution)/shard_map/ppermute | solution.py:547
  42.3 6.6 %collective-permute-start.17 = (bf16[2,96,512]{2,1,0:T(8,128)(2,1)S(1)}, bf16[2,96,512]{2,1,0:T(8,128)(2,1)S(1)}, u32[]{:S(2)}, u32[]{:S(2)}) collective-permute-start(bf16[2,96,512]{2,1,0:T(8,128)(2,1)S(1)} %collective-permute-done.13.refs_12_), channel_id=1, source_target_pairs={{0,8},{1,9},{2,10},{3,11},{8,16},{9,17},{10,18},{11,19},{16,24},{1... | collective-permute-start | bytes 589832 | tf_op jit(solution)/shard_map/ppermute | solution.py:547
  44.8 11.7 %collective-permute-start.3 = (bf16[128,1536]{1,0:T(8,128)(2,1)S(1)}, bf16[128,1536]{1,0:T(8,128)(2,1)S(1)}, u32[]{:S(2)}, u32[]{:S(2)}) collective-permute-start(bf16[128,1536]{1,0:T(8,128)(2,1)S(1)} %get-tuple-element.60.refs_2_.cot_ref), channel_id=1, source_target_pairs={{0,1},{1,0},{2,3},{3,2},{4,5},{5,4},{6,7},{7,6},{8,9},{9,8},{10,11... | collective-permute-start | bytes 1179656 | tf_op jit(solution)/shard_map/ppermute | solution.py:547
  44.8 12.0 %collective-permute-start.2 = (bf16[128,1536]{1,0:T(8,128)(2,1)S(1)}, bf16[128,1536]{1,0:T(8,128)(2,1)S(1)}, u32[]{:S(2)}, u32[]{:S(2)}) collective-permute-start(bf16[128,1536]{1,0:T(8,128)(2,1)S(1)} %get-tuple-element.59.refs_1_), channel_id=1, source_target_pairs={{0,1},{1,0},{2,3},{3,2},{4,5},{5,4},{6,7},{7,6},{8,9},{9,8},{10,11... | collective-permute-start | bytes 1179656 | tf_op jit(solution)/shard_map/ppermute | solution.py:547
  46.6 12.1 %collective-permute-start.5 = (bf16[128,1536]{1,0:T(8,128)(2,1)S(1)}, bf16[128,1536]{1,0:T(8,128)(2,1)S(1)}, u32[]{:S(2)}, u32[]{:S(2)}) collective-permute-start(bf16[128,1536]{1,0:T(8,128)(2,1)S(1)} %collective-permute-done.4.refs_4_), channel_id=1, source_target_pairs={{0,1},{1,0},{2,3},{3,2},{4,5},{5,4},{6,7},{7,6},{8,9},{9,8},{10,11... | collective-permute-start | bytes 1179656 | tf_op jit(solution)/shard_map/ppermute | solution.py:547
  47.1 13.7 %collective-permute-start.22 = (bf16[128,1536]{1,0:T(8,128)(2,1)S(1)}, bf16[128,1536]{1,0:T(8,128)(2,1)S(1)}, u32[]{:S(2)}, u32[]{:S(2)}) collective-permute-start(bf16[128,1536]{1,0:T(8,128)(2,1)S(1)} %collective-permute-done.21.refs_1_.far_ref), channel_id=1, source_target_pairs={{0,1},{1,0},{2,3},{3,2},{4,5},{5,4},{6,7},{7,6},{8,9},{9,8},{10,11... | collective-permute-start | bytes 1179656 | tf_op jit(solution)/shard_map/ppermute | solution.py:547
  49.0 5.7 %collective-permute-start.18 = (bf16[2,96,512]{2,1,0:T(8,128)(2,1)S(1)}, bf16[2,96,512]{2,1,0:T(8,128)(2,1)S(1)}, u32[]{:S(2)}, u32[]{:S(2)}) collective-permute-start(bf16[2,96,512]{2,1,0:T(8,128)(2,1)S(1)} %collective-permute-done.14.refs_13_), channel_id=1, source_target_pairs={{0,4},{1,5},{2,6},{3,7},{8,0},{9,1},{10,2},{11,3},{16,8},{17,9},{1... | collective-permute-start | bytes 589832 | tf_op jit(solution)/shard_map/ppermute | solution.py:547
  54.7 6.8 %collective-permute-start.25 = (bf16[1,96,512]{2,1,0:T(8,128)(2,1)S(1)}, bf16[1,96,512]{2,1,0:T(8,128)(2,1)S(1)}, u32[]{:S(2)}, u32[]{:S(2)}) collective-permute-start(bf16[1,96,512]{2,1,0:T(8,128)(2,1)S(1)} %slice.18), channel_id=1, source_target_pairs={{0,8},{1,9},{2,10},{3,11},{8,16},{9,17},{10,18},{11,19},{16,24},{1... | collective-permute-start | bytes 294920 | tf_op jit(solution)/shard_map/ppermute | solution.py:547
  56.5 5.0 %collective-permute-start.26 = (bf16[1,96,512]{2,1,0:T(8,128)(2,1)S(1)}, bf16[1,96,512]{2,1,0:T(8,128)(2,1)S(1)}, u32[]{:S(2)}, u32[]{:S(2)}) collective-permute-start(bf16[1,96,512]{2,1,0:T(8,128)(2,1)S(1)} %slice.19), channel_id=1, source_target_pairs={{0,4},{1,5},{2,6},{3,7},{8,0},{9,1},{10,2},{11,3},{16,8},{17,9},{1... | collective-permute-start | bytes 294920 | tf_op jit(solution)/shard_map/ppermute | solution.py:547
  56.8 4.8 %collective-permute-start.23 = (bf16[1,96,512]{2,1,0:T(8,128)(2,1)S(1)}, bf16[1,96,512]{2,1,0:T(8,128)(2,1)S(1)}, u32[]{:S(2)}, u32[]{:S(2)}) collective-permute-start(bf16[1,96,512]{2,1,0:T(8,128)(2,1)S(1)} %slice.16), channel_id=1, source_target_pairs={{0,8},{1,9},{2,10},{3,11},{8,16},{9,17},{10,18},{11,19},{16,24},{1... | collective-permute-start | bytes 294920 | tf_op jit(solution)/shard_map/ppermute | solution.py:547
  58.6 4.6 %collective-permute-start.24 = (bf16[1,96,512]{2,1,0:T(8,128)(2,1)S(1)}, bf16[1,96,512]{2,1,0:T(8,128)(2,1)S(1)}, u32[]{:S(2)}, u32[]{:S(2)}) collective-permute-start(bf16[1,96,512]{2,1,0:T(8,128)(2,1)S(1)} %slice.17), channel_id=1, source_target_pairs={{0,4},{1,5},{2,6},{3,7},{8,0},{9,1},{10,2},{11,3},{16,8},{17,9},{1... | collective-permute-start | bytes 294920 | tf_op jit(solution)/shard_map/ppermute | solution.py:547
  66.7 15.7 %collective-permute-start.28 = (bf16[128,1536]{1,0:T(8,128)(2,1)S(1)}, bf16[128,1536]{1,0:T(8,128)(2,1)S(1)}, u32[]{:S(2)}, u32[]{:S(2)}) collective-permute-start(bf16[128,1536]{1,0:T(8,128)(2,1)S(1)} %shard_map.136), channel_id=1, source_target_pairs={{0,2},{1,3},{2,0},{3,1},{4,6},{5,7},{6,4},{7,5},{8,10},{9,11},{10,... | collective-permute-start | bytes 1179656 | tf_op jit(solution)/shard_map/ppermute | solution.py:547
  67.8 10.5 %collective-permute-start.30 = (bf16[2,32,128]{2,1,0:T(8,128)(2,1)S(1)}, bf16[2,32,128]{2,1,0:T(8,128)(2,1)S(1)}, u32[]{:S(2)}, u32[]{:S(2)}) collective-permute-start(bf16[2,32,128]{2,1,0:T(8,128)(2,1)S(1)} %get-tuple-element.80), channel_id=1, source_target_pairs={{0,2},{1,3},{2,0},{3,1},{4,6},{5,7},{6,4},{7,5},{8,10},{9,11},{10,... | collective-permute-start | bytes 49160 | tf_op jit(solution)/shard_map/ppermute | solution.py:547
  79.7 7.7 %collective-permute-start.31 = (bf16[32,1536]{1,0:T(8,128)(2,1)S(1)}, bf16[32,1536]{1,0:T(8,128)(2,1)S(1)}, u32[]{:S(2)}, u32[]{:S(2)}) collective-permute-start(bf16[32,1536]{1,0:T(8,128)(2,1)S(1)} %get-tuple-element.81), channel_id=1, source_target_pairs={{0,31},{1,2},{2,1},{3,4},{4,3},{5,6},{6,5},{7,8},{8,7},{9,10},{10,... | collective-permute-start | bytes 294920 | tf_op jit(solution)/shard_map/ppermute | solution.py:547
  82.3 6.7 %collective-permute-start.32 = (bf16[32,1536]{1,0:T(8,128)(2,1)S(1)}, bf16[32,1536]{1,0:T(8,128)(2,1)S(1)}, u32[]{:S(2)}, u32[]{:S(2)}) collective-permute-start(bf16[32,1536]{1,0:T(8,128)(2,1)S(1)} %get-tuple-element.82), channel_id=1, source_target_pairs={{2,31},{3,2},{0,1},{1,4},{6,3},{7,6},{4,5},{5,8},{10,7},{11,10},{8... | collective-permute-start | bytes 294920 | tf_op jit(solution)/shard_map/ppermute | solution.py:547
  83.3 5.8 %collective-permute-start.29 = (bf16[32,1536]{1,0:T(8,128)(2,1)S(1)}, bf16[32,1536]{1,0:T(8,128)(2,1)S(1)}, u32[]{:S(2)}, u32[]{:S(2)}) collective-permute-start(bf16[32,1536]{1,0:T(8,128)(2,1)S(1)} %get-tuple-element.79), channel_id=1, source_target_pairs={{0,1},{1,0},{2,3},{3,2},{4,5},{5,4},{6,7},{7,6},{8,9},{9,8},{10,11... | collective-permute-start | bytes 294920 | tf_op jit(solution)/shard_map/ppermute | solution.py:547
  (1 other events, 2.4 us)

commit v3 on v2

--- a/solution.py
+++ b/solution.py
@@ -278,7 +278,7 @@
     return [mix_ref[i, pl.ds(at, border)] for i in range(2)]
 
 
-def conv_body(x_ref, inner_ref, outer_ref, mix_ref, form_ref, gain_ref, conv_ref, norm_ref, edge_ref, ext):
+def conv_body(x_ref, inner_ref, outer_ref, mix_ref, form_ref, gain_ref, conv_ref, norm_ref, edge_ref, scale_ref, ext):
     columns, width = x_ref.shape
     border = inner_ref.shape[0]
     odd = lax.axis_index("patch") % 2
@@ -303,6 +303,7 @@
         square = square + out * out
     scale = lax.rsqrt(jnp.sum(square, axis=1, keepdims=True) / width + 1e-05)
     norm_ref[...] = (conv_ref[...].astype(jnp.float32) * scale * gain_ref[...]).astype(jnp.bfloat16)
+    scale_ref[...] = jnp.broadcast_to(scale, scale_ref.shape)
     across = jnp.broadcast_to(scale, (columns, columns)).T[:1]
     for i, rows in enumerate(border_mix(mix_ref, columns, border, odd)):
         edge_ref[i] = (rows.astype(jnp.float32) * across).astype(jnp.bfloat16)
@@ -316,7 +317,7 @@
     return jnp.where(place < groups // 2, 2 * place, 2 * (groups - 1 - place) + 1)
 
 
-STACK = (1, 3, 0, 2)
+STACK = (3, 2, 1, 0)
 
 
 def far_owner(groups):
@@ -373,8 +374,13 @@
     pre_ref[...] = mm(xs[...], ups[...])
 
 
-def send_body(groups, ups_in, pre_a, pre_b, back_ref, xa_last, xb_last, g_last, *refs):
-    parts, (ups, gate_ref, send_ref, up, down) = refs[:4], refs[4:]
+def gated(pre_act, back):
+    gate = jax.nn.sigmoid(pre_act)
+    return (back * gate * (1.0 + pre_act * (1.0 - gate))).astype(jnp.bfloat16)
+
+
+def send_body(groups, ups_in, pre_ref, back_ref, x_last, g_last, *refs):
+    parts, (ups, up, down, gate_ref, send_ref) = refs[:4], refs[4:]
     member = lax.axis_index("patch") % TEAM
     rows = parts[0].shape[1] // 2
     for k in range(2):
@@ -385,26 +391,26 @@
             down[pl.ds(at, rows)] = parts[2 * k + 1][0, part]
     tall = up.shape[0]
     ups[pl.ds(pl.multiple_of(far_owner(groups) * tall, 16), tall)] = up[...]
-    columns = send_ref.shape[1]
-    first = pre_a[...] + mm(xa_last[...], up[...])
-    second = pre_b[...] + mm(xb_last[...], up[...])
-    pre_act = jnp.concatenate(
-        [first[:columns], second[:columns], first[columns:], second[columns:]], axis=0
-    )
-    back = back_ref[...] + mm(g_last[...], down[...])
-    gate = jax.nn.sigmoid(pre_act)
-    grad_pre = (back * gate * (1.0 + pre_act * (1.0 - gate))).astype(jnp.bfloat16)
-    gate_ref[...] = grad_pre
-    rows = mm(grad_pre[: 2 * columns], ups[...], ((1,), (1,))).astype(jnp.bfloat16)
-    send_ref[0] = rows[:columns]
-    send_ref[1] = rows[columns:]
-
-
-def keep_body(gate_ref, ups, mine_ref, cross_ref):
+    columns = send_ref.shape[0]
+    two = slice(0, 2 * columns)
+    pre_act = pre_ref[...] + mm(x_last[...], up[...])
+    grad_pre = gated(pre_act, back_ref[two] + mm(g_last[two], down[...]))
+    gate_ref[...] = grad_pre[columns:]
+    send_ref[...] = mm(grad_pre[:columns], ups[...], ((1,), (1,))).astype(jnp.bfloat16)
+
+
+def cross_body(gate_ref, ups, cross_ref):
+    cross_ref[...] = mm(gate_ref[...], ups[...], ((1,), (1,)))
+
+
+def keep_body(ups, up, down, pre_ref, back_ref, x_last, g_last, mine_ref, send_ref):
     columns = mine_ref.shape[0]
-    rows = mm(gate_ref[2 * columns :], ups[...], ((1,), (1,)))
-    mine_ref[...] = rows[:columns]
-    cross_ref[...] = rows[columns:]
+    two = slice(2 * columns, 4 * columns)
+    pre_act = pre_ref[...] + mm(x_last[...], up[...])
+    grad_pre = gated(pre_act, back_ref[two] + mm(g_last[two], down[...]))
+    rows = mm(grad_pre, ups[...], ((1,), (1,)))
+    send_ref[...] = rows[:columns].astype(jnp.bfloat16)
+    mine_ref[...] = rows[columns:]
 
 
 def shifted_back(mix, form, grads):
@@ -418,7 +424,7 @@
 
 
 def join_body(cross_ref, part_ref, out_ref):
-    out_ref[...] = (cross_ref[...] + part_ref[1].astype(jnp.float32)).astype(jnp.bfloat16)
+    out_ref[...] = (cross_ref[...] + part_ref[...].astype(jnp.float32)).astype(jnp.bfloat16)
 
 
 def column_grad(grad_normed, values, scale, gain):
@@ -427,65 +433,72 @@
     return scale * scaled - values * (scale * scale * scale * mixed)
 
 
-def scale_of(values):
-    return lax.rsqrt(jnp.sum(values * values, axis=1, keepdims=True) / values.shape[1] + 1e-05)
-
-
-def edge_body(
-    mine_ref, cross_ref, part_ref, conv_ref, cot_ref, far_ref, gain_ref, mix_ref, edge_ref, form_ref, own_ref, other_ref
-):
-    columns, _ = conv_ref.shape
-    border = own_ref.shape[0]
+def put_back(target, mix, form, grads):
+    for b, rows in enumerate(shifted_back(mix, form, grads)):
+        target[:, b * BLOCK : (b + 1) * BLOCK] = rows.astype(jnp.bfloat16)
+
+
+def other_body(cross_ref, part_ref, far_ref, gain_ref, edge_ref, form_ref, out_ref):
+    scaled_values = far_ref[...].astype(jnp.float32) / gain_ref[...]
+    share = cross_ref[...] + part_ref[...].astype(jnp.float32)
+    grads = column_grad(share, scaled_values, 1.0, gain_ref[...]).astype(jnp.bfloat16)
+    put_back(out_ref, [edge_ref[i] for i in range(2)], form_ref[0], grads)
+
+
+def edge_body(mine_ref, part_ref, conv_ref, cot_ref, scale_ref, gain_ref, mix_ref, form_ref, base_ref, out_ref):
+    values = conv_ref[...].astype(jnp.float32)
+    share = mine_ref[...] + part_ref[...].astype(jnp.float32)
+    grads = column_grad(share, values, scale_ref[:, :1], gain_ref[...])
+    grads = cot_ref[...].astype(jnp.float32) + grads
+    base_ref[...] = grads
     odd = lax.axis_index("patch") % 2
+    mix = border_mix(mix_ref, conv_ref.shape[0], out_ref.shape[0], odd)
+    put_back(out_ref, mix, form_ref[0], grads.astype(jnp.bfloat16))
+
+
+def grad_body(base_ref, cross_ref, conv_ref, scale_ref, gain_ref, mix_ref, form_ref, grad_ref, inner_ref):
     values = conv_ref[...].astype(jnp.float32)
-    share = mine_ref[...] + part_ref[0].astype(jnp.float32)
-    grads = column_grad(share, values, scale_of(values), gain_ref[...])
-    grads = (cot_ref[...].astype(jnp.float32) + grads).astype(jnp.bfloat16)
-    outer = border_mix(mix_ref, columns, border, odd)
-    scaled_values = far_ref[...].astype(jnp.float32) / gain_ref[...]
-    share = cross_ref[...] + part_ref[1].astype(jnp.float32)
-    others = column_grad(share, scaled_values, 1.0, gain_ref[...]).astype(jnp.bfloat16)
-    edge = [edge_ref[i] for i in range(2)]
-    for ref, mix, source in ((own_ref, outer, grads), (other_ref, edge, others)):
-        for b, rows in enumerate(shifted_back(mix, form_ref[0], source)):
-            ref[:, b * BLOCK : (b + 1) * BLOCK] = rows.astype(jnp.bfloat16)
-
-
-def grad_body(
-    mine_ref, part_ref, cross_ref, conv_ref, cot_ref, gain_ref, mix_ref, form_ref, grad_ref, inner_ref
-):
-    columns, _ = conv_ref.shape
-    border = inner_ref.shape[0]
+    share = cross_ref[...].astype(jnp.float32)
+    grads = column_grad(share, values, scale_ref[:, :1], gain_ref[...])
+    grads = (base_ref[...] + grads).astype(jnp.bfloat16)
+    grad_ref[...] = grads
     odd = lax.axis_index("patch") % 2
-    grad_normed = mine_ref[...] + part_ref[0].astype(jnp.float32) + cross_ref[...].astype(jnp.float32)
-    values = conv_ref[...].astype(jnp.float32)
-    grads = column_grad(grad_normed, values, scale_of(values), gain_ref[...])
-    grads = (cot_ref[...].astype(jnp.float32) + grads).astype(jnp.bfloat16)
-    grad_ref[...] = grads
-    inner = border_mix(mix_ref, columns, border, 1 - odd)
-    for b, rows in enumerate(shifted_back(inner, form_ref[0], grads)):
-        inner_ref[:, b * BLOCK : (b + 1) * BLOCK] = rows.astype(jnp.bfloat16)
+    mix = border_mix(mix_ref, conv_ref.shape[0], inner_ref.shape[0], 1 - odd)
+    put_back(inner_ref, mix, form_ref[0], grads)
+
+
+def parity_rows(bound_ref, columns, border):
+    chosen = picked(bound_ref, columns).astype(jnp.float32)
+    low, high = chosen[:, :border], chosen[:, border:]
+    inner = jnp.where(is_even(), high, low).astype(jnp.bfloat16)
+    outer = jnp.where(is_even(), low, high).astype(jnp.bfloat16)
+    return inner, outer
 
 
 def own_body(grad_ref, mix_ref, form_ref, local_ref):
     columns, _ = grad_ref.shape
     grads = grad_ref[...]
-    inner = [mix_ref[i, :columns] for i in range(2)]
-    for b, rows in enumerate(shifted_back(inner, form_ref[0], grads)):
+    mix = [mix_ref[i, :columns] for i in range(2)]
+    for b, rows in enumerate(shifted_back(mix, form_ref[0], grads)):
         at = slice(b * BLOCK, (b + 1) * BLOCK)
         own = grads[:, at]
-        local_ref[:, at] = own.astype(jnp.float32) + (mm(own, form_ref[1], ((1,), (1,))) + rows)
-
-
-def last_body(local_ref, inner_ref, outer_ref, other_ref, bound_ref, out_ref):
-    border = inner_ref.shape[0]
-    chosen = picked(bound_ref, local_ref.shape[0]).astype(jnp.float32)
-    low, high = chosen[:, :border], chosen[:, border:]
-    inner = jnp.where(is_even(), high, low).astype(jnp.bfloat16)
-    outer = jnp.where(is_even(), low, high).astype(jnp.bfloat16)
-    total = local_ref[...] + mm(inner, inner_ref[...])
-    total = total + (mm(outer, outer_ref[...]) + mm(outer, other_ref[...]))
-    out_ref[...] = total.astype(jnp.bfloat16)
+        rows = rows + mm(own, form_ref[1], ((1,), (1,)))
+        local_ref[:, at] = own.astype(jnp.float32) + rows
+
+
+def last_body(local_ref, inner_ref, outer_ref, other_ref, bound_ref, out_ref, held, sem):
+    columns, width = local_ref.shape
+    inner, outer = parity_rows(bound_ref, columns, inner_ref.shape[0])
+    pick = jnp.concatenate([inner, outer, outer], axis=1)
+    copies = []
+    for b in range(width // BLOCK // 2):
+        at = slice(2 * b * BLOCK, 2 * (b + 1) * BLOCK)
+        rows = jnp.concatenate([inner_ref[:, at], outer_ref[:, at], other_ref[:, at]], axis=0)
+        held[:, at] = (local_ref[:, at] + mm(pick, rows)).astype(jnp.bfloat16)
+        copies.append(pltpu.make_async_copy(held.at[:, at], out_ref.at[:, at], sem.at[b]))
+        copies[-1].start()
+    for one in copies:
+        one.wait()
 
 
 def per_device(
@@ -512,7 +525,7 @@
         lax.axis_size("level") == 1
         and samples == 1
         and devices % (2 * TEAM) == 0
-        and width % BLOCK == 0
+        and width % (2 * BLOCK) == 0
         and hidden % (TEAM * 128) == 0
         and rows % 16 == 0
         and border % 16 == 0
@@ -624,9 +637,13 @@
         ],
         tables,
     )
-    conv, norm, edge = call(
+    conv, norm, edge, scale = call(
         conv_body,
-        [struct((columns, width))] * 2 + [struct((2, border, columns))],
+        [
+            *[struct((columns, width))] * 2,
+            struct((2, border, columns)),
+            struct((columns, 128), jnp.float32),
+        ],
         [x, inner_rows, outer_rows, mix, form, gain],
         [pltpu.VMEM((extent, width), jnp.bfloat16)],
     )
@@ -660,35 +677,61 @@
         [norm_cross, norm_far, ups],
         [pltpu.VMEM((team // 2, width), jnp.bfloat16)],
     )
-    ups, gate, send = call(
+    ups, up_last, down_last, gate, send_cross = call(
         lambda *refs: send_body(groups, *refs),
-        [struct((width, span)), struct((team, span)), struct((2, columns, width))],
-        [ups, pre_a, pre_b, back_sum, xa_last, xb_last, g_last, *last_chunks],
-        [pltpu.VMEM((tall, span), jnp.bfloat16)] * 2,
+        [
+            struct((width, span)),
+            *[struct((tall, span))] * 2,
+            struct((columns, span)),
+            struct((columns, width)),
+        ],
+        [ups, pre_b, back_sum, xb_last, g_last, *last_chunks],
+        (),
         (),
         ((0, 0),),
     )
-    mine, cross = call(keep_body, [wide, wide], [gate, ups])
+    received_cross = swap(send_cross, 1)
+    cross = call(cross_body, wide, [gate, ups])
+    crossing = call(join_body, struct((columns, width)), [cross, received_cross])
+    crossed = swap(crossing, 2)
+    mine, send = call(
+        keep_body,
+        [wide, struct((columns, width))],
+        [ups, up_last, down_last, pre_a, back_sum, xa_last, g_last],
+    )
     received = swap(send, 1)
-    crossing = call(join_body, struct((columns, width)), [cross, received])
-    crossed = swap(crossing, 2)
-    own_rows, other_rows = call(
+    other_rows = call(
+        other_body, struct((border, width)), [cross, received_cross, norm_far, gain, edge, form]
+    )
+    other_rows = outer(other_rows, 2)
+    base, own_rows = call(
         edge_body,
-        [struct((border, width))] * 2,
-        [mine, cross, received, conv, cot, norm_far, gain, mix, edge, form],
+        [wide, struct((border, width))],
+        [mine, received, conv, cot, scale, gain, mix, form],
     )
     own_rows = outer(own_rows)
-    other_rows = outer(other_rows, 2)
     grads, inner_back = call(
         grad_body,
         [struct((columns, width)), struct((border, width))],
-        [mine, received, crossed, conv, cot, gain, mix, form],
+        [base, crossed, conv, scale, gain, mix, form],
     )
     inner_back = swap(inner_back, 1)
     local = call(own_body, wide, [grads, mix, form])
+    pieces = width // BLOCK // 2
     out = pl.pallas_call(
-        last_body, out_shape=jax.ShapeDtypeStruct((columns, width), jnp.bfloat16)
-    )(*(pltpu.with_memory_space_constraint(v, pltpu.VMEM) for v in (local, inner_back, own_rows, other_rows, boundary)))
+        last_body,
+        out_shape=jax.ShapeDtypeStruct((columns, width), jnp.bfloat16),
+        out_specs=pl.BlockSpec(memory_space=pl.ANY),
+        scratch_shapes=[
+            pltpu.VMEM((columns, width), jnp.bfloat16),
+            pltpu.SemaphoreType.DMA((pieces,)),
+        ],
+    )(
+        *(
+            pltpu.with_memory_space_constraint(value, pltpu.VMEM)
+            for value in (local, inner_back, own_rows, other_rows, boundary)
+        )
+    )
     return out[None]
 
 

time: 90.6 us -> 89.2 us (0.985)
  waiting for transfers between devices: 39.1 us -> 34.8 us
  starting transfers between devices: 37.7 us -> 39.7 us
    ppermute x33 -> x34, waiting for transfers between devices: 39.1 us -> 34.8 us  [permute(): return lax.ppermute(value, 'patch', pairs)]
    ppermute x33 -> x34, starting transfers between devices: 37.7 us -> 39.7 us  [permute(): return lax.ppermute(value, 'patch', pairs)]
    pallas_call x13 -> x15, Pallas kernels: 12 us -> 13 us  [call(): pl.pallas_call(body, out_shape=outs, in_specs=specs, out_specs=jax.tree.m...]
  transfers between devices with their start and end apart: 33 -> 34, of which waited for: 17 -> 15; matrix products, arithmetic and copies ran while one was open for 0% -> 0% of each run, Pallas kernels for 11% -> 12%
where the time goes in v3:
time: 89.2 us; the launch traced here: 89 us
  starting transfers between devices  39.7 us (45%)
  waiting for transfers between devices  34.8 us (39%)
  Pallas kernels  14.1 us (16%)
    ppermute x34, starting transfers between devices, permute(): return lax.ppermute(value, 'patch', pairs)  39.7 us
    ppermute x34, waiting for transfers between devices, permute(): return lax.ppermute(value, 'patch', pairs)  34.8 us
    pallas_call x15, Pallas kernels, call(): pl.pallas_call(body, out_shape=outs, in_specs=specs, out_specs=jax.tree.m...  13 us
  transfers between devices with their start and end apart: 34, of which 15 were waited for; matrix products, arithmetic and copies ran while one was open for 0% of the time, Pallas kernels for 12%

profile of v3, /device:TPU:0, one launch (start us, length us, event | category | flops | bytes accessed | tf_op | source)
XLA Modules:
  0.0 89.0 jit_solution(5437826901335417012)
XLA Ops:
  0.0 1.2 %shard_map.127 = (bf16[128,1536]{1,0:T(8,128)(2,1)S(1)}, bf16[128,1536]{1,0:T(8,128)(2,1)S(1)}, s32[1,64]{1,0:T(1,128)S(1)}, s32[6,128]{1,0:T(8,128)S(1)}, s32[6...) custom-call(bf16[128,1536]{1,0:T(8,128)(2,1)} %bitcast.7, ...), custom_call_target="tpu_custom_call" | custom-call | tf_op jit(solution)/shard_map/pallas_call | solution.py:174
  2.0 6.6 %collective-permute-start.1 = (bf16[32,1536]{1,0:T(8,128)(2,1)S(1)}, bf16[32,1536]{1,0:T(8,128)(2,1)S(1)}, u32[]{:S(2)}, u32[]{:S(2)}) collective-permute-start(bf16[32,1536]{1,0:T(8,128)(2,1)S(1)} %get-tuple-element.50), channel_id=1, source_target_pairs={{0,31},{1,2},{2,1},{3,4},{4,3},{5,6},{6,5},{7,8},{8,7},{9,10},{10,... | collective-permute-start | bytes 294920 | tf_op jit(solution)/shard_map/ppermute | solution.py:560
  8.6 1.0 %shard_map.131 = (bf16[2,48,512]{2,1,0:T(8,128)(2,1)S(1)}, bf16[2,48,512]{2,1,0:T(8,128)(2,1)S(1)}, bf16[2,48,512]{2,1,0:T(8,128)(2,1)S(1)}, bf16[2,48,512]{2,1,0:T(8,128)(2,1)S(1)}) custom-call(bf16[48,2048]{1,0:T(8,128)(2,1)} %up_ref.1, bf16[48,2048]{1,0:T(8,128)(2,1)} %down_ref.1), custom_call_target="tpu_custom_call" | custom-call | tf_op jit(solution)/shard_map/pallas_call | solution.py:174
  9.7 2.1 %collective-permute-start.7 = (bf16[2,48,512]{2,1,0:T(8,128)(2,1)S(1)}, bf16[2,48,512]{2,1,0:T(8,128)(2,1)S(1)}, u32[]{:S(2)}, u32[]{:S(2)}) collective-permute-start(bf16[2,48,512]{2,1,0:T(8,128)(2,1)S(1)} %get-tuple-element.66), channel_id=1, source_target_pairs={{0,2},{1,3},{2,0},{3,1},{4,6},{5,7},{6,4},{7,5},{8,10},{9,11},{10,... | collective-permute-start | bytes 294920 | tf_op jit(solution)/shard_map/ppermute | solution.py:560
  11.8 8.1 %collective-permute-done.7 = bf16[2,48,512]{2,1,0:T(8,128)(2,1)S(1)} collective-permute-done((bf16[2,48,512]{2,1,0:T(8,128)(2,1)S(1)}, bf16[2,48,512]{2,1,0:T(8,128)(2,1)S(1)}, u32[]{:S(2)}, u32[]{:S(2)}) %collective-permute-start.7) | collective-permute-done | bytes 98336 | tf_op jit(solution)/shard_map/ppermute | solution.py:560
  20.0 2.8 %collective-permute-start.11 = (bf16[2,96,512]{2,1,0:T(8,128)(2,1)S(1)}, bf16[2,96,512]{2,1,0:T(8,128)(2,1)S(1)}, u32[]{:S(2)}, u32[]{:S(2)}) collective-permute-start(bf16[2,96,512]{2,1,0:T(8,128)(2,1)S(1)} %constant_dynamic-update-slice_fusion.2.refs_7_), channel_id=1, source_target_pairs={{0,8},{1,9},{2,10},{3,11},{8,16},{9,17},{10,18},{11,19},{16,24},{1... | collective-permute-start | bytes 589832 | tf_op jit(solution)/shard_map/ppermute | solution.py:560
  22.9 2.1 %collective-permute-start.9 = (bf16[2,96,512]{2,1,0:T(8,128)(2,1)S(1)}, bf16[2,96,512]{2,1,0:T(8,128)(2,1)S(1)}, u32[]{:S(2)}, u32[]{:S(2)}) collective-permute-start(bf16[2,96,512]{2,1,0:T(8,128)(2,1)S(1)} %constant_dynamic-update-slice_fusion.refs_6_), channel_id=1, source_target_pairs={{0,8},{1,9},{2,10},{3,11},{8,16},{9,17},{10,18},{11,19},{16,24},{1... | collective-permute-start | bytes 589832 | tf_op jit(solution)/shard_map/ppermute | solution.py:560
  25.7 1.0 %shard_map.130 = (bf16[128,1536]{1,0:T(8,128)(2,1)S(1)}, bf16[128,1536]{1,0:T(8,128)(2,1)S(1)}, bf16[2,32,128]{2,1,0:T(8,128)(2,1)S(1)}, f32[128,128]{1,0:T(8,128)S(1)}) custom-call(bf16[128,1536]{1,0:T(8,128)(2,1)S(1)} %get-tuple-element.47.x_ref, bf16[32,1536]{1,0:T(8,128)(2,1)S(1)} %collective-permute-done.inner_ref, ...), custom_call_target="tpu_custom_call" | custom-call | tf_op jit(solution)/shard_map/pallas_call | solution.py:174
  26.7 1.6 %collective-permute-done.11.refs_10_ = bf16[2,96,512]{2,1,0:T(8,128)(2,1)S(1)} collective-permute-done((bf16[2,96,512]{2,1,0:T(8,128)(2,1)S(1)}, bf16[2,96,512]{2,1,0:T(8,128)(2,1)S(1)}, u32[]{:S(2)}, u32[]{:S(2)}) %collective-permute-start.11) | collective-permute-done | bytes 196640 | tf_op jit(solution)/shard_map/ppermute | solution.py:560
  29.3 1.3 %collective-permute-done.12.refs_11_ = bf16[2,96,512]{2,1,0:T(8,128)(2,1)S(1)} collective-permute-done((bf16[2,96,512]{2,1,0:T(8,128)(2,1)S(1)}, bf16[2,96,512]{2,1,0:T(8,128)(2,1)S(1)}, u32[]{:S(2)}, u32[]{:S(2)}) %collective-permute-start.12) | collective-permute-done | bytes 196640 | tf_op jit(solution)/shard_map/ppermute | solution.py:560
  30.6 1.6 %collective-permute-start.15 = (bf16[2,96,512]{2,1,0:T(8,128)(2,1)S(1)}, bf16[2,96,512]{2,1,0:T(8,128)(2,1)S(1)}, u32[]{:S(2)}, u32[]{:S(2)}) collective-permute-start(bf16[2,96,512]{2,1,0:T(8,128)(2,1)S(1)} %collective-permute-done.11.refs_10_), channel_id=1, source_target_pairs={{0,8},{1,9},{2,10},{3,11},{8,16},{9,17},{10,18},{11,19},{16,24},{1... | collective-permute-start | bytes 589832 | tf_op jit(solution)/shard_map/ppermute | solution.py:560
  32.5 2.0 %collective-permute-start.16 = (bf16[2,96,512]{2,1,0:T(8,128)(2,1)S(1)}, bf16[2,96,512]{2,1,0:T(8,128)(2,1)S(1)}, u32[]{:S(2)}, u32[]{:S(2)}) collective-permute-start(bf16[2,96,512]{2,1,0:T(8,128)(2,1)S(1)} %collective-permute-done.12.refs_11_), channel_id=1, source_target_pairs={{0,4},{1,5},{2,6},{3,7},{8,0},{9,1},{10,2},{11,3},{16,8},{17,9},{1... | collective-permute-start | bytes 589832 | tf_op jit(solution)/shard_map/ppermute | solution.py:560
  35.3 1.3 %collective-permute-start.14 = (bf16[2,96,512]{2,1,0:T(8,128)(2,1)S(1)}, bf16[2,96,512]{2,1,0:T(8,128)(2,1)S(1)}, u32[]{:S(2)}, u32[]{:S(2)}) collective-permute-start(bf16[2,96,512]{2,1,0:T(8,128)(2,1)S(1)} %collective-permute-done.10.refs_9_), channel_id=1, source_target_pairs={{0,4},{1,5},{2,6},{3,7},{8,0},{9,1},{10,2},{11,3},{16,8},{17,9},{1... | collective-permute-start | bytes 589832 | tf_op jit(solution)/shard_map/ppermute | solution.py:560
  37.1 2.5 %collective-permute-start.19 = (bf16[2,96,512]{2,1,0:T(8,128)(2,1)S(1)}, bf16[2,96,512]{2,1,0:T(8,128)(2,1)S(1)}, u32[]{:S(2)}, u32[]{:S(2)}) collective-permute-start(bf16[2,96,512]{2,1,0:T(8,128)(2,1)S(1)} %collective-permute-done.15.refs_14_), channel_id=1, source_target_pairs={{0,8},{1,9},{2,10},{3,11},{8,16},{9,17},{10,18},{11,19},{16,24},{1... | collective-permute-start | bytes 589832 | tf_op jit(solution)/shard_map/ppermute | solution.py:560
  39.5 1.1 %collective-permute-done.16.refs_15_ = bf16[2,96,512]{2,1,0:T(8,128)(2,1)S(1)} collective-permute-done((bf16[2,96,512]{2,1,0:T(8,128)(2,1)S(1)}, bf16[2,96,512]{2,1,0:T(8,128)(2,1)S(1)}, u32[]{:S(2)}, u32[]{:S(2)}) %collective-permute-start.16) | collective-permute-done | bytes 196640 | tf_op jit(solution)/shard_map/ppermute | solution.py:560
  40.6 1.7 %collective-permute-start.20 = (bf16[2,96,512]{2,1,0:T(8,128)(2,1)S(1)}, bf16[2,96,512]{2,1,0:T(8,128)(2,1)S(1)}, u32[]{:S(2)}, u32[]{:S(2)}) collective-permute-start(bf16[2,96,512]{2,1,0:T(8,128)(2,1)S(1)} %collective-permute-done.16.refs_15_), channel_id=1, source_target_pairs={{0,4},{1,5},{2,6},{3,7},{8,0},{9,1},{10,2},{11,3},{16,8},{17,9},{1... | collective-permute-start | bytes 589832 | tf_op jit(solution)/shard_map/ppermute | solution.py:560
  42.3 1.4 %collective-permute-start.17 = (bf16[2,96,512]{2,1,0:T(8,128)(2,1)S(1)}, bf16[2,96,512]{2,1,0:T(8,128)(2,1)S(1)}, u32[]{:S(2)}, u32[]{:S(2)}) collective-permute-start(bf16[2,96,512]{2,1,0:T(8,128)(2,1)S(1)} %collective-permute-done.13.refs_12_), channel_id=1, source_target_pairs={{0,8},{1,9},{2,10},{3,11},{8,16},{9,17},{10,18},{11,19},{16,24},{1... | collective-permute-start | bytes 589832 | tf_op jit(solution)/shard_map/ppermute | solution.py:560
  43.8 1.0 %collective-permute-done.14.refs_13_ = bf16[2,96,512]{2,1,0:T(8,128)(2,1)S(1)} collective-permute-done((bf16[2,96,512]{2,1,0:T(8,128)(2,1)S(1)}, bf16[2,96,512]{2,1,0:T(8,128)(2,1)S(1)}, u32[]{:S(2)}, u32[]{:S(2)}) %collective-permute-start.14) | collective-permute-done | bytes 196640 | tf_op jit(solution)/shard_map/ppermute | solution.py:560
  45.3 1.2 %collective-permute-done.19.refs_18_ = bf16[2,96,512]{2,1,0:T(8,128)(2,1)S(1)} collective-permute-done((bf16[2,96,512]{2,1,0:T(8,128)(2,1)S(1)}, bf16[2,96,512]{2,1,0:T(8,128)(2,1)S(1)}, u32[]{:S(2)}, u32[]{:S(2)}) %collective-permute-start.19) | collective-permute-done | bytes 196640 | tf_op jit(solution)/shard_map/ppermute | solution.py:560
  47.1 1.9 %collective-permute-done.17.refs_16_ = bf16[2,96,512]{2,1,0:T(8,128)(2,1)S(1)} collective-permute-done((bf16[2,96,512]{2,1,0:T(8,128)(2,1)S(1)}, bf16[2,96,512]{2,1,0:T(8,128)(2,1)S(1)}, u32[]{:S(2)}, u32[]{:S(2)}) %collective-permute-start.17) | collective-permute-done | bytes 196640 | tf_op jit(solution)/shard_map/ppermute | solution.py:560
  49.0 1.7 %collective-permute-start.18 = (bf16[2,96,512]{2,1,0:T(8,128)(2,1)S(1)}, bf16[2,96,512]{2,1,0:T(8,128)(2,1)S(1)}, u32[]{:S(2)}, u32[]{:S(2)}) collective-permute-start(bf16[2,96,512]{2,1,0:T(8,128)(2,1)S(1)} %collective-permute-done.14.refs_13_), channel_id=1, source_target_pairs={{0,4},{1,5},{2,6},{3,7},{8,0},{9,1},{10,2},{11,3},{16,8},{17,9},{1... | collective-permute-start | bytes 589832 | tf_op jit(solution)/shard_map/ppermute | solution.py:560
  50.8 3.9 %collective-permute-done.18.refs_17_ = bf16[2,96,512]{2,1,0:T(8,128)(2,1)S(1)} collective-permute-done((bf16[2,96,512]{2,1,0:T(8,128)(2,1)S(1)}, bf16[2,96,512]{2,1,0:T(8,128)(2,1)S(1)}, u32[]{:S(2)}, u32[]{:S(2)}) %collective-permute-start.18) | collective-permute-done | bytes 196640 | tf_op jit(solution)/shard_map/ppermute | solution.py:560
  54.7 1.8 %collective-permute-start.25 = (bf16[1,96,512]{2,1,0:T(8,128)(2,1)S(1)}, bf16[1,96,512]{2,1,0:T(8,128)(2,1)S(1)}, u32[]{:S(2)}, u32[]{:S(2)}) collective-permute-start(bf16[1,96,512]{2,1,0:T(8,128)(2,1)S(1)} %slice.18), channel_id=1, source_target_pairs={{0,8},{1,9},{2,10},{3,11},{8,16},{9,17},{10,18},{11,19},{16,24},{1... | collective-permute-start | bytes 294920 | tf_op jit(solution)/shard_map/ppermute | solution.py:560
  56.8 1.8 %collective-permute-start.23 = (bf16[1,96,512]{2,1,0:T(8,128)(2,1)S(1)}, bf16[1,96,512]{2,1,0:T(8,128)(2,1)S(1)}, u32[]{:S(2)}, u32[]{:S(2)}) collective-permute-start(bf16[1,96,512]{2,1,0:T(8,128)(2,1)S(1)} %slice.16), channel_id=1, source_target_pairs={{0,8},{1,9},{2,10},{3,11},{8,16},{9,17},{10,18},{11,19},{16,24},{1... | collective-permute-start | bytes 294920 | tf_op jit(solution)/shard_map/ppermute | solution.py:560
  58.8 1.9 %shard_map.132 = (bf16[1536,512]{1,0:T(8,128)(2,1)S(1)}, f32[256,512]{1,0:T(8,128)S(1)}, f32[512,512]{1,0:T(8,128)S(1)}, bf16[256,192]{1,0:T(8,128)(2,1)S(1)}, bf16[512,192]{1,0:T(8,128)(2,1)S(1)}) custom-call(bf16[128,1536]{1,0:T(8,128)(2,1)S(1)} %collective-permute-done.2.refs_0_, bf16[128,1536]{1,0:T(8,128)(2,1)S(1)} %get-tuple-element.62.refs_1_, ...), custom_call_target="tpu_custom_call" | custom-call | tf_op jit(solution)/shard_map/pallas_call | solution.py:174
  61.6 1.7 %collective-permute-done.24.refs_6_ = bf16[1,96,512]{2,1,0:T(8,128)(2,1)S(1)} collective-permute-done((bf16[1,96,512]{2,1,0:T(8,128)(2,1)S(1)}, bf16[1,96,512]{2,1,0:T(8,128)(2,1)S(1)}, u32[]{:S(2)}, u32[]{:S(2)}) %collective-permute-start.24) | collective-permute-done | bytes 98336 | tf_op jit(solution)/shard_map/ppermute | solution.py:560
  66.4 1.1 %collective-permute-start.29 = (bf16[128,1536]{1,0:T(8,128)(2,1)S(1)}, bf16[128,1536]{1,0:T(8,128)(2,1)S(1)}, u32[]{:S(2)}, u32[]{:S(2)}) collective-permute-start(bf16[128,1536]{1,0:T(8,128)(2,1)S(1)} %shard_map.138), channel_id=1, source_target_pairs={{0,2},{1,3},{2,0},{3,1},{4,6},{5,7},{6,4},{7,5},{8,10},{9,11},{10,... | collective-permute-start | bytes 1179656 | tf_op jit(solution)/shard_map/ppermute | solution.py:560
  67.5 1.0 %collective-permute-start.32 = (bf16[2,32,128]{2,1,0:T(8,128)(2,1)S(1)}, bf16[2,32,128]{2,1,0:T(8,128)(2,1)S(1)}, u32[]{:S(2)}, u32[]{:S(2)}) collective-permute-start(bf16[2,32,128]{2,1,0:T(8,128)(2,1)S(1)} %get-tuple-element.88), channel_id=1, source_target_pairs={{0,2},{1,3},{2,0},{3,1},{4,6},{5,7},{6,4},{7,5},{8,10},{9,11},{10,... | collective-permute-start | bytes 49160 | tf_op jit(solution)/shard_map/ppermute | solution.py:560
  68.5 9.4 %collective-permute-done.32.edge_ref = bf16[2,32,128]{2,1,0:T(8,128)(2,1)S(1)} collective-permute-done((bf16[2,32,128]{2,1,0:T(8,128)(2,1)S(1)}, bf16[2,32,128]{2,1,0:T(8,128)(2,1)S(1)}, u32[]{:S(2)}, u32[]{:S(2)}) %collective-permute-start.32) | collective-permute-done | bytes 16416 | tf_op jit(solution)/shard_map/ppermute | solution.py:560
  79.9 3.8 %collective-permute-start.31 = (bf16[32,1536]{1,0:T(8,128)(2,1)S(1)}, bf16[32,1536]{1,0:T(8,128)(2,1)S(1)}, u32[]{:S(2)}, u32[]{:S(2)}) collective-permute-start(bf16[32,1536]{1,0:T(8,128)(2,1)S(1)} %get-tuple-element.87), channel_id=1, source_target_pairs={{0,31},{1,2},{2,1},{3,4},{4,3},{5,6},{6,5},{7,8},{8,7},{9,10},{10,... | collective-permute-start | bytes 294920 | tf_op jit(solution)/shard_map/ppermute | solution.py:560
  85.7 2.0 %collective-permute-done.31.outer_ref = bf16[32,1536]{1,0:T(8,128)(2,1)S(1)} collective-permute-done((bf16[32,1536]{1,0:T(8,128)(2,1)S(1)}, bf16[32,1536]{1,0:T(8,128)(2,1)S(1)}, u32[]{:S(2)}, u32[]{:S(2)}) %collective-permute-start.31) | collective-permute-done | bytes 98336 | tf_op jit(solution)/shard_map/ppermute | solution.py:560
  87.7 1.1 %shard_map.142 = bf16[128,1536]{1,0:T(8,128)(2,1)} custom-call(f32[128,1536]{1,0:T(8,128)S(1)} %shard_map.140.local_ref, bf16[32,1536]{1,0:T(8,128)(2,1)S(1)} %collective-permute-done.30.inner_ref, bf16[32,1536]{1,0:T(8,128)(2,1)S(1)} %collective-permute-done.31.outer_ref, bf16[32,1536]{1,0:T(8,128)(2,1)S(1)} %collective-permute-done.33.other_ref, ...), custom_call_target="tpu_custom_call" | custom-call | tf_op jit(solution)/shard_map/pallas_call | solution.py:721
  (60 shorter events, 13.6 us)
Async XLA Ops:
  1.5 21.4 %collective-permute-start = (bf16[32,1536]{1,0:T(8,128)(2,1)S(1)}, bf16[32,1536]{1,0:T(8,128)(2,1)S(1)}, u32[]{:S(2)}, u32[]{:S(2)}) collective-permute-start(bf16[32,1536]{1,0:T(8,128)(2,1)S(1)} %get-tuple-element.49), channel_id=1, source_target_pairs={{0,1},{1,0},{2,3},{3,2},{4,5},{5,4},{6,7},{7,6},{8,9},{9,8},{10,11... | collective-permute-start | bytes 294920 | tf_op jit(solution)/shard_map/ppermute | solution.py:560
  2.0 23.6 %collective-permute-start.1 = (bf16[32,1536]{1,0:T(8,128)(2,1)S(1)}, bf16[32,1536]{1,0:T(8,128)(2,1)S(1)}, u32[]{:S(2)}, u32[]{:S(2)}) collective-permute-start(bf16[32,1536]{1,0:T(8,128)(2,1)S(1)} %get-tuple-element.50), channel_id=1, source_target_pairs={{0,31},{1,2},{2,1},{3,4},{4,3},{5,6},{6,5},{7,8},{8,7},{9,10},{10,... | collective-permute-start | bytes 294920 | tf_op jit(solution)/shard_map/ppermute | solution.py:560
  8.6 26.7 %collective-permute-start.4 = (bf16[128,1536]{1,0:T(8,128)(2,1)S(1)}, bf16[128,1536]{1,0:T(8,128)(2,1)S(1)}, u32[]{:S(2)}, u32[]{:S(2)}) collective-permute-start(bf16[128,1536]{1,0:T(8,128)(2,1)S(1)} %get-tuple-element.63.refs_2_.cot_ref), channel_id=1, source_target_pairs={{0,2},{1,3},{2,0},{3,1},{4,6},{5,7},{6,4},{7,5},{8,10},{9,11},{10,... | collective-permute-start | bytes 1179656 | tf_op jit(solution)/shard_map/ppermute | solution.py:560
  9.7 10.2 %collective-permute-start.7 = (bf16[2,48,512]{2,1,0:T(8,128)(2,1)S(1)}, bf16[2,48,512]{2,1,0:T(8,128)(2,1)S(1)}, u32[]{:S(2)}, u32[]{:S(2)}) collective-permute-start(bf16[2,48,512]{2,1,0:T(8,128)(2,1)S(1)} %get-tuple-element.66), channel_id=1, source_target_pairs={{0,2},{1,3},{2,0},{3,1},{4,6},{5,7},{6,4},{7,5},{8,10},{9,11},{10,... | collective-permute-start | bytes 294920 | tf_op jit(solution)/shard_map/ppermute | solution.py:560
  11.8 8.2 %collective-permute-start.8 = (bf16[2,48,512]{2,1,0:T(8,128)(2,1)S(1)}, bf16[2,48,512]{2,1,0:T(8,128)(2,1)S(1)}, u32[]{:S(2)}, u32[]{:S(2)}) collective-permute-start(bf16[2,48,512]{2,1,0:T(8,128)(2,1)S(1)} %get-tuple-element.67), channel_id=1, source_target_pairs={{0,3},{1,2},{2,1},{3,0},{4,7},{5,6},{6,5},{7,4},{8,11},{9,10},{10,... | collective-permute-start | bytes 294920 | tf_op jit(solution)/shard_map/ppermute | solution.py:560
  19.8 3.0 %collective-permute-start.6 = (bf16[2,48,512]{2,1,0:T(8,128)(2,1)S(1)}, bf16[2,48,512]{2,1,0:T(8,128)(2,1)S(1)}, u32[]{:S(2)}, u32[]{:S(2)}) collective-permute-start(bf16[2,48,512]{2,1,0:T(8,128)(2,1)S(1)} %get-tuple-element.65), channel_id=1, source_target_pairs={{0,1},{1,0},{2,3},{3,2},{4,5},{5,4},{6,7},{7,6},{8,9},{9,8},{10,11... | collective-permute-start | bytes 294920 | tf_op jit(solution)/shard_map/ppermute | solution.py:560
  20.0 8.3 %collective-permute-start.11 = (bf16[2,96,512]{2,1,0:T(8,128)(2,1)S(1)}, bf16[2,96,512]{2,1,0:T(8,128)(2,1)S(1)}, u32[]{:S(2)}, u32[]{:S(2)}) collective-permute-start(bf16[2,96,512]{2,1,0:T(8,128)(2,1)S(1)} %constant_dynamic-update-slice_fusion.2.refs_7_), channel_id=1, source_target_pairs={{0,8},{1,9},{2,10},{3,11},{8,16},{9,17},{10,18},{11,19},{16,24},{1... | collective-permute-start | bytes 589832 | tf_op jit(solution)/shard_map/ppermute | solution.py:560
  22.9 7.8 %collective-permute-start.12 = (bf16[2,96,512]{2,1,0:T(8,128)(2,1)S(1)}, bf16[2,96,512]{2,1,0:T(8,128)(2,1)S(1)}, u32[]{:S(2)}, u32[]{:S(2)}) collective-permute-start(bf16[2,96,512]{2,1,0:T(8,128)(2,1)S(1)} %constant_dynamic-update-slice_fusion.2.refs_7_), channel_id=1, source_target_pairs={{0,4},{1,5},{2,6},{3,7},{8,0},{9,1},{10,2},{11,3},{16,8},{17,9},{1... | collective-permute-start | bytes 589832 | tf_op jit(solution)/shard_map/ppermute | solution.py:560
  22.9 9.7 %collective-permute-start.9 = (bf16[2,96,512]{2,1,0:T(8,128)(2,1)S(1)}, bf16[2,96,512]{2,1,0:T(8,128)(2,1)S(1)}, u32[]{:S(2)}, u32[]{:S(2)}) collective-permute-start(bf16[2,96,512]{2,1,0:T(8,128)(2,1)S(1)} %constant_dynamic-update-slice_fusion.refs_6_), channel_id=1, source_target_pairs={{0,8},{1,9},{2,10},{3,11},{8,16},{9,17},{10,18},{11,19},{16,24},{1... | collective-permute-start | bytes 589832 | tf_op jit(solution)/shard_map/ppermute | solution.py:560
  25.6 8.9 %collective-permute-start.10 = (bf16[2,96,512]{2,1,0:T(8,128)(2,1)S(1)}, bf16[2,96,512]{2,1,0:T(8,128)(2,1)S(1)}, u32[]{:S(2)}, u32[]{:S(2)}) collective-permute-start(bf16[2,96,512]{2,1,0:T(8,128)(2,1)S(1)} %constant_dynamic-update-slice_fusion.refs_6_), channel_id=1, source_target_pairs={{0,4},{1,5},{2,6},{3,7},{8,0},{9,1},{10,2},{11,3},{16,8},{17,9},{1... | collective-permute-start | bytes 589832 | tf_op jit(solution)/shard_map/ppermute | solution.py:560
  28.3 16.5 %collective-permute-start.21 = (bf16[128,1536]{1,0:T(8,128)(2,1)S(1)}, bf16[128,1536]{1,0:T(8,128)(2,1)S(1)}, u32[]{:S(2)}, u32[]{:S(2)}) collective-permute-start(bf16[128,1536]{1,0:T(8,128)(2,1)S(1)} %get-tuple-element.62.refs_1_), channel_id=1, source_target_pairs={{0,2},{1,3},{2,0},{3,1},{4,6},{5,7},{6,4},{7,5},{8,10},{9,11},{10,... | collective-permute-start | bytes 1179656 | tf_op jit(solution)/shard_map/ppermute | solution.py:560
  30.6 6.4 %collective-permute-start.15 = (bf16[2,96,512]{2,1,0:T(8,128)(2,1)S(1)}, bf16[2,96,512]{2,1,0:T(8,128)(2,1)S(1)}, u32[]{:S(2)}, u32[]{:S(2)}) collective-permute-start(bf16[2,96,512]{2,1,0:T(8,128)(2,1)S(1)} %collective-permute-done.11.refs_10_), channel_id=1, source_target_pairs={{0,8},{1,9},{2,10},{3,11},{8,16},{9,17},{10,18},{11,19},{16,24},{1... | collective-permute-start | bytes 589832 | tf_op jit(solution)/shard_map/ppermute | solution.py:560
  32.5 8.1 %collective-permute-start.16 = (bf16[2,96,512]{2,1,0:T(8,128)(2,1)S(1)}, bf16[2,96,512]{2,1,0:T(8,128)(2,1)S(1)}, u32[]{:S(2)}, u32[]{:S(2)}) collective-permute-start(bf16[2,96,512]{2,1,0:T(8,128)(2,1)S(1)} %collective-permute-done.12.refs_11_), channel_id=1, source_target_pairs={{0,4},{1,5},{2,6},{3,7},{8,0},{9,1},{10,2},{11,3},{16,8},{17,9},{1... | collective-permute-start | bytes 589832 | tf_op jit(solution)/shard_map/ppermute | solution.py:560
  34.6 7.8 %collective-permute-start.13 = (bf16[2,96,512]{2,1,0:T(8,128)(2,1)S(1)}, bf16[2,96,512]{2,1,0:T(8,128)(2,1)S(1)}, u32[]{:S(2)}, u32[]{:S(2)}) collective-permute-start(bf16[2,96,512]{2,1,0:T(8,128)(2,1)S(1)} %collective-permute-done.9.refs_8_), channel_id=1, source_target_pairs={{0,8},{1,9},{2,10},{3,11},{8,16},{9,17},{10,18},{11,19},{16,24},{1... | collective-permute-start | bytes 589832 | tf_op jit(solution)/shard_map/ppermute | solution.py:560
  35.3 9.5 %collective-permute-start.14 = (bf16[2,96,512]{2,1,0:T(8,128)(2,1)S(1)}, bf16[2,96,512]{2,1,0:T(8,128)(2,1)S(1)}, u32[]{:S(2)}, u32[]{:S(2)}) collective-permute-start(bf16[2,96,512]{2,1,0:T(8,128)(2,1)S(1)} %collective-permute-done.10.refs_9_), channel_id=1, source_target_pairs={{0,4},{1,5},{2,6},{3,7},{8,0},{9,1},{10,2},{11,3},{16,8},{17,9},{1... | collective-permute-start | bytes 589832 | tf_op jit(solution)/shard_map/ppermute | solution.py:560
  37.1 9.5 %collective-permute-start.19 = (bf16[2,96,512]{2,1,0:T(8,128)(2,1)S(1)}, bf16[2,96,512]{2,1,0:T(8,128)(2,1)S(1)}, u32[]{:S(2)}, u32[]{:S(2)}) collective-permute-start(bf16[2,96,512]{2,1,0:T(8,128)(2,1)S(1)} %collective-permute-done.15.refs_14_), channel_id=1, source_target_pairs={{0,8},{1,9},{2,10},{3,11},{8,16},{9,17},{10,18},{11,19},{16,24},{1... | collective-permute-start | bytes 589832 | tf_op jit(solution)/shard_map/ppermute | solution.py:560
  40.6 6.5 %collective-permute-start.20 = (bf16[2,96,512]{2,1,0:T(8,128)(2,1)S(1)}, bf16[2,96,512]{2,1,0:T(8,128)(2,1)S(1)}, u32[]{:S(2)}, u32[]{:S(2)}) collective-permute-start(bf16[2,96,512]{2,1,0:T(8,128)(2,1)S(1)} %collective-permute-done.16.refs_15_), channel_id=1, source_target_pairs={{0,4},{1,5},{2,6},{3,7},{8,0},{9,1},{10,2},{11,3},{16,8},{17,9},{1... | collective-permute-start | bytes 589832 | tf_op jit(solution)/shard_map/ppermute | solution.py:560
  42.3 6.6 %collective-permute-start.17 = (bf16[2,96,512]{2,1,0:T(8,128)(2,1)S(1)}, bf16[2,96,512]{2,1,0:T(8,128)(2,1)S(1)}, u32[]{:S(2)}, u32[]{:S(2)}) collective-permute-start(bf16[2,96,512]{2,1,0:T(8,128)(2,1)S(1)} %collective-permute-done.13.refs_12_), channel_id=1, source_target_pairs={{0,8},{1,9},{2,10},{3,11},{8,16},{9,17},{10,18},{11,19},{16,24},{1... | collective-permute-start | bytes 589832 | tf_op jit(solution)/shard_map/ppermute | solution.py:560
  44.8 11.7 %collective-permute-start.3 = (bf16[128,1536]{1,0:T(8,128)(2,1)S(1)}, bf16[128,1536]{1,0:T(8,128)(2,1)S(1)}, u32[]{:S(2)}, u32[]{:S(2)}) collective-permute-start(bf16[128,1536]{1,0:T(8,128)(2,1)S(1)} %get-tuple-element.63.refs_2_.cot_ref), channel_id=1, source_target_pairs={{0,1},{1,0},{2,3},{3,2},{4,5},{5,4},{6,7},{7,6},{8,9},{9,8},{10,11... | collective-permute-start | bytes 1179656 | tf_op jit(solution)/shard_map/ppermute | solution.py:560
  44.8 12.0 %collective-permute-start.2 = (bf16[128,1536]{1,0:T(8,128)(2,1)S(1)}, bf16[128,1536]{1,0:T(8,128)(2,1)S(1)}, u32[]{:S(2)}, u32[]{:S(2)}) collective-permute-start(bf16[128,1536]{1,0:T(8,128)(2,1)S(1)} %get-tuple-element.62.refs_1_), channel_id=1, source_target_pairs={{0,1},{1,0},{2,3},{3,2},{4,5},{5,4},{6,7},{7,6},{8,9},{9,8},{10,11... | collective-permute-start | bytes 1179656 | tf_op jit(solution)/shard_map/ppermute | solution.py:560
  46.6 12.1 %collective-permute-start.5 = (bf16[128,1536]{1,0:T(8,128)(2,1)S(1)}, bf16[128,1536]{1,0:T(8,128)(2,1)S(1)}, u32[]{:S(2)}, u32[]{:S(2)}) collective-permute-start(bf16[128,1536]{1,0:T(8,128)(2,1)S(1)} %collective-permute-done.4.refs_4_), channel_id=1, source_target_pairs={{0,1},{1,0},{2,3},{3,2},{4,5},{5,4},{6,7},{7,6},{8,9},{9,8},{10,11... | collective-permute-start | bytes 1179656 | tf_op jit(solution)/shard_map/ppermute | solution.py:560
  47.1 13.7 %collective-permute-start.22 = (bf16[128,1536]{1,0:T(8,128)(2,1)S(1)}, bf16[128,1536]{1,0:T(8,128)(2,1)S(1)}, u32[]{:S(2)}, u32[]{:S(2)}) collective-permute-start(bf16[128,1536]{1,0:T(8,128)(2,1)S(1)} %collective-permute-done.21.refs_1_.far_ref), channel_id=1, source_target_pairs={{0,1},{1,0},{2,3},{3,2},{4,5},{5,4},{6,7},{7,6},{8,9},{9,8},{10,11... | collective-permute-start | bytes 1179656 | tf_op jit(solution)/shard_map/ppermute | solution.py:560
  49.0 5.7 %collective-permute-start.18 = (bf16[2,96,512]{2,1,0:T(8,128)(2,1)S(1)}, bf16[2,96,512]{2,1,0:T(8,128)(2,1)S(1)}, u32[]{:S(2)}, u32[]{:S(2)}) collective-permute-start(bf16[2,96,512]{2,1,0:T(8,128)(2,1)S(1)} %collective-permute-done.14.refs_13_), channel_id=1, source_target_pairs={{0,4},{1,5},{2,6},{3,7},{8,0},{9,1},{10,2},{11,3},{16,8},{17,9},{1... | collective-permute-start | bytes 589832 | tf_op jit(solution)/shard_map/ppermute | solution.py:560
  54.7 6.8 %collective-permute-start.25 = (bf16[1,96,512]{2,1,0:T(8,128)(2,1)S(1)}, bf16[1,96,512]{2,1,0:T(8,128)(2,1)S(1)}, u32[]{:S(2)}, u32[]{:S(2)}) collective-permute-start(bf16[1,96,512]{2,1,0:T(8,128)(2,1)S(1)} %slice.18), channel_id=1, source_target_pairs={{0,8},{1,9},{2,10},{3,11},{8,16},{9,17},{10,18},{11,19},{16,24},{1... | collective-permute-start | bytes 294920 | tf_op jit(solution)/shard_map/ppermute | solution.py:560
  56.5 5.0 %collective-permute-start.26 = (bf16[1,96,512]{2,1,0:T(8,128)(2,1)S(1)}, bf16[1,96,512]{2,1,0:T(8,128)(2,1)S(1)}, u32[]{:S(2)}, u32[]{:S(2)}) collective-permute-start(bf16[1,96,512]{2,1,0:T(8,128)(2,1)S(1)} %slice.19), channel_id=1, source_target_pairs={{0,4},{1,5},{2,6},{3,7},{8,0},{9,1},{10,2},{11,3},{16,8},{17,9},{1... | collective-permute-start | bytes 294920 | tf_op jit(solution)/shard_map/ppermute | solution.py:560
  56.8 4.8 %collective-permute-start.23 = (bf16[1,96,512]{2,1,0:T(8,128)(2,1)S(1)}, bf16[1,96,512]{2,1,0:T(8,128)(2,1)S(1)}, u32[]{:S(2)}, u32[]{:S(2)}) collective-permute-start(bf16[1,96,512]{2,1,0:T(8,128)(2,1)S(1)} %slice.16), channel_id=1, source_target_pairs={{0,8},{1,9},{2,10},{3,11},{8,16},{9,17},{10,18},{11,19},{16,24},{1... | collective-permute-start | bytes 294920 | tf_op jit(solution)/shard_map/ppermute | solution.py:560
  58.6 4.6 %collective-permute-start.24 = (bf16[1,96,512]{2,1,0:T(8,128)(2,1)S(1)}, bf16[1,96,512]{2,1,0:T(8,128)(2,1)S(1)}, u32[]{:S(2)}, u32[]{:S(2)}) collective-permute-start(bf16[1,96,512]{2,1,0:T(8,128)(2,1)S(1)} %slice.17), channel_id=1, source_target_pairs={{0,4},{1,5},{2,6},{3,7},{8,0},{9,1},{10,2},{11,3},{16,8},{17,9},{1... | collective-permute-start | bytes 294920 | tf_op jit(solution)/shard_map/ppermute | solution.py:560
  65.1 13.9 %collective-permute-start.27 = (bf16[128,1536]{1,0:T(8,128)(2,1)S(1)}, bf16[128,1536]{1,0:T(8,128)(2,1)S(1)}, u32[]{:S(2)}, u32[]{:S(2)}) collective-permute-start(bf16[128,1536]{1,0:T(8,128)(2,1)S(1)} %get-tuple-element.79), channel_id=1, source_target_pairs={{0,1},{1,0},{2,3},{3,2},{4,5},{5,4},{6,7},{7,6},{8,9},{9,8},{10,11... | collective-permute-start | bytes 1179656 | tf_op jit(solution)/shard_map/ppermute | solution.py:560
  66.4 17.4 %collective-permute-start.29 = (bf16[128,1536]{1,0:T(8,128)(2,1)S(1)}, bf16[128,1536]{1,0:T(8,128)(2,1)S(1)}, u32[]{:S(2)}, u32[]{:S(2)}) collective-permute-start(bf16[128,1536]{1,0:T(8,128)(2,1)S(1)} %shard_map.138), channel_id=1, source_target_pairs={{0,2},{1,3},{2,0},{3,1},{4,6},{5,7},{6,4},{7,5},{8,10},{9,11},{10,... | collective-permute-start | bytes 1179656 | tf_op jit(solution)/shard_map/ppermute | solution.py:560
  67.5 10.4 %collective-permute-start.32 = (bf16[2,32,128]{2,1,0:T(8,128)(2,1)S(1)}, bf16[2,32,128]{2,1,0:T(8,128)(2,1)S(1)}, u32[]{:S(2)}, u32[]{:S(2)}) collective-permute-start(bf16[2,32,128]{2,1,0:T(8,128)(2,1)S(1)} %get-tuple-element.88), channel_id=1, source_target_pairs={{0,2},{1,3},{2,0},{3,1},{4,6},{5,7},{6,4},{7,5},{8,10},{9,11},{10,... | collective-permute-start | bytes 49160 | tf_op jit(solution)/shard_map/ppermute | solution.py:560
  78.7 7.0 %collective-permute-start.33 = (bf16[32,1536]{1,0:T(8,128)(2,1)S(1)}, bf16[32,1536]{1,0:T(8,128)(2,1)S(1)}, u32[]{:S(2)}, u32[]{:S(2)}) collective-permute-start(bf16[32,1536]{1,0:T(8,128)(2,1)S(1)} %shard_map.141), channel_id=1, source_target_pairs={{2,31},{3,2},{0,1},{1,4},{6,3},{7,6},{4,5},{5,8},{10,7},{11,10},{8... | collective-permute-start | bytes 294920 | tf_op jit(solution)/shard_map/ppermute | solution.py:560
  79.9 7.8 %collective-permute-start.31 = (bf16[32,1536]{1,0:T(8,128)(2,1)S(1)}, bf16[32,1536]{1,0:T(8,128)(2,1)S(1)}, u32[]{:S(2)}, u32[]{:S(2)}) collective-permute-start(bf16[32,1536]{1,0:T(8,128)(2,1)S(1)} %get-tuple-element.87), channel_id=1, source_target_pairs={{0,31},{1,2},{2,1},{3,4},{4,3},{5,6},{6,5},{7,8},{8,7},{9,10},{10,... | collective-permute-start | bytes 294920 | tf_op jit(solution)/shard_map/ppermute | solution.py:560
  (2 other events, 5.2 us)

commit v4 on v3

--- a/solution.py
+++ b/solution.py
@@ -162,6 +162,16 @@
     later = pltpu.roll(values, width - half, 1)
     earlier = pltpu.roll(values, half, 1)
     return jnp.where(iota(values.shape, 1) % CH < half, -later, earlier)
+
+
+def stacked(values):
+    width = values.shape[1]
+    return jnp.concatenate([values[:, at : at + BLOCK] for at in range(0, width, BLOCK)], axis=0)
+
+
+def unstacked(values, rows):
+    count = values.shape[0]
+    return jnp.concatenate([values[at : at + rows] for at in range(0, count, rows)], axis=1)
 
 
 def call(body, outs, args, scratch=(), raw=(), aliases=()):
@@ -289,18 +299,14 @@
     if rest:
         ext[columns + 2 * border :] = jnp.zeros((rest, width), jnp.bfloat16)
     source = ext[...]
-    over = ((0,), (0,))
-    gathered = mm(mix_ref[0], source, over) + turn(mm(mix_ref[1], source, over))
-    gathered = gathered.astype(jnp.bfloat16)
-    square = jnp.zeros((columns, BLOCK), jnp.float32)
-    for b in range(width // BLOCK):
-        at = slice(b * BLOCK, (b + 1) * BLOCK)
-        x = x_ref[:, at]
-        out = x.astype(jnp.float32) + (mm(gathered[:, at], form_ref[0]) + mm(x, form_ref[1]))
-        out = out.astype(jnp.bfloat16)
-        conv_ref[:, at] = out
-        out = out.astype(jnp.float32)
-        square = square + out * out
+    gathered = mm(jnp.concatenate([mix_ref[0], mix_ref[1]], axis=1), source, ((0,), (0,)))
+    gathered = (gathered[:columns] + turn(gathered[columns:])).astype(jnp.bfloat16)
+    x = x_ref[...]
+    folded = mm(stacked(gathered), form_ref[0]) + mm(stacked(x), form_ref[1])
+    out = (x.astype(jnp.float32) + unstacked(folded, columns)).astype(jnp.bfloat16)
+    conv_ref[...] = out
+    out = out.astype(jnp.float32)
+    square = out * out
     scale = lax.rsqrt(jnp.sum(square, axis=1, keepdims=True) / width + 1e-05)
     norm_ref[...] = (conv_ref[...].astype(jnp.float32) * scale * gain_ref[...]).astype(jnp.bfloat16)
     scale_ref[...] = jnp.broadcast_to(scale, scale_ref.shape)
@@ -413,14 +419,10 @@
     mine_ref[...] = rows[columns:]
 
 
-def shifted_back(mix, form, grads):
-    spread = mm(mix[0], grads) - turn(mm(mix[1], grads))
-    spread = spread.astype(jnp.bfloat16)
-    width = grads.shape[1]
-    return [
-        mm(spread[:, b * BLOCK : (b + 1) * BLOCK], form, ((1,), (1,)))
-        for b in range(width // BLOCK)
-    ]
+def shifted_back(mix, grads):
+    rows = mix[0].shape[0]
+    spread = mm(jnp.concatenate(mix, axis=0), grads)
+    return (spread[:rows] - turn(spread[rows:])).astype(jnp.bfloat16)
 
 
 def join_body(cross_ref, part_ref, out_ref):
@@ -434,8 +436,8 @@
 
 
 def put_back(target, mix, form, grads):
-    for b, rows in enumerate(shifted_back(mix, form, grads)):
-        target[:, b * BLOCK : (b + 1) * BLOCK] = rows.astype(jnp.bfloat16)
+    rows = mm(stacked(shifted_back(mix, grads)), form, ((1,), (1,))).astype(jnp.bfloat16)
+    target[...] = unstacked(rows, target.shape[0])
 
 
 def other_body(cross_ref, part_ref, far_ref, gain_ref, edge_ref, form_ref, out_ref):
@@ -476,14 +478,12 @@
 
 
 def own_body(grad_ref, mix_ref, form_ref, local_ref):
-    columns, _ = grad_ref.shape
+    columns = grad_ref.shape[0]
     grads = grad_ref[...]
-    mix = [mix_ref[i, :columns] for i in range(2)]
-    for b, rows in enumerate(shifted_back(mix, form_ref[0], grads)):
-        at = slice(b * BLOCK, (b + 1) * BLOCK)
-        own = grads[:, at]
-        rows = rows + mm(own, form_ref[1], ((1,), (1,)))
-        local_ref[:, at] = own.astype(jnp.float32) + rows
+    spread = shifted_back([mix_ref[i, :columns] for i in range(2)], grads)
+    across = ((1,), (1,))
+    rows = mm(stacked(spread), form_ref[0], across) + mm(stacked(grads), form_ref[1], across)
+    local_ref[...] = grads.astype(jnp.float32) + unstacked(rows, columns)
 
 
 def last_body(local_ref, inner_ref, outer_ref, other_ref, bound_ref, out_ref, held, sem):

time: 89.2 us -> 88.6 us (level)
  transfers between devices with their start and end apart: 34 -> 34, of which waited for: 15 -> 16; matrix products, arithmetic and copies ran while one was open for 0% -> 0% of each run, Pallas kernels for 12% -> 11%
where the time goes in v4:
time: 88.6 us; the launch traced here: 88.4 us
  starting transfers between devices  39.5 us (45%)
  waiting for transfers between devices  35 us (40%)
  Pallas kernels  13.6 us (15%)
    ppermute x34, starting transfers between devices, permute(): return lax.ppermute(value, 'patch', pairs)  39.5 us
    ppermute x34, waiting for transfers between devices, permute(): return lax.ppermute(value, 'patch', pairs)  35 us
    pallas_call x15, Pallas kernels, call(): pl.pallas_call(body, out_shape=outs, in_specs=specs, out_specs=jax.tree.m...  12.5 us
  transfers between devices with their start and end apart: 34, of which 16 were waited for; matrix products, arithmetic and copies ran while one was open for 0% of the time, Pallas kernels for 11%

profile of v4, /device:TPU:0, one launch (start us, length us, event | category | flops | bytes accessed | tf_op | source)
XLA Modules:
  0.0 88.4 jit_solution(12766991693411129221)
XLA Ops:
  0.0 1.2 %shard_map.127 = (bf16[128,1536]{1,0:T(8,128)(2,1)S(1)}, bf16[128,1536]{1,0:T(8,128)(2,1)S(1)}, s32[1,64]{1,0:T(1,128)S(1)}, s32[6,128]{1,0:T(8,128)S(1)}, s32[6...) custom-call(bf16[128,1536]{1,0:T(8,128)(2,1)} %bitcast.7, ...), custom_call_target="tpu_custom_call" | custom-call | tf_op jit(solution)/shard_map/pallas_call | solution.py:184
  2.0 6.6 %collective-permute-start.1 = (bf16[32,1536]{1,0:T(8,128)(2,1)S(1)}, bf16[32,1536]{1,0:T(8,128)(2,1)S(1)}, u32[]{:S(2)}, u32[]{:S(2)}) collective-permute-start(bf16[32,1536]{1,0:T(8,128)(2,1)S(1)} %get-tuple-element.50), channel_id=1, source_target_pairs={{0,31},{1,2},{2,1},{3,4},{4,3},{5,6},{6,5},{7,8},{8,7},{9,10},{10,... | collective-permute-start | bytes 294920 | tf_op jit(solution)/shard_map/ppermute | solution.py:560
  8.6 1.0 %shard_map.131 = (bf16[2,48,512]{2,1,0:T(8,128)(2,1)S(1)}, bf16[2,48,512]{2,1,0:T(8,128)(2,1)S(1)}, bf16[2,48,512]{2,1,0:T(8,128)(2,1)S(1)}, bf16[2,48,512]{2,1,0:T(8,128)(2,1)S(1)}) custom-call(bf16[48,2048]{1,0:T(8,128)(2,1)} %up_ref.1, bf16[48,2048]{1,0:T(8,128)(2,1)} %down_ref.1), custom_call_target="tpu_custom_call" | custom-call | tf_op jit(solution)/shard_map/pallas_call | solution.py:184
  9.7 2.1 %collective-permute-start.7 = (bf16[2,48,512]{2,1,0:T(8,128)(2,1)S(1)}, bf16[2,48,512]{2,1,0:T(8,128)(2,1)S(1)}, u32[]{:S(2)}, u32[]{:S(2)}) collective-permute-start(bf16[2,48,512]{2,1,0:T(8,128)(2,1)S(1)} %get-tuple-element.66), channel_id=1, source_target_pairs={{0,2},{1,3},{2,0},{3,1},{4,6},{5,7},{6,4},{7,5},{8,10},{9,11},{10,... | collective-permute-start | bytes 294920 | tf_op jit(solution)/shard_map/ppermute | solution.py:560
  11.8 8.1 %collective-permute-done.7 = bf16[2,48,512]{2,1,0:T(8,128)(2,1)S(1)} collective-permute-done((bf16[2,48,512]{2,1,0:T(8,128)(2,1)S(1)}, bf16[2,48,512]{2,1,0:T(8,128)(2,1)S(1)}, u32[]{:S(2)}, u32[]{:S(2)}) %collective-permute-start.7) | collective-permute-done | bytes 98336 | tf_op jit(solution)/shard_map/ppermute | solution.py:560
  20.0 2.8 %collective-permute-start.11 = (bf16[2,96,512]{2,1,0:T(8,128)(2,1)S(1)}, bf16[2,96,512]{2,1,0:T(8,128)(2,1)S(1)}, u32[]{:S(2)}, u32[]{:S(2)}) collective-permute-start(bf16[2,96,512]{2,1,0:T(8,128)(2,1)S(1)} %constant_dynamic-update-slice_fusion.2.refs_7_), channel_id=1, source_target_pairs={{0,8},{1,9},{2,10},{3,11},{8,16},{9,17},{10,18},{11,19},{16,24},{1... | collective-permute-start | bytes 589832 | tf_op jit(solution)/shard_map/ppermute | solution.py:560
  22.9 2.1 %collective-permute-start.9 = (bf16[2,96,512]{2,1,0:T(8,128)(2,1)S(1)}, bf16[2,96,512]{2,1,0:T(8,128)(2,1)S(1)}, u32[]{:S(2)}, u32[]{:S(2)}) collective-permute-start(bf16[2,96,512]{2,1,0:T(8,128)(2,1)S(1)} %constant_dynamic-update-slice_fusion.refs_6_), channel_id=1, source_target_pairs={{0,8},{1,9},{2,10},{3,11},{8,16},{9,17},{10,18},{11,19},{16,24},{1... | collective-permute-start | bytes 589832 | tf_op jit(solution)/shard_map/ppermute | solution.py:560
  25.7 1.1 %shard_map.130 = (bf16[128,1536]{1,0:T(8,128)(2,1)S(1)}, bf16[128,1536]{1,0:T(8,128)(2,1)S(1)}, bf16[2,32,128]{2,1,0:T(8,128)(2,1)S(1)}, f32[128,128]{1,0:T(8,128)S(1)}) custom-call(bf16[128,1536]{1,0:T(8,128)(2,1)S(1)} %get-tuple-element.47.x_ref, bf16[32,1536]{1,0:T(8,128)(2,1)S(1)} %collective-permute-done.inner_ref, ...), custom_call_target="tpu_custom_call" | custom-call | tf_op jit(solution)/shard_map/pallas_call | solution.py:184
  26.8 1.6 %collective-permute-done.11.refs_10_ = bf16[2,96,512]{2,1,0:T(8,128)(2,1)S(1)} collective-permute-done((bf16[2,96,512]{2,1,0:T(8,128)(2,1)S(1)}, bf16[2,96,512]{2,1,0:T(8,128)(2,1)S(1)}, u32[]{:S(2)}, u32[]{:S(2)}) %collective-permute-start.11) | collective-permute-done | bytes 196640 | tf_op jit(solution)/shard_map/ppermute | solution.py:560
  29.3 1.3 %collective-permute-done.12.refs_11_ = bf16[2,96,512]{2,1,0:T(8,128)(2,1)S(1)} collective-permute-done((bf16[2,96,512]{2,1,0:T(8,128)(2,1)S(1)}, bf16[2,96,512]{2,1,0:T(8,128)(2,1)S(1)}, u32[]{:S(2)}, u32[]{:S(2)}) %collective-permute-start.12) | collective-permute-done | bytes 196640 | tf_op jit(solution)/shard_map/ppermute | solution.py:560
  30.6 1.6 %collective-permute-start.15 = (bf16[2,96,512]{2,1,0:T(8,128)(2,1)S(1)}, bf16[2,96,512]{2,1,0:T(8,128)(2,1)S(1)}, u32[]{:S(2)}, u32[]{:S(2)}) collective-permute-start(bf16[2,96,512]{2,1,0:T(8,128)(2,1)S(1)} %collective-permute-done.11.refs_10_), channel_id=1, source_target_pairs={{0,8},{1,9},{2,10},{3,11},{8,16},{9,17},{10,18},{11,19},{16,24},{1... | collective-permute-start | bytes 589832 | tf_op jit(solution)/shard_map/ppermute | solution.py:560
  32.5 2.0 %collective-permute-start.16 = (bf16[2,96,512]{2,1,0:T(8,128)(2,1)S(1)}, bf16[2,96,512]{2,1,0:T(8,128)(2,1)S(1)}, u32[]{:S(2)}, u32[]{:S(2)}) collective-permute-start(bf16[2,96,512]{2,1,0:T(8,128)(2,1)S(1)} %collective-permute-done.12.refs_11_), channel_id=1, source_target_pairs={{0,4},{1,5},{2,6},{3,7},{8,0},{9,1},{10,2},{11,3},{16,8},{17,9},{1... | collective-permute-start | bytes 589832 | tf_op jit(solution)/shard_map/ppermute | solution.py:560
  35.3 1.3 %collective-permute-start.14 = (bf16[2,96,512]{2,1,0:T(8,128)(2,1)S(1)}, bf16[2,96,512]{2,1,0:T(8,128)(2,1)S(1)}, u32[]{:S(2)}, u32[]{:S(2)}) collective-permute-start(bf16[2,96,512]{2,1,0:T(8,128)(2,1)S(1)} %collective-permute-done.10.refs_9_), channel_id=1, source_target_pairs={{0,4},{1,5},{2,6},{3,7},{8,0},{9,1},{10,2},{11,3},{16,8},{17,9},{1... | collective-permute-start | bytes 589832 | tf_op jit(solution)/shard_map/ppermute | solution.py:560
  37.1 2.5 %collective-permute-start.19 = (bf16[2,96,512]{2,1,0:T(8,128)(2,1)S(1)}, bf16[2,96,512]{2,1,0:T(8,128)(2,1)S(1)}, u32[]{:S(2)}, u32[]{:S(2)}) collective-permute-start(bf16[2,96,512]{2,1,0:T(8,128)(2,1)S(1)} %collective-permute-done.15.refs_14_), channel_id=1, source_target_pairs={{0,8},{1,9},{2,10},{3,11},{8,16},{9,17},{10,18},{11,19},{16,24},{1... | collective-permute-start | bytes 589832 | tf_op jit(solution)/shard_map/ppermute | solution.py:560
  39.5 1.0 %collective-permute-done.16.refs_15_ = bf16[2,96,512]{2,1,0:T(8,128)(2,1)S(1)} collective-permute-done((bf16[2,96,512]{2,1,0:T(8,128)(2,1)S(1)}, bf16[2,96,512]{2,1,0:T(8,128)(2,1)S(1)}, u32[]{:S(2)}, u32[]{:S(2)}) %collective-permute-start.16) | collective-permute-done | bytes 196640 | tf_op jit(solution)/shard_map/ppermute | solution.py:560
  40.6 1.7 %collective-permute-start.20 = (bf16[2,96,512]{2,1,0:T(8,128)(2,1)S(1)}, bf16[2,96,512]{2,1,0:T(8,128)(2,1)S(1)}, u32[]{:S(2)}, u32[]{:S(2)}) collective-permute-start(bf16[2,96,512]{2,1,0:T(8,128)(2,1)S(1)} %collective-permute-done.16.refs_15_), channel_id=1, source_target_pairs={{0,4},{1,5},{2,6},{3,7},{8,0},{9,1},{10,2},{11,3},{16,8},{17,9},{1... | collective-permute-start | bytes 589832 | tf_op jit(solution)/shard_map/ppermute | solution.py:560
  42.3 1.4 %collective-permute-start.17 = (bf16[2,96,512]{2,1,0:T(8,128)(2,1)S(1)}, bf16[2,96,512]{2,1,0:T(8,128)(2,1)S(1)}, u32[]{:S(2)}, u32[]{:S(2)}) collective-permute-start(bf16[2,96,512]{2,1,0:T(8,128)(2,1)S(1)} %collective-permute-done.13.refs_12_), channel_id=1, source_target_pairs={{0,8},{1,9},{2,10},{3,11},{8,16},{9,17},{10,18},{11,19},{16,24},{1... | collective-permute-start | bytes 589832 | tf_op jit(solution)/shard_map/ppermute | solution.py:560
  43.8 1.0 %collective-permute-done.14.refs_13_ = bf16[2,96,512]{2,1,0:T(8,128)(2,1)S(1)} collective-permute-done((bf16[2,96,512]{2,1,0:T(8,128)(2,1)S(1)}, bf16[2,96,512]{2,1,0:T(8,128)(2,1)S(1)}, u32[]{:S(2)}, u32[]{:S(2)}) %collective-permute-start.14) | collective-permute-done | bytes 196640 | tf_op jit(solution)/shard_map/ppermute | solution.py:560
  45.3 1.2 %collective-permute-done.19.refs_18_ = bf16[2,96,512]{2,1,0:T(8,128)(2,1)S(1)} collective-permute-done((bf16[2,96,512]{2,1,0:T(8,128)(2,1)S(1)}, bf16[2,96,512]{2,1,0:T(8,128)(2,1)S(1)}, u32[]{:S(2)}, u32[]{:S(2)}) %collective-permute-start.19) | collective-permute-done | bytes 196640 | tf_op jit(solution)/shard_map/ppermute | solution.py:560
  47.1 1.9 %collective-permute-done.17.refs_16_ = bf16[2,96,512]{2,1,0:T(8,128)(2,1)S(1)} collective-permute-done((bf16[2,96,512]{2,1,0:T(8,128)(2,1)S(1)}, bf16[2,96,512]{2,1,0:T(8,128)(2,1)S(1)}, u32[]{:S(2)}, u32[]{:S(2)}) %collective-permute-start.17) | collective-permute-done | bytes 196640 | tf_op jit(solution)/shard_map/ppermute | solution.py:560
  49.0 1.7 %collective-permute-start.18 = (bf16[2,96,512]{2,1,0:T(8,128)(2,1)S(1)}, bf16[2,96,512]{2,1,0:T(8,128)(2,1)S(1)}, u32[]{:S(2)}, u32[]{:S(2)}) collective-permute-start(bf16[2,96,512]{2,1,0:T(8,128)(2,1)S(1)} %collective-permute-done.14.refs_13_), channel_id=1, source_target_pairs={{0,4},{1,5},{2,6},{3,7},{8,0},{9,1},{10,2},{11,3},{16,8},{17,9},{1... | collective-permute-start | bytes 589832 | tf_op jit(solution)/shard_map/ppermute | solution.py:560
  50.8 3.9 %collective-permute-done.18.refs_17_ = bf16[2,96,512]{2,1,0:T(8,128)(2,1)S(1)} collective-permute-done((bf16[2,96,512]{2,1,0:T(8,128)(2,1)S(1)}, bf16[2,96,512]{2,1,0:T(8,128)(2,1)S(1)}, u32[]{:S(2)}, u32[]{:S(2)}) %collective-permute-start.18) | collective-permute-done | bytes 196640 | tf_op jit(solution)/shard_map/ppermute | solution.py:560
  54.7 1.8 %collective-permute-start.25 = (bf16[1,96,512]{2,1,0:T(8,128)(2,1)S(1)}, bf16[1,96,512]{2,1,0:T(8,128)(2,1)S(1)}, u32[]{:S(2)}, u32[]{:S(2)}) collective-permute-start(bf16[1,96,512]{2,1,0:T(8,128)(2,1)S(1)} %slice.18), channel_id=1, source_target_pairs={{0,8},{1,9},{2,10},{3,11},{8,16},{9,17},{10,18},{11,19},{16,24},{1... | collective-permute-start | bytes 294920 | tf_op jit(solution)/shard_map/ppermute | solution.py:560
  56.8 1.8 %collective-permute-start.23 = (bf16[1,96,512]{2,1,0:T(8,128)(2,1)S(1)}, bf16[1,96,512]{2,1,0:T(8,128)(2,1)S(1)}, u32[]{:S(2)}, u32[]{:S(2)}) collective-permute-start(bf16[1,96,512]{2,1,0:T(8,128)(2,1)S(1)} %slice.16), channel_id=1, source_target_pairs={{0,8},{1,9},{2,10},{3,11},{8,16},{9,17},{10,18},{11,19},{16,24},{1... | collective-permute-start | bytes 294920 | tf_op jit(solution)/shard_map/ppermute | solution.py:560
  58.8 1.9 %shard_map.132 = (bf16[1536,512]{1,0:T(8,128)(2,1)S(1)}, f32[256,512]{1,0:T(8,128)S(1)}, f32[512,512]{1,0:T(8,128)S(1)}, bf16[256,192]{1,0:T(8,128)(2,1)S(1)}, bf16[512,192]{1,0:T(8,128)(2,1)S(1)}) custom-call(bf16[128,1536]{1,0:T(8,128)(2,1)S(1)} %collective-permute-done.2.refs_0_, bf16[128,1536]{1,0:T(8,128)(2,1)S(1)} %get-tuple-element.62.refs_1_, ...), custom_call_target="tpu_custom_call" | custom-call | tf_op jit(solution)/shard_map/pallas_call | solution.py:184
  61.6 1.7 %collective-permute-done.24.refs_6_ = bf16[1,96,512]{2,1,0:T(8,128)(2,1)S(1)} collective-permute-done((bf16[1,96,512]{2,1,0:T(8,128)(2,1)S(1)}, bf16[1,96,512]{2,1,0:T(8,128)(2,1)S(1)}, u32[]{:S(2)}, u32[]{:S(2)}) %collective-permute-start.24) | collective-permute-done | bytes 98336 | tf_op jit(solution)/shard_map/ppermute | solution.py:560
  66.4 1.1 %collective-permute-start.29 = (bf16[128,1536]{1,0:T(8,128)(2,1)S(1)}, bf16[128,1536]{1,0:T(8,128)(2,1)S(1)}, u32[]{:S(2)}, u32[]{:S(2)}) collective-permute-start(bf16[128,1536]{1,0:T(8,128)(2,1)S(1)} %shard_map.138), channel_id=1, source_target_pairs={{0,2},{1,3},{2,0},{3,1},{4,6},{5,7},{6,4},{7,5},{8,10},{9,11},{10,... | collective-permute-start | bytes 1179656 | tf_op jit(solution)/shard_map/ppermute | solution.py:560
  67.5 1.0 %collective-permute-start.32 = (bf16[2,32,128]{2,1,0:T(8,128)(2,1)S(1)}, bf16[2,32,128]{2,1,0:T(8,128)(2,1)S(1)}, u32[]{:S(2)}, u32[]{:S(2)}) collective-permute-start(bf16[2,32,128]{2,1,0:T(8,128)(2,1)S(1)} %get-tuple-element.88), channel_id=1, source_target_pairs={{0,2},{1,3},{2,0},{3,1},{4,6},{5,7},{6,4},{7,5},{8,10},{9,11},{10,... | collective-permute-start | bytes 49160 | tf_op jit(solution)/shard_map/ppermute | solution.py:560
  68.5 9.4 %collective-permute-done.32.edge_ref = bf16[2,32,128]{2,1,0:T(8,128)(2,1)S(1)} collective-permute-done((bf16[2,32,128]{2,1,0:T(8,128)(2,1)S(1)}, bf16[2,32,128]{2,1,0:T(8,128)(2,1)S(1)}, u32[]{:S(2)}, u32[]{:S(2)}) %collective-permute-start.32) | collective-permute-done | bytes 16416 | tf_op jit(solution)/shard_map/ppermute | solution.py:560
  79.5 3.8 %collective-permute-start.31 = (bf16[32,1536]{1,0:T(8,128)(2,1)S(1)}, bf16[32,1536]{1,0:T(8,128)(2,1)S(1)}, u32[]{:S(2)}, u32[]{:S(2)}) collective-permute-start(bf16[32,1536]{1,0:T(8,128)(2,1)S(1)} %get-tuple-element.87), channel_id=1, source_target_pairs={{0,31},{1,2},{2,1},{3,4},{4,3},{5,6},{6,5},{7,8},{8,7},{9,10},{10,... | collective-permute-start | bytes 294920 | tf_op jit(solution)/shard_map/ppermute | solution.py:560
  85.4 1.9 %collective-permute-done.31.outer_ref = bf16[32,1536]{1,0:T(8,128)(2,1)S(1)} collective-permute-done((bf16[32,1536]{1,0:T(8,128)(2,1)S(1)}, bf16[32,1536]{1,0:T(8,128)(2,1)S(1)}, u32[]{:S(2)}, u32[]{:S(2)}) %collective-permute-start.31) | collective-permute-done | bytes 98336 | tf_op jit(solution)/shard_map/ppermute | solution.py:560
  87.3 1.1 %shard_map.142 = bf16[128,1536]{1,0:T(8,128)(2,1)} custom-call(f32[128,1536]{1,0:T(8,128)S(1)} %shard_map.140.local_ref, bf16[32,1536]{1,0:T(8,128)(2,1)S(1)} %collective-permute-done.30.inner_ref, bf16[32,1536]{1,0:T(8,128)(2,1)S(1)} %collective-permute-done.31.outer_ref, bf16[32,1536]{1,0:T(8,128)(2,1)S(1)} %collective-permute-done.33.other_ref, ...), custom_call_target="tpu_custom_call" | custom-call | tf_op jit(solution)/shard_map/pallas_call | solution.py:721
  (60 shorter events, 13.3 us)
Async XLA Ops:
  1.5 21.4 %collective-permute-start = (bf16[32,1536]{1,0:T(8,128)(2,1)S(1)}, bf16[32,1536]{1,0:T(8,128)(2,1)S(1)}, u32[]{:S(2)}, u32[]{:S(2)}) collective-permute-start(bf16[32,1536]{1,0:T(8,128)(2,1)S(1)} %get-tuple-element.49), channel_id=1, source_target_pairs={{0,1},{1,0},{2,3},{3,2},{4,5},{5,4},{6,7},{7,6},{8,9},{9,8},{10,11... | collective-permute-start | bytes 294920 | tf_op jit(solution)/shard_map/ppermute | solution.py:560
  2.0 23.6 %collective-permute-start.1 = (bf16[32,1536]{1,0:T(8,128)(2,1)S(1)}, bf16[32,1536]{1,0:T(8,128)(2,1)S(1)}, u32[]{:S(2)}, u32[]{:S(2)}) collective-permute-start(bf16[32,1536]{1,0:T(8,128)(2,1)S(1)} %get-tuple-element.50), channel_id=1, source_target_pairs={{0,31},{1,2},{2,1},{3,4},{4,3},{5,6},{6,5},{7,8},{8,7},{9,10},{10,... | collective-permute-start | bytes 294920 | tf_op jit(solution)/shard_map/ppermute | solution.py:560
  8.6 26.7 %collective-permute-start.4 = (bf16[128,1536]{1,0:T(8,128)(2,1)S(1)}, bf16[128,1536]{1,0:T(8,128)(2,1)S(1)}, u32[]{:S(2)}, u32[]{:S(2)}) collective-permute-start(bf16[128,1536]{1,0:T(8,128)(2,1)S(1)} %get-tuple-element.63.refs_2_.cot_ref), channel_id=1, source_target_pairs={{0,2},{1,3},{2,0},{3,1},{4,6},{5,7},{6,4},{7,5},{8,10},{9,11},{10,... | collective-permute-start | bytes 1179656 | tf_op jit(solution)/shard_map/ppermute | solution.py:560
  9.7 10.2 %collective-permute-start.7 = (bf16[2,48,512]{2,1,0:T(8,128)(2,1)S(1)}, bf16[2,48,512]{2,1,0:T(8,128)(2,1)S(1)}, u32[]{:S(2)}, u32[]{:S(2)}) collective-permute-start(bf16[2,48,512]{2,1,0:T(8,128)(2,1)S(1)} %get-tuple-element.66), channel_id=1, source_target_pairs={{0,2},{1,3},{2,0},{3,1},{4,6},{5,7},{6,4},{7,5},{8,10},{9,11},{10,... | collective-permute-start | bytes 294920 | tf_op jit(solution)/shard_map/ppermute | solution.py:560
  11.8 8.2 %collective-permute-start.8 = (bf16[2,48,512]{2,1,0:T(8,128)(2,1)S(1)}, bf16[2,48,512]{2,1,0:T(8,128)(2,1)S(1)}, u32[]{:S(2)}, u32[]{:S(2)}) collective-permute-start(bf16[2,48,512]{2,1,0:T(8,128)(2,1)S(1)} %get-tuple-element.67), channel_id=1, source_target_pairs={{0,3},{1,2},{2,1},{3,0},{4,7},{5,6},{6,5},{7,4},{8,11},{9,10},{10,... | collective-permute-start | bytes 294920 | tf_op jit(solution)/shard_map/ppermute | solution.py:560
  20.0 8.3 %collective-permute-start.11 = (bf16[2,96,512]{2,1,0:T(8,128)(2,1)S(1)}, bf16[2,96,512]{2,1,0:T(8,128)(2,1)S(1)}, u32[]{:S(2)}, u32[]{:S(2)}) collective-permute-start(bf16[2,96,512]{2,1,0:T(8,128)(2,1)S(1)} %constant_dynamic-update-slice_fusion.2.refs_7_), channel_id=1, source_target_pairs={{0,8},{1,9},{2,10},{3,11},{8,16},{9,17},{10,18},{11,19},{16,24},{1... | collective-permute-start | bytes 589832 | tf_op jit(solution)/shard_map/ppermute | solution.py:560
  22.9 7.8 %collective-permute-start.12 = (bf16[2,96,512]{2,1,0:T(8,128)(2,1)S(1)}, bf16[2,96,512]{2,1,0:T(8,128)(2,1)S(1)}, u32[]{:S(2)}, u32[]{:S(2)}) collective-permute-start(bf16[2,96,512]{2,1,0:T(8,128)(2,1)S(1)} %constant_dynamic-update-slice_fusion.2.refs_7_), channel_id=1, source_target_pairs={{0,4},{1,5},{2,6},{3,7},{8,0},{9,1},{10,2},{11,3},{16,8},{17,9},{1... | collective-permute-start | bytes 589832 | tf_op jit(solution)/shard_map/ppermute | solution.py:560
  22.9 9.7 %collective-permute-start.9 = (bf16[2,96,512]{2,1,0:T(8,128)(2,1)S(1)}, bf16[2,96,512]{2,1,0:T(8,128)(2,1)S(1)}, u32[]{:S(2)}, u32[]{:S(2)}) collective-permute-start(bf16[2,96,512]{2,1,0:T(8,128)(2,1)S(1)} %constant_dynamic-update-slice_fusion.refs_6_), channel_id=1, source_target_pairs={{0,8},{1,9},{2,10},{3,11},{8,16},{9,17},{10,18},{11,19},{16,24},{1... | collective-permute-start | bytes 589832 | tf_op jit(solution)/shard_map/ppermute | solution.py:560
  25.6 8.9 %collective-permute-start.10 = (bf16[2,96,512]{2,1,0:T(8,128)(2,1)S(1)}, bf16[2,96,512]{2,1,0:T(8,128)(2,1)S(1)}, u32[]{:S(2)}, u32[]{:S(2)}) collective-permute-start(bf16[2,96,512]{2,1,0:T(8,128)(2,1)S(1)} %constant_dynamic-update-slice_fusion.refs_6_), channel_id=1, source_target_pairs={{0,4},{1,5},{2,6},{3,7},{8,0},{9,1},{10,2},{11,3},{16,8},{17,9},{1... | collective-permute-start | bytes 589832 | tf_op jit(solution)/shard_map/ppermute | solution.py:560
  28.3 16.5 %collective-permute-start.21 = (bf16[128,1536]{1,0:T(8,128)(2,1)S(1)}, bf16[128,1536]{1,0:T(8,128)(2,1)S(1)}, u32[]{:S(2)}, u32[]{:S(2)}) collective-permute-start(bf16[128,1536]{1,0:T(8,128)(2,1)S(1)} %get-tuple-element.62.refs_1_), channel_id=1, source_target_pairs={{0,2},{1,3},{2,0},{3,1},{4,6},{5,7},{6,4},{7,5},{8,10},{9,11},{10,... | collective-permute-start | bytes 1179656 | tf_op jit(solution)/shard_map/ppermute | solution.py:560
  30.6 6.4 %collective-permute-start.15 = (bf16[2,96,512]{2,1,0:T(8,128)(2,1)S(1)}, bf16[2,96,512]{2,1,0:T(8,128)(2,1)S(1)}, u32[]{:S(2)}, u32[]{:S(2)}) collective-permute-start(bf16[2,96,512]{2,1,0:T(8,128)(2,1)S(1)} %collective-permute-done.11.refs_10_), channel_id=1, source_target_pairs={{0,8},{1,9},{2,10},{3,11},{8,16},{9,17},{10,18},{11,19},{16,24},{1... | collective-permute-start | bytes 589832 | tf_op jit(solution)/shard_map/ppermute | solution.py:560
  32.5 8.1 %collective-permute-start.16 = (bf16[2,96,512]{2,1,0:T(8,128)(2,1)S(1)}, bf16[2,96,512]{2,1,0:T(8,128)(2,1)S(1)}, u32[]{:S(2)}, u32[]{:S(2)}) collective-permute-start(bf16[2,96,512]{2,1,0:T(8,128)(2,1)S(1)} %collective-permute-done.12.refs_11_), channel_id=1, source_target_pairs={{0,4},{1,5},{2,6},{3,7},{8,0},{9,1},{10,2},{11,3},{16,8},{17,9},{1... | collective-permute-start | bytes 589832 | tf_op jit(solution)/shard_map/ppermute | solution.py:560
  34.6 7.8 %collective-permute-start.13 = (bf16[2,96,512]{2,1,0:T(8,128)(2,1)S(1)}, bf16[2,96,512]{2,1,0:T(8,128)(2,1)S(1)}, u32[]{:S(2)}, u32[]{:S(2)}) collective-permute-start(bf16[2,96,512]{2,1,0:T(8,128)(2,1)S(1)} %collective-permute-done.9.refs_8_), channel_id=1, source_target_pairs={{0,8},{1,9},{2,10},{3,11},{8,16},{9,17},{10,18},{11,19},{16,24},{1... | collective-permute-start | bytes 589832 | tf_op jit(solution)/shard_map/ppermute | solution.py:560
  35.3 9.5 %collective-permute-start.14 = (bf16[2,96,512]{2,1,0:T(8,128)(2,1)S(1)}, bf16[2,96,512]{2,1,0:T(8,128)(2,1)S(1)}, u32[]{:S(2)}, u32[]{:S(2)}) collective-permute-start(bf16[2,96,512]{2,1,0:T(8,128)(2,1)S(1)} %collective-permute-done.10.refs_9_), channel_id=1, source_target_pairs={{0,4},{1,5},{2,6},{3,7},{8,0},{9,1},{10,2},{11,3},{16,8},{17,9},{1... | collective-permute-start | bytes 589832 | tf_op jit(solution)/shard_map/ppermute | solution.py:560
  37.1 9.5 %collective-permute-start.19 = (bf16[2,96,512]{2,1,0:T(8,128)(2,1)S(1)}, bf16[2,96,512]{2,1,0:T(8,128)(2,1)S(1)}, u32[]{:S(2)}, u32[]{:S(2)}) collective-permute-start(bf16[2,96,512]{2,1,0:T(8,128)(2,1)S(1)} %collective-permute-done.15.refs_14_), channel_id=1, source_target_pairs={{0,8},{1,9},{2,10},{3,11},{8,16},{9,17},{10,18},{11,19},{16,24},{1... | collective-permute-start | bytes 589832 | tf_op jit(solution)/shard_map/ppermute | solution.py:560
  40.6 6.5 %collective-permute-start.20 = (bf16[2,96,512]{2,1,0:T(8,128)(2,1)S(1)}, bf16[2,96,512]{2,1,0:T(8,128)(2,1)S(1)}, u32[]{:S(2)}, u32[]{:S(2)}) collective-permute-start(bf16[2,96,512]{2,1,0:T(8,128)(2,1)S(1)} %collective-permute-done.16.refs_15_), channel_id=1, source_target_pairs={{0,4},{1,5},{2,6},{3,7},{8,0},{9,1},{10,2},{11,3},{16,8},{17,9},{1... | collective-permute-start | bytes 589832 | tf_op jit(solution)/shard_map/ppermute | solution.py:560
  42.3 6.6 %collective-permute-start.17 = (bf16[2,96,512]{2,1,0:T(8,128)(2,1)S(1)}, bf16[2,96,512]{2,1,0:T(8,128)(2,1)S(1)}, u32[]{:S(2)}, u32[]{:S(2)}) collective-permute-start(bf16[2,96,512]{2,1,0:T(8,128)(2,1)S(1)} %collective-permute-done.13.refs_12_), channel_id=1, source_target_pairs={{0,8},{1,9},{2,10},{3,11},{8,16},{9,17},{10,18},{11,19},{16,24},{1... | collective-permute-start | bytes 589832 | tf_op jit(solution)/shard_map/ppermute | solution.py:560
  44.8 11.7 %collective-permute-start.3 = (bf16[128,1536]{1,0:T(8,128)(2,1)S(1)}, bf16[128,1536]{1,0:T(8,128)(2,1)S(1)}, u32[]{:S(2)}, u32[]{:S(2)}) collective-permute-start(bf16[128,1536]{1,0:T(8,128)(2,1)S(1)} %get-tuple-element.63.refs_2_.cot_ref), channel_id=1, source_target_pairs={{0,1},{1,0},{2,3},{3,2},{4,5},{5,4},{6,7},{7,6},{8,9},{9,8},{10,11... | collective-permute-start | bytes 1179656 | tf_op jit(solution)/shard_map/ppermute | solution.py:560
  44.8 12.0 %collective-permute-start.2 = (bf16[128,1536]{1,0:T(8,128)(2,1)S(1)}, bf16[128,1536]{1,0:T(8,128)(2,1)S(1)}, u32[]{:S(2)}, u32[]{:S(2)}) collective-permute-start(bf16[128,1536]{1,0:T(8,128)(2,1)S(1)} %get-tuple-element.62.refs_1_), channel_id=1, source_target_pairs={{0,1},{1,0},{2,3},{3,2},{4,5},{5,4},{6,7},{7,6},{8,9},{9,8},{10,11... | collective-permute-start | bytes 1179656 | tf_op jit(solution)/shard_map/ppermute | solution.py:560
  46.6 12.1 %collective-permute-start.5 = (bf16[128,1536]{1,0:T(8,128)(2,1)S(1)}, bf16[128,1536]{1,0:T(8,128)(2,1)S(1)}, u32[]{:S(2)}, u32[]{:S(2)}) collective-permute-start(bf16[128,1536]{1,0:T(8,128)(2,1)S(1)} %collective-permute-done.4.refs_4_), channel_id=1, source_target_pairs={{0,1},{1,0},{2,3},{3,2},{4,5},{5,4},{6,7},{7,6},{8,9},{9,8},{10,11... | collective-permute-start | bytes 1179656 | tf_op jit(solution)/shard_map/ppermute | solution.py:560
  47.1 13.7 %collective-permute-start.22 = (bf16[128,1536]{1,0:T(8,128)(2,1)S(1)}, bf16[128,1536]{1,0:T(8,128)(2,1)S(1)}, u32[]{:S(2)}, u32[]{:S(2)}) collective-permute-start(bf16[128,1536]{1,0:T(8,128)(2,1)S(1)} %collective-permute-done.21.refs_1_.far_ref), channel_id=1, source_target_pairs={{0,1},{1,0},{2,3},{3,2},{4,5},{5,4},{6,7},{7,6},{8,9},{9,8},{10,11... | collective-permute-start | bytes 1179656 | tf_op jit(solution)/shard_map/ppermute | solution.py:560
  49.0 5.7 %collective-permute-start.18 = (bf16[2,96,512]{2,1,0:T(8,128)(2,1)S(1)}, bf16[2,96,512]{2,1,0:T(8,128)(2,1)S(1)}, u32[]{:S(2)}, u32[]{:S(2)}) collective-permute-start(bf16[2,96,512]{2,1,0:T(8,128)(2,1)S(1)} %collective-permute-done.14.refs_13_), channel_id=1, source_target_pairs={{0,4},{1,5},{2,6},{3,7},{8,0},{9,1},{10,2},{11,3},{16,8},{17,9},{1... | collective-permute-start | bytes 589832 | tf_op jit(solution)/shard_map/ppermute | solution.py:560
  54.7 6.8 %collective-permute-start.25 = (bf16[1,96,512]{2,1,0:T(8,128)(2,1)S(1)}, bf16[1,96,512]{2,1,0:T(8,128)(2,1)S(1)}, u32[]{:S(2)}, u32[]{:S(2)}) collective-permute-start(bf16[1,96,512]{2,1,0:T(8,128)(2,1)S(1)} %slice.18), channel_id=1, source_target_pairs={{0,8},{1,9},{2,10},{3,11},{8,16},{9,17},{10,18},{11,19},{16,24},{1... | collective-permute-start | bytes 294920 | tf_op jit(solution)/shard_map/ppermute | solution.py:560
  56.5 5.0 %collective-permute-start.26 = (bf16[1,96,512]{2,1,0:T(8,128)(2,1)S(1)}, bf16[1,96,512]{2,1,0:T(8,128)(2,1)S(1)}, u32[]{:S(2)}, u32[]{:S(2)}) collective-permute-start(bf16[1,96,512]{2,1,0:T(8,128)(2,1)S(1)} %slice.19), channel_id=1, source_target_pairs={{0,4},{1,5},{2,6},{3,7},{8,0},{9,1},{10,2},{11,3},{16,8},{17,9},{1... | collective-permute-start | bytes 294920 | tf_op jit(solution)/shard_map/ppermute | solution.py:560
  56.8 4.8 %collective-permute-start.23 = (bf16[1,96,512]{2,1,0:T(8,128)(2,1)S(1)}, bf16[1,96,512]{2,1,0:T(8,128)(2,1)S(1)}, u32[]{:S(2)}, u32[]{:S(2)}) collective-permute-start(bf16[1,96,512]{2,1,0:T(8,128)(2,1)S(1)} %slice.16), channel_id=1, source_target_pairs={{0,8},{1,9},{2,10},{3,11},{8,16},{9,17},{10,18},{11,19},{16,24},{1... | collective-permute-start | bytes 294920 | tf_op jit(solution)/shard_map/ppermute | solution.py:560
  58.6 4.6 %collective-permute-start.24 = (bf16[1,96,512]{2,1,0:T(8,128)(2,1)S(1)}, bf16[1,96,512]{2,1,0:T(8,128)(2,1)S(1)}, u32[]{:S(2)}, u32[]{:S(2)}) collective-permute-start(bf16[1,96,512]{2,1,0:T(8,128)(2,1)S(1)} %slice.17), channel_id=1, source_target_pairs={{0,4},{1,5},{2,6},{3,7},{8,0},{9,1},{10,2},{11,3},{16,8},{17,9},{1... | collective-permute-start | bytes 294920 | tf_op jit(solution)/shard_map/ppermute | solution.py:560
  65.1 13.6 %collective-permute-start.27 = (bf16[128,1536]{1,0:T(8,128)(2,1)S(1)}, bf16[128,1536]{1,0:T(8,128)(2,1)S(1)}, u32[]{:S(2)}, u32[]{:S(2)}) collective-permute-start(bf16[128,1536]{1,0:T(8,128)(2,1)S(1)} %get-tuple-element.79), channel_id=1, source_target_pairs={{0,1},{1,0},{2,3},{3,2},{4,5},{5,4},{6,7},{7,6},{8,9},{9,8},{10,11... | collective-permute-start | bytes 1179656 | tf_op jit(solution)/shard_map/ppermute | solution.py:560
  66.4 16.9 %collective-permute-start.29 = (bf16[128,1536]{1,0:T(8,128)(2,1)S(1)}, bf16[128,1536]{1,0:T(8,128)(2,1)S(1)}, u32[]{:S(2)}, u32[]{:S(2)}) collective-permute-start(bf16[128,1536]{1,0:T(8,128)(2,1)S(1)} %shard_map.138), channel_id=1, source_target_pairs={{0,2},{1,3},{2,0},{3,1},{4,6},{5,7},{6,4},{7,5},{8,10},{9,11},{10,... | collective-permute-start | bytes 1179656 | tf_op jit(solution)/shard_map/ppermute | solution.py:560
  67.5 10.4 %collective-permute-start.32 = (bf16[2,32,128]{2,1,0:T(8,128)(2,1)S(1)}, bf16[2,32,128]{2,1,0:T(8,128)(2,1)S(1)}, u32[]{:S(2)}, u32[]{:S(2)}) collective-permute-start(bf16[2,32,128]{2,1,0:T(8,128)(2,1)S(1)} %get-tuple-element.88), channel_id=1, source_target_pairs={{0,2},{1,3},{2,0},{3,1},{4,6},{5,7},{6,4},{7,5},{8,10},{9,11},{10,... | collective-permute-start | bytes 49160 | tf_op jit(solution)/shard_map/ppermute | solution.py:560
  78.6 6.8 %collective-permute-start.33 = (bf16[32,1536]{1,0:T(8,128)(2,1)S(1)}, bf16[32,1536]{1,0:T(8,128)(2,1)S(1)}, u32[]{:S(2)}, u32[]{:S(2)}) collective-permute-start(bf16[32,1536]{1,0:T(8,128)(2,1)S(1)} %shard_map.141), channel_id=1, source_target_pairs={{2,31},{3,2},{0,1},{1,4},{6,3},{7,6},{4,5},{5,8},{10,7},{11,10},{8... | collective-permute-start | bytes 294920 | tf_op jit(solution)/shard_map/ppermute | solution.py:560
  79.5 7.8 %collective-permute-start.31 = (bf16[32,1536]{1,0:T(8,128)(2,1)S(1)}, bf16[32,1536]{1,0:T(8,128)(2,1)S(1)}, u32[]{:S(2)}, u32[]{:S(2)}) collective-permute-start(bf16[32,1536]{1,0:T(8,128)(2,1)S(1)} %get-tuple-element.87), channel_id=1, source_target_pairs={{0,31},{1,2},{2,1},{3,4},{4,3},{5,6},{6,5},{7,8},{8,7},{9,10},{10,... | collective-permute-start | bytes 294920 | tf_op jit(solution)/shard_map/ppermute | solution.py:560
  84.1 3.2 %collective-permute-start.30 = (bf16[32,1536]{1,0:T(8,128)(2,1)S(1)}, bf16[32,1536]{1,0:T(8,128)(2,1)S(1)}, u32[]{:S(2)}, u32[]{:S(2)}) collective-permute-start(bf16[32,1536]{1,0:T(8,128)(2,1)S(1)} %get-tuple-element.86), channel_id=1, source_target_pairs={{0,1},{1,0},{2,3},{3,2},{4,5},{5,4},{6,7},{7,6},{8,9},{9,8},{10,11... | collective-permute-start | bytes 294920 | tf_op jit(solution)/shard_map/ppermute | solution.py:560
  (2 other events, 5.2 us)

commit v5 on v4

--- a/solution.py
+++ b/solution.py
@@ -386,7 +386,7 @@
 
 
 def send_body(groups, ups_in, pre_ref, back_ref, x_last, g_last, *refs):
-    parts, (ups, up, down, gate_ref, send_ref) = refs[:4], refs[4:]
+    parts, (ups, up, down, send_ref) = refs[:4], refs[4:]
     member = lax.axis_index("patch") % TEAM
     rows = parts[0].shape[1] // 2
     for k in range(2):
@@ -398,15 +398,18 @@
     tall = up.shape[0]
     ups[pl.ds(pl.multiple_of(far_owner(groups) * tall, 16), tall)] = up[...]
     columns = send_ref.shape[0]
-    two = slice(0, 2 * columns)
-    pre_act = pre_ref[...] + mm(x_last[...], up[...])
-    grad_pre = gated(pre_act, back_ref[two] + mm(g_last[two], down[...]))
-    gate_ref[...] = grad_pre[columns:]
-    send_ref[...] = mm(grad_pre[:columns], ups[...], ((1,), (1,))).astype(jnp.bfloat16)
-
-
-def cross_body(gate_ref, ups, cross_ref):
-    cross_ref[...] = mm(gate_ref[...], ups[...], ((1,), (1,)))
+    one = slice(0, columns)
+    pre_act = pre_ref[one] + mm(x_last[one], up[...])
+    grad_pre = gated(pre_act, back_ref[one] + mm(g_last[one], down[...]))
+    send_ref[...] = mm(grad_pre, ups[...], ((1,), (1,))).astype(jnp.bfloat16)
+
+
+def cross_body(ups, up, down, pre_ref, back_ref, x_last, g_last, cross_ref):
+    columns = cross_ref.shape[0]
+    one = slice(columns, 2 * columns)
+    pre_act = pre_ref[one] + mm(x_last[one], up[...])
+    grad_pre = gated(pre_act, back_ref[one] + mm(g_last[one], down[...]))
+    cross_ref[...] = mm(grad_pre, ups[...], ((1,), (1,)))
 
 
 def keep_body(ups, up, down, pre_ref, back_ref, x_last, g_last, mine_ref, send_ref):
@@ -677,12 +680,11 @@
         [norm_cross, norm_far, ups],
         [pltpu.VMEM((team // 2, width), jnp.bfloat16)],
     )
-    ups, up_last, down_last, gate, send_cross = call(
+    ups, up_last, down_last, send_cross = call(
         lambda *refs: send_body(groups, *refs),
         [
             struct((width, span)),
             *[struct((tall, span))] * 2,
-            struct((columns, span)),
             struct((columns, width)),
         ],
         [ups, pre_b, back_sum, xb_last, g_last, *last_chunks],
@@ -691,7 +693,7 @@
         ((0, 0),),
     )
     received_cross = swap(send_cross, 1)
-    cross = call(cross_body, wide, [gate, ups])
+    cross = call(cross_body, wide, [ups, up_last, down_last, pre_b, back_sum, xb_last, g_last])
     crossing = call(join_body, struct((columns, width)), [cross, received_cross])
     crossed = swap(crossing, 2)
     mine, send = call(

time: 88.6 us -> 88.6 us (level)
  transfers between devices with their start and end apart: 34 -> 34, of which waited for: 16 -> 16; matrix products, arithmetic and copies ran while one was open for 0% -> 0% of each run, Pallas kernels for 11% -> 12%
where the time goes in v5:
time: 88.6 us; the launch traced here: 88.4 us
  starting transfers between devices  39.5 us (45%)
  waiting for transfers between devices  35 us (40%)
  Pallas kernels  13.6 us (15%)
    ppermute x34, starting transfers between devices, permute(): return lax.ppermute(value, 'patch', pairs)  39.5 us
    ppermute x34, waiting for transfers between devices, permute(): return lax.ppermute(value, 'patch', pairs)  35 us
    pallas_call x15, Pallas kernels, call(): pl.pallas_call(body, out_shape=outs, in_specs=specs, out_specs=jax.tree.m...  12.6 us
  transfers between devices with their start and end apart: 34, of which 16 were waited for; matrix products, arithmetic and copies ran while one was open for 0% of the time, Pallas kernels for 12%

profile of v5, /device:TPU:0, one launch (start us, length us, event | category | flops | bytes accessed | tf_op | source)
XLA Modules:
  0.0 88.4 jit_solution(2508073938424074483)
XLA Ops:
  0.0 1.2 %shard_map.127 = (bf16[128,1536]{1,0:T(8,128)(2,1)S(1)}, bf16[128,1536]{1,0:T(8,128)(2,1)S(1)}, s32[1,64]{1,0:T(1,128)S(1)}, s32[6,128]{1,0:T(8,128)S(1)}, s32[6...) custom-call(bf16[128,1536]{1,0:T(8,128)(2,1)} %bitcast.7, ...), custom_call_target="tpu_custom_call" | custom-call | tf_op jit(solution)/shard_map/pallas_call | solution.py:184
  2.0 6.6 %collective-permute-start.1 = (bf16[32,1536]{1,0:T(8,128)(2,1)S(1)}, bf16[32,1536]{1,0:T(8,128)(2,1)S(1)}, u32[]{:S(2)}, u32[]{:S(2)}) collective-permute-start(bf16[32,1536]{1,0:T(8,128)(2,1)S(1)} %get-tuple-element.49), channel_id=1, source_target_pairs={{0,31},{1,2},{2,1},{3,4},{4,3},{5,6},{6,5},{7,8},{8,7},{9,10},{10,... | collective-permute-start | bytes 294920 | tf_op jit(solution)/shard_map/ppermute | solution.py:563
  8.6 1.0 %shard_map.131 = (bf16[2,48,512]{2,1,0:T(8,128)(2,1)S(1)}, bf16[2,48,512]{2,1,0:T(8,128)(2,1)S(1)}, bf16[2,48,512]{2,1,0:T(8,128)(2,1)S(1)}, bf16[2,48,512]{2,1,0:T(8,128)(2,1)S(1)}) custom-call(bf16[48,2048]{1,0:T(8,128)(2,1)} %up_ref.1, bf16[48,2048]{1,0:T(8,128)(2,1)} %down_ref.1), custom_call_target="tpu_custom_call" | custom-call | tf_op jit(solution)/shard_map/pallas_call | solution.py:184
  9.7 2.1 %collective-permute-start.7 = (bf16[2,48,512]{2,1,0:T(8,128)(2,1)S(1)}, bf16[2,48,512]{2,1,0:T(8,128)(2,1)S(1)}, u32[]{:S(2)}, u32[]{:S(2)}) collective-permute-start(bf16[2,48,512]{2,1,0:T(8,128)(2,1)S(1)} %get-tuple-element.65), channel_id=1, source_target_pairs={{0,2},{1,3},{2,0},{3,1},{4,6},{5,7},{6,4},{7,5},{8,10},{9,11},{10,... | collective-permute-start | bytes 294920 | tf_op jit(solution)/shard_map/ppermute | solution.py:563
  11.8 8.1 %collective-permute-done.7 = bf16[2,48,512]{2,1,0:T(8,128)(2,1)S(1)} collective-permute-done((bf16[2,48,512]{2,1,0:T(8,128)(2,1)S(1)}, bf16[2,48,512]{2,1,0:T(8,128)(2,1)S(1)}, u32[]{:S(2)}, u32[]{:S(2)}) %collective-permute-start.7) | collective-permute-done | bytes 98336 | tf_op jit(solution)/shard_map/ppermute | solution.py:563
  20.0 2.8 %collective-permute-start.11 = (bf16[2,96,512]{2,1,0:T(8,128)(2,1)S(1)}, bf16[2,96,512]{2,1,0:T(8,128)(2,1)S(1)}, u32[]{:S(2)}, u32[]{:S(2)}) collective-permute-start(bf16[2,96,512]{2,1,0:T(8,128)(2,1)S(1)} %constant_dynamic-update-slice_fusion.2.refs_7_), channel_id=1, source_target_pairs={{0,8},{1,9},{2,10},{3,11},{8,16},{9,17},{10,18},{11,19},{16,24},{1... | collective-permute-start | bytes 589832 | tf_op jit(solution)/shard_map/ppermute | solution.py:563
  22.9 2.1 %collective-permute-start.9 = (bf16[2,96,512]{2,1,0:T(8,128)(2,1)S(1)}, bf16[2,96,512]{2,1,0:T(8,128)(2,1)S(1)}, u32[]{:S(2)}, u32[]{:S(2)}) collective-permute-start(bf16[2,96,512]{2,1,0:T(8,128)(2,1)S(1)} %constant_dynamic-update-slice_fusion.refs_6_), channel_id=1, source_target_pairs={{0,8},{1,9},{2,10},{3,11},{8,16},{9,17},{10,18},{11,19},{16,24},{1... | collective-permute-start | bytes 589832 | tf_op jit(solution)/shard_map/ppermute | solution.py:563
  25.7 1.1 %shard_map.130 = (bf16[128,1536]{1,0:T(8,128)(2,1)S(1)}, bf16[128,1536]{1,0:T(8,128)(2,1)S(1)}, bf16[2,32,128]{2,1,0:T(8,128)(2,1)S(1)}, f32[128,128]{1,0:T(8,128)S(1)}) custom-call(bf16[128,1536]{1,0:T(8,128)(2,1)S(1)} %get-tuple-element.46.x_ref, bf16[32,1536]{1,0:T(8,128)(2,1)S(1)} %collective-permute-done.inner_ref, ...), custom_call_target="tpu_custom_call" | custom-call | tf_op jit(solution)/shard_map/pallas_call | solution.py:184
  26.8 1.6 %collective-permute-done.11.refs_10_ = bf16[2,96,512]{2,1,0:T(8,128)(2,1)S(1)} collective-permute-done((bf16[2,96,512]{2,1,0:T(8,128)(2,1)S(1)}, bf16[2,96,512]{2,1,0:T(8,128)(2,1)S(1)}, u32[]{:S(2)}, u32[]{:S(2)}) %collective-permute-start.11) | collective-permute-done | bytes 196640 | tf_op jit(solution)/shard_map/ppermute | solution.py:563
  29.3 1.3 %collective-permute-done.12.refs_11_ = bf16[2,96,512]{2,1,0:T(8,128)(2,1)S(1)} collective-permute-done((bf16[2,96,512]{2,1,0:T(8,128)(2,1)S(1)}, bf16[2,96,512]{2,1,0:T(8,128)(2,1)S(1)}, u32[]{:S(2)}, u32[]{:S(2)}) %collective-permute-start.12) | collective-permute-done | bytes 196640 | tf_op jit(solution)/shard_map/ppermute | solution.py:563
  30.6 1.6 %collective-permute-start.15 = (bf16[2,96,512]{2,1,0:T(8,128)(2,1)S(1)}, bf16[2,96,512]{2,1,0:T(8,128)(2,1)S(1)}, u32[]{:S(2)}, u32[]{:S(2)}) collective-permute-start(bf16[2,96,512]{2,1,0:T(8,128)(2,1)S(1)} %collective-permute-done.11.refs_10_), channel_id=1, source_target_pairs={{0,8},{1,9},{2,10},{3,11},{8,16},{9,17},{10,18},{11,19},{16,24},{1... | collective-permute-start | bytes 589832 | tf_op jit(solution)/shard_map/ppermute | solution.py:563
  32.5 2.0 %collective-permute-start.16 = (bf16[2,96,512]{2,1,0:T(8,128)(2,1)S(1)}, bf16[2,96,512]{2,1,0:T(8,128)(2,1)S(1)}, u32[]{:S(2)}, u32[]{:S(2)}) collective-permute-start(bf16[2,96,512]{2,1,0:T(8,128)(2,1)S(1)} %collective-permute-done.12.refs_11_), channel_id=1, source_target_pairs={{0,4},{1,5},{2,6},{3,7},{8,0},{9,1},{10,2},{11,3},{16,8},{17,9},{1... | collective-permute-start | bytes 589832 | tf_op jit(solution)/shard_map/ppermute | solution.py:563
  35.3 1.3 %collective-permute-start.14 = (bf16[2,96,512]{2,1,0:T(8,128)(2,1)S(1)}, bf16[2,96,512]{2,1,0:T(8,128)(2,1)S(1)}, u32[]{:S(2)}, u32[]{:S(2)}) collective-permute-start(bf16[2,96,512]{2,1,0:T(8,128)(2,1)S(1)} %collective-permute-done.10.refs_9_), channel_id=1, source_target_pairs={{0,4},{1,5},{2,6},{3,7},{8,0},{9,1},{10,2},{11,3},{16,8},{17,9},{1... | collective-permute-start | bytes 589832 | tf_op jit(solution)/shard_map/ppermute | solution.py:563
  37.1 2.5 %collective-permute-start.19 = (bf16[2,96,512]{2,1,0:T(8,128)(2,1)S(1)}, bf16[2,96,512]{2,1,0:T(8,128)(2,1)S(1)}, u32[]{:S(2)}, u32[]{:S(2)}) collective-permute-start(bf16[2,96,512]{2,1,0:T(8,128)(2,1)S(1)} %collective-permute-done.15.refs_14_), channel_id=1, source_target_pairs={{0,8},{1,9},{2,10},{3,11},{8,16},{9,17},{10,18},{11,19},{16,24},{1... | collective-permute-start | bytes 589832 | tf_op jit(solution)/shard_map/ppermute | solution.py:563
  39.5 1.0 %collective-permute-done.16.refs_15_ = bf16[2,96,512]{2,1,0:T(8,128)(2,1)S(1)} collective-permute-done((bf16[2,96,512]{2,1,0:T(8,128)(2,1)S(1)}, bf16[2,96,512]{2,1,0:T(8,128)(2,1)S(1)}, u32[]{:S(2)}, u32[]{:S(2)}) %collective-permute-start.16) | collective-permute-done | bytes 196640 | tf_op jit(solution)/shard_map/ppermute | solution.py:563
  40.6 1.7 %collective-permute-start.20 = (bf16[2,96,512]{2,1,0:T(8,128)(2,1)S(1)}, bf16[2,96,512]{2,1,0:T(8,128)(2,1)S(1)}, u32[]{:S(2)}, u32[]{:S(2)}) collective-permute-start(bf16[2,96,512]{2,1,0:T(8,128)(2,1)S(1)} %collective-permute-done.16.refs_15_), channel_id=1, source_target_pairs={{0,4},{1,5},{2,6},{3,7},{8,0},{9,1},{10,2},{11,3},{16,8},{17,9},{1... | collective-permute-start | bytes 589832 | tf_op jit(solution)/shard_map/ppermute | solution.py:563
  42.3 1.4 %collective-permute-start.17 = (bf16[2,96,512]{2,1,0:T(8,128)(2,1)S(1)}, bf16[2,96,512]{2,1,0:T(8,128)(2,1)S(1)}, u32[]{:S(2)}, u32[]{:S(2)}) collective-permute-start(bf16[2,96,512]{2,1,0:T(8,128)(2,1)S(1)} %collective-permute-done.13.refs_12_), channel_id=1, source_target_pairs={{0,8},{1,9},{2,10},{3,11},{8,16},{9,17},{10,18},{11,19},{16,24},{1... | collective-permute-start | bytes 589832 | tf_op jit(solution)/shard_map/ppermute | solution.py:563
  43.8 1.0 %collective-permute-done.14.refs_13_ = bf16[2,96,512]{2,1,0:T(8,128)(2,1)S(1)} collective-permute-done((bf16[2,96,512]{2,1,0:T(8,128)(2,1)S(1)}, bf16[2,96,512]{2,1,0:T(8,128)(2,1)S(1)}, u32[]{:S(2)}, u32[]{:S(2)}) %collective-permute-start.14) | collective-permute-done | bytes 196640 | tf_op jit(solution)/shard_map/ppermute | solution.py:563
  45.3 1.2 %collective-permute-done.19.refs_18_ = bf16[2,96,512]{2,1,0:T(8,128)(2,1)S(1)} collective-permute-done((bf16[2,96,512]{2,1,0:T(8,128)(2,1)S(1)}, bf16[2,96,512]{2,1,0:T(8,128)(2,1)S(1)}, u32[]{:S(2)}, u32[]{:S(2)}) %collective-permute-start.19) | collective-permute-done | bytes 196640 | tf_op jit(solution)/shard_map/ppermute | solution.py:563
  47.1 1.9 %collective-permute-done.17.refs_16_ = bf16[2,96,512]{2,1,0:T(8,128)(2,1)S(1)} collective-permute-done((bf16[2,96,512]{2,1,0:T(8,128)(2,1)S(1)}, bf16[2,96,512]{2,1,0:T(8,128)(2,1)S(1)}, u32[]{:S(2)}, u32[]{:S(2)}) %collective-permute-start.17) | collective-permute-done | bytes 196640 | tf_op jit(solution)/shard_map/ppermute | solution.py:563
  49.0 1.7 %collective-permute-start.18 = (bf16[2,96,512]{2,1,0:T(8,128)(2,1)S(1)}, bf16[2,96,512]{2,1,0:T(8,128)(2,1)S(1)}, u32[]{:S(2)}, u32[]{:S(2)}) collective-permute-start(bf16[2,96,512]{2,1,0:T(8,128)(2,1)S(1)} %collective-permute-done.14.refs_13_), channel_id=1, source_target_pairs={{0,4},{1,5},{2,6},{3,7},{8,0},{9,1},{10,2},{11,3},{16,8},{17,9},{1... | collective-permute-start | bytes 589832 | tf_op jit(solution)/shard_map/ppermute | solution.py:563
  50.8 3.9 %collective-permute-done.18.refs_17_ = bf16[2,96,512]{2,1,0:T(8,128)(2,1)S(1)} collective-permute-done((bf16[2,96,512]{2,1,0:T(8,128)(2,1)S(1)}, bf16[2,96,512]{2,1,0:T(8,128)(2,1)S(1)}, u32[]{:S(2)}, u32[]{:S(2)}) %collective-permute-start.18) | collective-permute-done | bytes 196640 | tf_op jit(solution)/shard_map/ppermute | solution.py:563
  54.7 1.8 %collective-permute-start.25 = (bf16[1,96,512]{2,1,0:T(8,128)(2,1)S(1)}, bf16[1,96,512]{2,1,0:T(8,128)(2,1)S(1)}, u32[]{:S(2)}, u32[]{:S(2)}) collective-permute-start(bf16[1,96,512]{2,1,0:T(8,128)(2,1)S(1)} %slice.18), channel_id=1, source_target_pairs={{0,8},{1,9},{2,10},{3,11},{8,16},{9,17},{10,18},{11,19},{16,24},{1... | collective-permute-start | bytes 294920 | tf_op jit(solution)/shard_map/ppermute | solution.py:563
  56.8 1.8 %collective-permute-start.23 = (bf16[1,96,512]{2,1,0:T(8,128)(2,1)S(1)}, bf16[1,96,512]{2,1,0:T(8,128)(2,1)S(1)}, u32[]{:S(2)}, u32[]{:S(2)}) collective-permute-start(bf16[1,96,512]{2,1,0:T(8,128)(2,1)S(1)} %slice.16), channel_id=1, source_target_pairs={{0,8},{1,9},{2,10},{3,11},{8,16},{9,17},{10,18},{11,19},{16,24},{1... | collective-permute-start | bytes 294920 | tf_op jit(solution)/shard_map/ppermute | solution.py:563
  58.8 1.9 %shard_map.132 = (bf16[1536,512]{1,0:T(8,128)(2,1)S(1)}, f32[256,512]{1,0:T(8,128)S(1)}, f32[512,512]{1,0:T(8,128)S(1)}, bf16[256,192]{1,0:T(8,128)(2,1)S(1)}, bf16[512,192]{1,0:T(8,128)(2,1)S(1)}) custom-call(bf16[128,1536]{1,0:T(8,128)(2,1)S(1)} %collective-permute-done.2.refs_0_, bf16[128,1536]{1,0:T(8,128)(2,1)S(1)} %get-tuple-element.61.refs_1_, ...), custom_call_target="tpu_custom_call" | custom-call | tf_op jit(solution)/shard_map/pallas_call | solution.py:184
  61.6 1.7 %collective-permute-done.24.refs_6_ = bf16[1,96,512]{2,1,0:T(8,128)(2,1)S(1)} collective-permute-done((bf16[1,96,512]{2,1,0:T(8,128)(2,1)S(1)}, bf16[1,96,512]{2,1,0:T(8,128)(2,1)S(1)}, u32[]{:S(2)}, u32[]{:S(2)}) %collective-permute-start.24) | collective-permute-done | bytes 98336 | tf_op jit(solution)/shard_map/ppermute | solution.py:563
  66.5 1.1 %collective-permute-start.29 = (bf16[128,1536]{1,0:T(8,128)(2,1)S(1)}, bf16[128,1536]{1,0:T(8,128)(2,1)S(1)}, u32[]{:S(2)}, u32[]{:S(2)}) collective-permute-start(bf16[128,1536]{1,0:T(8,128)(2,1)S(1)} %shard_map.138), channel_id=1, source_target_pairs={{0,2},{1,3},{2,0},{3,1},{4,6},{5,7},{6,4},{7,5},{8,10},{9,11},{10,... | collective-permute-start | bytes 1179656 | tf_op jit(solution)/shard_map/ppermute | solution.py:563
  67.5 1.0 %collective-permute-start.32 = (bf16[2,32,128]{2,1,0:T(8,128)(2,1)S(1)}, bf16[2,32,128]{2,1,0:T(8,128)(2,1)S(1)}, u32[]{:S(2)}, u32[]{:S(2)}) collective-permute-start(bf16[2,32,128]{2,1,0:T(8,128)(2,1)S(1)} %get-tuple-element.86), channel_id=1, source_target_pairs={{0,2},{1,3},{2,0},{3,1},{4,6},{5,7},{6,4},{7,5},{8,10},{9,11},{10,... | collective-permute-start | bytes 49160 | tf_op jit(solution)/shard_map/ppermute | solution.py:563
  68.6 9.4 %collective-permute-done.32.edge_ref = bf16[2,32,128]{2,1,0:T(8,128)(2,1)S(1)} collective-permute-done((bf16[2,32,128]{2,1,0:T(8,128)(2,1)S(1)}, bf16[2,32,128]{2,1,0:T(8,128)(2,1)S(1)}, u32[]{:S(2)}, u32[]{:S(2)}) %collective-permute-start.32) | collective-permute-done | bytes 16416 | tf_op jit(solution)/shard_map/ppermute | solution.py:563
  79.5 3.8 %collective-permute-start.31 = (bf16[32,1536]{1,0:T(8,128)(2,1)S(1)}, bf16[32,1536]{1,0:T(8,128)(2,1)S(1)}, u32[]{:S(2)}, u32[]{:S(2)}) collective-permute-start(bf16[32,1536]{1,0:T(8,128)(2,1)S(1)} %get-tuple-element.85), channel_id=1, source_target_pairs={{0,31},{1,2},{2,1},{3,4},{4,3},{5,6},{6,5},{7,8},{8,7},{9,10},{10,... | collective-permute-start | bytes 294920 | tf_op jit(solution)/shard_map/ppermute | solution.py:563
  85.4 1.9 %collective-permute-done.31.outer_ref = bf16[32,1536]{1,0:T(8,128)(2,1)S(1)} collective-permute-done((bf16[32,1536]{1,0:T(8,128)(2,1)S(1)}, bf16[32,1536]{1,0:T(8,128)(2,1)S(1)}, u32[]{:S(2)}, u32[]{:S(2)}) %collective-permute-start.31) | collective-permute-done | bytes 98336 | tf_op jit(solution)/shard_map/ppermute | solution.py:563
  87.3 1.1 %shard_map.142 = bf16[128,1536]{1,0:T(8,128)(2,1)} custom-call(f32[128,1536]{1,0:T(8,128)S(1)} %shard_map.140.local_ref, bf16[32,1536]{1,0:T(8,128)(2,1)S(1)} %collective-permute-done.30.inner_ref, bf16[32,1536]{1,0:T(8,128)(2,1)S(1)} %collective-permute-done.31.outer_ref, bf16[32,1536]{1,0:T(8,128)(2,1)S(1)} %collective-permute-done.33.other_ref, ...), custom_call_target="tpu_custom_call" | custom-call | tf_op jit(solution)/shard_map/pallas_call | solution.py:723
  (60 shorter events, 13.3 us)
Async XLA Ops:
  1.5 21.4 %collective-permute-start = (bf16[32,1536]{1,0:T(8,128)(2,1)S(1)}, bf16[32,1536]{1,0:T(8,128)(2,1)S(1)}, u32[]{:S(2)}, u32[]{:S(2)}) collective-permute-start(bf16[32,1536]{1,0:T(8,128)(2,1)S(1)} %get-tuple-element.48), channel_id=1, source_target_pairs={{0,1},{1,0},{2,3},{3,2},{4,5},{5,4},{6,7},{7,6},{8,9},{9,8},{10,11... | collective-permute-start | bytes 294920 | tf_op jit(solution)/shard_map/ppermute | solution.py:563
  2.0 23.6 %collective-permute-start.1 = (bf16[32,1536]{1,0:T(8,128)(2,1)S(1)}, bf16[32,1536]{1,0:T(8,128)(2,1)S(1)}, u32[]{:S(2)}, u32[]{:S(2)}) collective-permute-start(bf16[32,1536]{1,0:T(8,128)(2,1)S(1)} %get-tuple-element.49), channel_id=1, source_target_pairs={{0,31},{1,2},{2,1},{3,4},{4,3},{5,6},{6,5},{7,8},{8,7},{9,10},{10,... | collective-permute-start | bytes 294920 | tf_op jit(solution)/shard_map/ppermute | solution.py:563
  8.6 26.7 %collective-permute-start.4 = (bf16[128,1536]{1,0:T(8,128)(2,1)S(1)}, bf16[128,1536]{1,0:T(8,128)(2,1)S(1)}, u32[]{:S(2)}, u32[]{:S(2)}) collective-permute-start(bf16[128,1536]{1,0:T(8,128)(2,1)S(1)} %get-tuple-element.62.refs_2_.cot_ref), channel_id=1, source_target_pairs={{0,2},{1,3},{2,0},{3,1},{4,6},{5,7},{6,4},{7,5},{8,10},{9,11},{10,... | collective-permute-start | bytes 1179656 | tf_op jit(solution)/shard_map/ppermute | solution.py:563
  9.7 10.2 %collective-permute-start.7 = (bf16[2,48,512]{2,1,0:T(8,128)(2,1)S(1)}, bf16[2,48,512]{2,1,0:T(8,128)(2,1)S(1)}, u32[]{:S(2)}, u32[]{:S(2)}) collective-permute-start(bf16[2,48,512]{2,1,0:T(8,128)(2,1)S(1)} %get-tuple-element.65), channel_id=1, source_target_pairs={{0,2},{1,3},{2,0},{3,1},{4,6},{5,7},{6,4},{7,5},{8,10},{9,11},{10,... | collective-permute-start | bytes 294920 | tf_op jit(solution)/shard_map/ppermute | solution.py:563
  11.8 8.2 %collective-permute-start.8 = (bf16[2,48,512]{2,1,0:T(8,128)(2,1)S(1)}, bf16[2,48,512]{2,1,0:T(8,128)(2,1)S(1)}, u32[]{:S(2)}, u32[]{:S(2)}) collective-permute-start(bf16[2,48,512]{2,1,0:T(8,128)(2,1)S(1)} %get-tuple-element.66), channel_id=1, source_target_pairs={{0,3},{1,2},{2,1},{3,0},{4,7},{5,6},{6,5},{7,4},{8,11},{9,10},{10,... | collective-permute-start | bytes 294920 | tf_op jit(solution)/shard_map/ppermute | solution.py:563
  20.0 8.3 %collective-permute-start.11 = (bf16[2,96,512]{2,1,0:T(8,128)(2,1)S(1)}, bf16[2,96,512]{2,1,0:T(8,128)(2,1)S(1)}, u32[]{:S(2)}, u32[]{:S(2)}) collective-permute-start(bf16[2,96,512]{2,1,0:T(8,128)(2,1)S(1)} %constant_dynamic-update-slice_fusion.2.refs_7_), channel_id=1, source_target_pairs={{0,8},{1,9},{2,10},{3,11},{8,16},{9,17},{10,18},{11,19},{16,24},{1... | collective-permute-start | bytes 589832 | tf_op jit(solution)/shard_map/ppermute | solution.py:563
  22.9 7.8 %collective-permute-start.12 = (bf16[2,96,512]{2,1,0:T(8,128)(2,1)S(1)}, bf16[2,96,512]{2,1,0:T(8,128)(2,1)S(1)}, u32[]{:S(2)}, u32[]{:S(2)}) collective-permute-start(bf16[2,96,512]{2,1,0:T(8,128)(2,1)S(1)} %constant_dynamic-update-slice_fusion.2.refs_7_), channel_id=1, source_target_pairs={{0,4},{1,5},{2,6},{3,7},{8,0},{9,1},{10,2},{11,3},{16,8},{17,9},{1... | collective-permute-start | bytes 589832 | tf_op jit(solution)/shard_map/ppermute | solution.py:563
  22.9 9.7 %collective-permute-start.9 = (bf16[2,96,512]{2,1,0:T(8,128)(2,1)S(1)}, bf16[2,96,512]{2,1,0:T(8,128)(2,1)S(1)}, u32[]{:S(2)}, u32[]{:S(2)}) collective-permute-start(bf16[2,96,512]{2,1,0:T(8,128)(2,1)S(1)} %constant_dynamic-update-slice_fusion.refs_6_), channel_id=1, source_target_pairs={{0,8},{1,9},{2,10},{3,11},{8,16},{9,17},{10,18},{11,19},{16,24},{1... | collective-permute-start | bytes 589832 | tf_op jit(solution)/shard_map/ppermute | solution.py:563
  25.6 8.9 %collective-permute-start.10 = (bf16[2,96,512]{2,1,0:T(8,128)(2,1)S(1)}, bf16[2,96,512]{2,1,0:T(8,128)(2,1)S(1)}, u32[]{:S(2)}, u32[]{:S(2)}) collective-permute-start(bf16[2,96,512]{2,1,0:T(8,128)(2,1)S(1)} %constant_dynamic-update-slice_fusion.refs_6_), channel_id=1, source_target_pairs={{0,4},{1,5},{2,6},{3,7},{8,0},{9,1},{10,2},{11,3},{16,8},{17,9},{1... | collective-permute-start | bytes 589832 | tf_op jit(solution)/shard_map/ppermute | solution.py:563
  28.3 16.5 %collective-permute-start.21 = (bf16[128,1536]{1,0:T(8,128)(2,1)S(1)}, bf16[128,1536]{1,0:T(8,128)(2,1)S(1)}, u32[]{:S(2)}, u32[]{:S(2)}) collective-permute-start(bf16[128,1536]{1,0:T(8,128)(2,1)S(1)} %get-tuple-element.61.refs_1_), channel_id=1, source_target_pairs={{0,2},{1,3},{2,0},{3,1},{4,6},{5,7},{6,4},{7,5},{8,10},{9,11},{10,... | collective-permute-start | bytes 1179656 | tf_op jit(solution)/shard_map/ppermute | solution.py:563
  30.6 6.4 %collective-permute-start.15 = (bf16[2,96,512]{2,1,0:T(8,128)(2,1)S(1)}, bf16[2,96,512]{2,1,0:T(8,128)(2,1)S(1)}, u32[]{:S(2)}, u32[]{:S(2)}) collective-permute-start(bf16[2,96,512]{2,1,0:T(8,128)(2,1)S(1)} %collective-permute-done.11.refs_10_), channel_id=1, source_target_pairs={{0,8},{1,9},{2,10},{3,11},{8,16},{9,17},{10,18},{11,19},{16,24},{1... | collective-permute-start | bytes 589832 | tf_op jit(solution)/shard_map/ppermute | solution.py:563
  32.5 8.1 %collective-permute-start.16 = (bf16[2,96,512]{2,1,0:T(8,128)(2,1)S(1)}, bf16[2,96,512]{2,1,0:T(8,128)(2,1)S(1)}, u32[]{:S(2)}, u32[]{:S(2)}) collective-permute-start(bf16[2,96,512]{2,1,0:T(8,128)(2,1)S(1)} %collective-permute-done.12.refs_11_), channel_id=1, source_target_pairs={{0,4},{1,5},{2,6},{3,7},{8,0},{9,1},{10,2},{11,3},{16,8},{17,9},{1... | collective-permute-start | bytes 589832 | tf_op jit(solution)/shard_map/ppermute | solution.py:563
  34.6 7.8 %collective-permute-start.13 = (bf16[2,96,512]{2,1,0:T(8,128)(2,1)S(1)}, bf16[2,96,512]{2,1,0:T(8,128)(2,1)S(1)}, u32[]{:S(2)}, u32[]{:S(2)}) collective-permute-start(bf16[2,96,512]{2,1,0:T(8,128)(2,1)S(1)} %collective-permute-done.9.refs_8_), channel_id=1, source_target_pairs={{0,8},{1,9},{2,10},{3,11},{8,16},{9,17},{10,18},{11,19},{16,24},{1... | collective-permute-start | bytes 589832 | tf_op jit(solution)/shard_map/ppermute | solution.py:563
  35.3 9.5 %collective-permute-start.14 = (bf16[2,96,512]{2,1,0:T(8,128)(2,1)S(1)}, bf16[2,96,512]{2,1,0:T(8,128)(2,1)S(1)}, u32[]{:S(2)}, u32[]{:S(2)}) collective-permute-start(bf16[2,96,512]{2,1,0:T(8,128)(2,1)S(1)} %collective-permute-done.10.refs_9_), channel_id=1, source_target_pairs={{0,4},{1,5},{2,6},{3,7},{8,0},{9,1},{10,2},{11,3},{16,8},{17,9},{1... | collective-permute-start | bytes 589832 | tf_op jit(solution)/shard_map/ppermute | solution.py:563
  37.1 9.5 %collective-permute-start.19 = (bf16[2,96,512]{2,1,0:T(8,128)(2,1)S(1)}, bf16[2,96,512]{2,1,0:T(8,128)(2,1)S(1)}, u32[]{:S(2)}, u32[]{:S(2)}) collective-permute-start(bf16[2,96,512]{2,1,0:T(8,128)(2,1)S(1)} %collective-permute-done.15.refs_14_), channel_id=1, source_target_pairs={{0,8},{1,9},{2,10},{3,11},{8,16},{9,17},{10,18},{11,19},{16,24},{1... | collective-permute-start | bytes 589832 | tf_op jit(solution)/shard_map/ppermute | solution.py:563
  40.6 6.5 %collective-permute-start.20 = (bf16[2,96,512]{2,1,0:T(8,128)(2,1)S(1)}, bf16[2,96,512]{2,1,0:T(8,128)(2,1)S(1)}, u32[]{:S(2)}, u32[]{:S(2)}) collective-permute-start(bf16[2,96,512]{2,1,0:T(8,128)(2,1)S(1)} %collective-permute-done.16.refs_15_), channel_id=1, source_target_pairs={{0,4},{1,5},{2,6},{3,7},{8,0},{9,1},{10,2},{11,3},{16,8},{17,9},{1... | collective-permute-start | bytes 589832 | tf_op jit(solution)/shard_map/ppermute | solution.py:563
  42.3 6.6 %collective-permute-start.17 = (bf16[2,96,512]{2,1,0:T(8,128)(2,1)S(1)}, bf16[2,96,512]{2,1,0:T(8,128)(2,1)S(1)}, u32[]{:S(2)}, u32[]{:S(2)}) collective-permute-start(bf16[2,96,512]{2,1,0:T(8,128)(2,1)S(1)} %collective-permute-done.13.refs_12_), channel_id=1, source_target_pairs={{0,8},{1,9},{2,10},{3,11},{8,16},{9,17},{10,18},{11,19},{16,24},{1... | collective-permute-start | bytes 589832 | tf_op jit(solution)/shard_map/ppermute | solution.py:563
  44.8 11.7 %collective-permute-start.3 = (bf16[128,1536]{1,0:T(8,128)(2,1)S(1)}, bf16[128,1536]{1,0:T(8,128)(2,1)S(1)}, u32[]{:S(2)}, u32[]{:S(2)}) collective-permute-start(bf16[128,1536]{1,0:T(8,128)(2,1)S(1)} %get-tuple-element.62.refs_2_.cot_ref), channel_id=1, source_target_pairs={{0,1},{1,0},{2,3},{3,2},{4,5},{5,4},{6,7},{7,6},{8,9},{9,8},{10,11... | collective-permute-start | bytes 1179656 | tf_op jit(solution)/shard_map/ppermute | solution.py:563
  44.8 12.0 %collective-permute-start.2 = (bf16[128,1536]{1,0:T(8,128)(2,1)S(1)}, bf16[128,1536]{1,0:T(8,128)(2,1)S(1)}, u32[]{:S(2)}, u32[]{:S(2)}) collective-permute-start(bf16[128,1536]{1,0:T(8,128)(2,1)S(1)} %get-tuple-element.61.refs_1_), channel_id=1, source_target_pairs={{0,1},{1,0},{2,3},{3,2},{4,5},{5,4},{6,7},{7,6},{8,9},{9,8},{10,11... | collective-permute-start | bytes 1179656 | tf_op jit(solution)/shard_map/ppermute | solution.py:563
  46.6 12.1 %collective-permute-start.5 = (bf16[128,1536]{1,0:T(8,128)(2,1)S(1)}, bf16[128,1536]{1,0:T(8,128)(2,1)S(1)}, u32[]{:S(2)}, u32[]{:S(2)}) collective-permute-start(bf16[128,1536]{1,0:T(8,128)(2,1)S(1)} %collective-permute-done.4.refs_4_), channel_id=1, source_target_pairs={{0,1},{1,0},{2,3},{3,2},{4,5},{5,4},{6,7},{7,6},{8,9},{9,8},{10,11... | collective-permute-start | bytes 1179656 | tf_op jit(solution)/shard_map/ppermute | solution.py:563
  47.1 13.7 %collective-permute-start.22 = (bf16[128,1536]{1,0:T(8,128)(2,1)S(1)}, bf16[128,1536]{1,0:T(8,128)(2,1)S(1)}, u32[]{:S(2)}, u32[]{:S(2)}) collective-permute-start(bf16[128,1536]{1,0:T(8,128)(2,1)S(1)} %collective-permute-done.21.refs_1_.far_ref), channel_id=1, source_target_pairs={{0,1},{1,0},{2,3},{3,2},{4,5},{5,4},{6,7},{7,6},{8,9},{9,8},{10,11... | collective-permute-start | bytes 1179656 | tf_op jit(solution)/shard_map/ppermute | solution.py:563
  49.0 5.7 %collective-permute-start.18 = (bf16[2,96,512]{2,1,0:T(8,128)(2,1)S(1)}, bf16[2,96,512]{2,1,0:T(8,128)(2,1)S(1)}, u32[]{:S(2)}, u32[]{:S(2)}) collective-permute-start(bf16[2,96,512]{2,1,0:T(8,128)(2,1)S(1)} %collective-permute-done.14.refs_13_), channel_id=1, source_target_pairs={{0,4},{1,5},{2,6},{3,7},{8,0},{9,1},{10,2},{11,3},{16,8},{17,9},{1... | collective-permute-start | bytes 589832 | tf_op jit(solution)/shard_map/ppermute | solution.py:563
  54.7 6.8 %collective-permute-start.25 = (bf16[1,96,512]{2,1,0:T(8,128)(2,1)S(1)}, bf16[1,96,512]{2,1,0:T(8,128)(2,1)S(1)}, u32[]{:S(2)}, u32[]{:S(2)}) collective-permute-start(bf16[1,96,512]{2,1,0:T(8,128)(2,1)S(1)} %slice.18), channel_id=1, source_target_pairs={{0,8},{1,9},{2,10},{3,11},{8,16},{9,17},{10,18},{11,19},{16,24},{1... | collective-permute-start | bytes 294920 | tf_op jit(solution)/shard_map/ppermute | solution.py:563
  56.5 5.0 %collective-permute-start.26 = (bf16[1,96,512]{2,1,0:T(8,128)(2,1)S(1)}, bf16[1,96,512]{2,1,0:T(8,128)(2,1)S(1)}, u32[]{:S(2)}, u32[]{:S(2)}) collective-permute-start(bf16[1,96,512]{2,1,0:T(8,128)(2,1)S(1)} %slice.19), channel_id=1, source_target_pairs={{0,4},{1,5},{2,6},{3,7},{8,0},{9,1},{10,2},{11,3},{16,8},{17,9},{1... | collective-permute-start | bytes 294920 | tf_op jit(solution)/shard_map/ppermute | solution.py:563
  56.8 4.8 %collective-permute-start.23 = (bf16[1,96,512]{2,1,0:T(8,128)(2,1)S(1)}, bf16[1,96,512]{2,1,0:T(8,128)(2,1)S(1)}, u32[]{:S(2)}, u32[]{:S(2)}) collective-permute-start(bf16[1,96,512]{2,1,0:T(8,128)(2,1)S(1)} %slice.16), channel_id=1, source_target_pairs={{0,8},{1,9},{2,10},{3,11},{8,16},{9,17},{10,18},{11,19},{16,24},{1... | collective-permute-start | bytes 294920 | tf_op jit(solution)/shard_map/ppermute | solution.py:563
  58.6 4.6 %collective-permute-start.24 = (bf16[1,96,512]{2,1,0:T(8,128)(2,1)S(1)}, bf16[1,96,512]{2,1,0:T(8,128)(2,1)S(1)}, u32[]{:S(2)}, u32[]{:S(2)}) collective-permute-start(bf16[1,96,512]{2,1,0:T(8,128)(2,1)S(1)} %slice.17), channel_id=1, source_target_pairs={{0,4},{1,5},{2,6},{3,7},{8,0},{9,1},{10,2},{11,3},{16,8},{17,9},{1... | collective-permute-start | bytes 294920 | tf_op jit(solution)/shard_map/ppermute | solution.py:563
  65.0 13.7 %collective-permute-start.27 = (bf16[128,1536]{1,0:T(8,128)(2,1)S(1)}, bf16[128,1536]{1,0:T(8,128)(2,1)S(1)}, u32[]{:S(2)}, u32[]{:S(2)}) collective-permute-start(bf16[128,1536]{1,0:T(8,128)(2,1)S(1)} %get-tuple-element.78), channel_id=1, source_target_pairs={{0,1},{1,0},{2,3},{3,2},{4,5},{5,4},{6,7},{7,6},{8,9},{9,8},{10,11... | collective-permute-start | bytes 1179656 | tf_op jit(solution)/shard_map/ppermute | solution.py:563
  66.5 16.9 %collective-permute-start.29 = (bf16[128,1536]{1,0:T(8,128)(2,1)S(1)}, bf16[128,1536]{1,0:T(8,128)(2,1)S(1)}, u32[]{:S(2)}, u32[]{:S(2)}) collective-permute-start(bf16[128,1536]{1,0:T(8,128)(2,1)S(1)} %shard_map.138), channel_id=1, source_target_pairs={{0,2},{1,3},{2,0},{3,1},{4,6},{5,7},{6,4},{7,5},{8,10},{9,11},{10,... | collective-permute-start | bytes 1179656 | tf_op jit(solution)/shard_map/ppermute | solution.py:563
  67.5 10.4 %collective-permute-start.32 = (bf16[2,32,128]{2,1,0:T(8,128)(2,1)S(1)}, bf16[2,32,128]{2,1,0:T(8,128)(2,1)S(1)}, u32[]{:S(2)}, u32[]{:S(2)}) collective-permute-start(bf16[2,32,128]{2,1,0:T(8,128)(2,1)S(1)} %get-tuple-element.86), channel_id=1, source_target_pairs={{0,2},{1,3},{2,0},{3,1},{4,6},{5,7},{6,4},{7,5},{8,10},{9,11},{10,... | collective-permute-start | bytes 49160 | tf_op jit(solution)/shard_map/ppermute | solution.py:563
  78.7 6.8 %collective-permute-start.33 = (bf16[32,1536]{1,0:T(8,128)(2,1)S(1)}, bf16[32,1536]{1,0:T(8,128)(2,1)S(1)}, u32[]{:S(2)}, u32[]{:S(2)}) collective-permute-start(bf16[32,1536]{1,0:T(8,128)(2,1)S(1)} %shard_map.141), channel_id=1, source_target_pairs={{2,31},{3,2},{0,1},{1,4},{6,3},{7,6},{4,5},{5,8},{10,7},{11,10},{8... | collective-permute-start | bytes 294920 | tf_op jit(solution)/shard_map/ppermute | solution.py:563
  79.5 7.8 %collective-permute-start.31 = (bf16[32,1536]{1,0:T(8,128)(2,1)S(1)}, bf16[32,1536]{1,0:T(8,128)(2,1)S(1)}, u32[]{:S(2)}, u32[]{:S(2)}) collective-permute-start(bf16[32,1536]{1,0:T(8,128)(2,1)S(1)} %get-tuple-element.85), channel_id=1, source_target_pairs={{0,31},{1,2},{2,1},{3,4},{4,3},{5,6},{6,5},{7,8},{8,7},{9,10},{10,... | collective-permute-start | bytes 294920 | tf_op jit(solution)/shard_map/ppermute | solution.py:563
  84.2 3.2 %collective-permute-start.30 = (bf16[32,1536]{1,0:T(8,128)(2,1)S(1)}, bf16[32,1536]{1,0:T(8,128)(2,1)S(1)}, u32[]{:S(2)}, u32[]{:S(2)}) collective-permute-start(bf16[32,1536]{1,0:T(8,128)(2,1)S(1)} %get-tuple-element.84), channel_id=1, source_target_pairs={{0,1},{1,0},{2,3},{3,2},{4,5},{5,4},{6,7},{7,6},{8,9},{9,8},{10,11... | collective-permute-start | bytes 294920 | tf_op jit(solution)/shard_map/ppermute | solution.py:563
  (2 other events, 5.3 us)
